TPU v7x, 512 devices: a whole 4x8x8 slice. The times are simulated.
512 devices in a mesh: src: 16 (over y, core), tgt: 32 (over x, z).
Axes of the slice: x: 4, y: 8, z: 8, core: 2. Of those that a mesh axis runs over, the one named last changes fastest.
Arguments:
- noise: float32 [16384, 384], P(('src', 'tgt')), may hold values from -16 to 16
- data: float32 [32768, 384], P('tgt', 'src'), may hold values from -6 to 6
Outputs:
- velocity: float32 [16384, 384], P(('src', 'tgt'))
- target_potential: float32 [32768], P('tgt')
All inputs are finite; a program needn't handle non-finite values.
Results may differ from a plain program's by a relative error of at most 0.0003.
Values sent between devices are 32-bit elements; how exact they have to be, the bound alone decides.
No kernel may reach another device: no remote copies, remote signals or barrier semaphores. Data moves between devices by JAX's collectives and lax.ppermute only.
A program may use at most 64 MiB of HBM per device.

v0:
```python
import math

import jax
import jax.numpy as jnp
from jax import lax
from jax.sharding import PartitionSpec as P

ITERS = 3


EPS = 0.05


def row_merge(z_tile):
    local_top = jnp.max(z_tile, axis=1)
    top = lax.pmax(local_top, "tgt")
    total = lax.psum(jnp.sum(jnp.exp(z_tile - top[:, None]), axis=1), "tgt")
    return top + jnp.log(total)


def col_merge(z_tile):
    local_top = jnp.max(z_tile, axis=0)
    top = lax.pmax(local_top, "src")
    total = lax.psum(jnp.sum(jnp.exp(z_tile - top[None, :]), axis=0), "src")
    return top + jnp.log(total)


def per_device(noise, data):
    source_rows = lax.all_gather(noise, "tgt", axis=0, tiled=True)
    target_rows = lax.all_gather(data, "src", axis=1, tiled=True)
    feat_width = source_rows.shape[1]
    src_total = source_rows.shape[0] * lax.axis_size("src")
    tgt_total = target_rows.shape[0] * lax.axis_size("tgt")
    source_sq = jnp.sum(source_rows * source_rows, axis=1)
    target_sq = jnp.sum(target_rows * target_rows, axis=1)
    cross = jnp.dot(
        source_rows,
        target_rows.T,
        precision=lax.Precision.HIGHEST,
        preferred_element_type=jnp.float32,
    )
    cost_tile = (source_sq[:, None] + target_sq[None, :] - 2.0 * cross) / feat_width
    g_pot = jnp.zeros((target_rows.shape[0],), jnp.float32)
    for step_index in range(ITERS):
        f_pot = -EPS * (math.log(src_total) + row_merge((g_pot[None, :] - cost_tile) / EPS))
        g_pot = -EPS * (math.log(tgt_total) + col_merge((f_pot[:, None] - cost_tile) / EPS))
    z_final = (g_pot[None, :] - cost_tile) / EPS
    lrow = row_merge(z_final)
    weight = jnp.exp(z_final - lrow[:, None])
    own_rows = noise.shape[0]
    whole = lax.psum(
        jnp.dot(
            weight, target_rows, precision=lax.Precision.HIGHEST, preferred_element_type=jnp.float32
        ),
        "tgt",
    )
    bary = lax.dynamic_slice_in_dim(whole, lax.axis_index("tgt") * own_rows, own_rows, 0)
    return (bary - noise, g_pot)


def solution(mesh):
    placed = (P(("src", "tgt"), None), P("tgt", "src"))
    return jax.shard_map(
        per_device,
        mesh=mesh,
        in_specs=placed,
        out_specs=(P(("src", "tgt"), None), P("tgt")),
        check_vma=False,
    )
```

profile of v0, /device:TPU:8, one launch (start us, length us, event | category | flops | bytes accessed | tf_op | source)
XLA Modules:
  0.0 1082.2 jit_solution(13867403295693776282)
XLA Ops:
  7.2 0.0 all-gather.5.cloned.1.call-start
  7.2 0.7 all-gather.5.cloned.1.call-update
  7.9 0.0 all-gather.3.cloned.1.call-start
  7.9 0.7 all-gather.3.cloned.1.call-update
  8.6 0.0 all-reduce.2.cloned.1.call-start
  8.7 47.0 %all-gather.5.cloned.1.call-done = f32[1024,384]{0,1:T(8,128)} async-done(((f32[1024,24]{0,1:T(8,128)}), f32[1024,384]{0,1:T(8,128)}) %all-gather.5.cloned.1.call-update) | async-done | bytes 1572880 | tf_op jit(solution)/shard_map/all_gather | solution.py:30
  55.7 1.5 multiply_reduce_fusion
  57.3 84.2 %all-gather.3.cloned.1.call-done = f32[1024,384]{1,0:T(8,128)} async-done(((f32[32,384]{1,0:T(8,128)}), f32[1024,384]{1,0:T(8,128)}) %all-gather.3.cloned.1.call-update) | async-done | bytes 1572880 | tf_op jit(solution)/shard_map/all_gather | solution.py:29
  141.5 1.6 multiply_reduce_fusion.1
  143.1 10.5 fusion.3
  153.6 72.1 %pmax.49 = f32[1024]{0:T(1024)S(1)} all-reduce(f32[1024]{0:T(1024)S(1)} %get-tuple-element.2), channel_id=1, replica_groups=mesh['src'=16,'tgt'=32] {'tgt'}, use_global_device_ids=true, to_apply=%region_3.0 | all-reduce | flops 1024 | bytes 8192 | tf_op jit(solution)/shard_map/pmax | solution.py:16
  225.7 3.0 exponential_reduce_fusion.6
  228.7 69.6 %psum.56 = f32[1024]{0:T(1024)S(1)} all-reduce(f32[1024]{0:T(1024)S(1)} %exponential_reduce_fusion.6), channel_id=1, replica_groups=mesh['src'=16,'tgt'=32] {'tgt'}, use_global_device_ids=true, to_apply=%region_5.0 | all-reduce | flops 1024 | bytes 8192 | tf_op jit(solution)/shard_map/psum | solution.py:17
  298.4 2.7 fusion.4
  301.1 20.6 %pmax.50 = f32[1024]{0:T(1024)S(1)} all-reduce(f32[1024]{0:T(1024)S(1)} %fusion.4), channel_id=1, replica_groups=mesh['src'=16,'tgt'=32] {'src'}, use_global_device_ids=true, to_apply=%region_7.0 | all-reduce | flops 1024 | bytes 8192 | tf_op jit(solution)/shard_map/pmax | solution.py:23
  321.7 3.2 exponential_reduce_fusion.5
  324.8 23.6 %psum.57 = f32[1024]{0:T(1024)S(1)} all-reduce(f32[1024]{0:T(1024)S(1)} %exponential_reduce_fusion.5), channel_id=1, replica_groups=mesh['src'=16,'tgt'=32] {'src'}, use_global_device_ids=true, to_apply=%region_9.0 | all-reduce | flops 1024 | bytes 8192 | tf_op jit(solution)/shard_map/psum | solution.py:24
  348.4 2.7 fusion.5
  351.1 71.6 %pmax.51 = f32[1024]{0:T(1024)S(1)} all-reduce(f32[1024]{0:T(1024)S(1)} %fusion.5), channel_id=1, replica_groups=mesh['src'=16,'tgt'=32] {'tgt'}, use_global_device_ids=true, to_apply=%region_11.0 | all-reduce | flops 1024 | bytes 8192 | tf_op jit(solution)/shard_map/pmax | solution.py:16
  422.7 3.1 exponential_reduce_fusion.4
  425.8 69.6 %psum.58 = f32[1024]{0:T(1024)S(1)} all-reduce(f32[1024]{0:T(1024)S(1)} %exponential_reduce_fusion.4), channel_id=1, replica_groups=mesh['src'=16,'tgt'=32] {'tgt'}, use_global_device_ids=true, to_apply=%region_13.0 | all-reduce | flops 1024 | bytes 8192 | tf_op jit(solution)/shard_map/psum | solution.py:17
  495.5 2.7 fusion.6
  498.1 23.6 %pmax.52 = f32[1024]{0:T(1024)S(1)} all-reduce(f32[1024]{0:T(1024)S(1)} %fusion.6), channel_id=1, replica_groups=mesh['src'=16,'tgt'=32] {'src'}, use_global_device_ids=true, to_apply=%region_15.0 | all-reduce | flops 1024 | bytes 8192 | tf_op jit(solution)/shard_map/pmax | solution.py:23
  521.7 3.2 exponential_reduce_fusion.3
  524.9 23.6 %psum.59 = f32[1024]{0:T(1024)S(1)} all-reduce(f32[1024]{0:T(1024)S(1)} %exponential_reduce_fusion.3), channel_id=1, replica_groups=mesh['src'=16,'tgt'=32] {'src'}, use_global_device_ids=true, to_apply=%region_17.0 | all-reduce | flops 1024 | bytes 8192 | tf_op jit(solution)/shard_map/psum | solution.py:24
  548.4 2.7 fusion.7
  551.1 71.8 %pmax.53 = f32[1024]{0:T(1024)S(1)} all-reduce(f32[1024]{0:T(1024)S(1)} %fusion.7), channel_id=1, replica_groups=mesh['src'=16,'tgt'=32] {'tgt'}, use_global_device_ids=true, to_apply=%region_19.0 | all-reduce | flops 1024 | bytes 8192 | tf_op jit(solution)/shard_map/pmax | solution.py:16
  622.9 3.1 exponential_reduce_fusion.2
  626.0 69.7 %psum.60 = f32[1024]{0:T(1024)S(1)} all-reduce(f32[1024]{0:T(1024)S(1)} %exponential_reduce_fusion.2), channel_id=1, replica_groups=mesh['src'=16,'tgt'=32] {'tgt'}, use_global_device_ids=true, to_apply=%region_21.0 | all-reduce | flops 1024 | bytes 8192 | tf_op jit(solution)/shard_map/psum | solution.py:17
  695.7 2.7 fusion.8
  698.3 23.6 %pmax.54 = f32[1024]{0:T(1024)S(1)} all-reduce(f32[1024]{0:T(1024)S(1)} %fusion.8), channel_id=1, replica_groups=mesh['src'=16,'tgt'=32] {'src'}, use_global_device_ids=true, to_apply=%region_23.0 | all-reduce | flops 1024 | bytes 8192 | tf_op jit(solution)/shard_map/pmax | solution.py:23
  721.9 3.2 exponential_reduce_fusion.1
  725.1 23.6 %psum.61 = f32[1024]{0:T(1024)S(1)} all-reduce(f32[1024]{0:T(1024)S(1)} %exponential_reduce_fusion.1), channel_id=1, replica_groups=mesh['src'=16,'tgt'=32] {'src'}, use_global_device_ids=true, to_apply=%region_25.0 | all-reduce | flops 1024 | bytes 8192 | tf_op jit(solution)/shard_map/psum | solution.py:24
  748.6 0.0 copy-start.2
  748.6 0.0 copy-start
  748.6 2.8 fusion.9
  751.4 71.6 %pmax.55 = f32[1024]{0:T(1024)S(1)} all-reduce(f32[1024]{0:T(1024)S(1)} %fusion.9), channel_id=1, replica_groups=mesh['src'=16,'tgt'=32] {'tgt'}, use_global_device_ids=true, to_apply=%region_27.0 | all-reduce | flops 1024 | bytes 8192 | tf_op jit(solution)/shard_map/pmax | solution.py:16
  823.0 3.1 exponential_reduce_fusion
  826.1 69.7 %psum.62 = f32[1024]{0:T(1024)S(1)} all-reduce(f32[1024]{0:T(1024)S(1)} %exponential_reduce_fusion), channel_id=1, replica_groups=mesh['src'=16,'tgt'=32] {'tgt'}, use_global_device_ids=true, to_apply=%region_29.0 | all-reduce | flops 1024 | bytes 8192 | tf_op jit(solution)/shard_map/psum | solution.py:17
  895.8 0.0 copy-done.2
  895.8 0.0 copy-done
  895.8 0.0 copy-start.1
  895.8 16.5 %fusion = f32[1024,384]{1,0:T(8,128)} fusion(f32[1024,384]{0,1:T(8,128)S(1)} %copy-done, f32[1024,1024]{0,1:T(8,128)} %get-tuple-element.3, f32[1024]{0:T(1024)S(1)} %log_add_fusion, f32[1024]{0:T(1024)S(1)} %add_multiply_fusion), kind=kOutput, calls=%fused_computation | convolution fusion | flops 4834983936 | bytes 7348224 | tf_op jit(solution)/shard_map/dot_general | solution.py:52
  912.3 0.0 all-reduce.2.cloned.1.call-update
  912.3 161.9 %all-reduce.2.cloned.1.call-done = f32[1024,384]{1,0:T(8,128)} async-done(((f32[1024,384]{1,0:T(8,128)}), f32[1024,384]{1,0:T(8,128)}) %all-reduce.2.cloned.1.call-update) | async-done | bytes 1572880 | tf_op jit(solution)/shard_map/psum | solution.py:51
  1074.2 0.0 copy-done.1
  1074.2 1.4 dynamic-slice_subtract_fusion
  (7 shorter events, 0.1 us)
Async XLA Ops:
  7.2 48.6 %all-gather.5.cloned.1.call-start = ((), (), s32[]{:S(2)}) async-start(), calls=%async_computation.1 | async-start | bytes 1671168 | tf_op jit(solution)/shard_map/all_gather | solution.py:30
  7.9 133.6 %all-gather.3.cloned.1.call-start = ((), (), s32[]{:S(2)}) async-start(), calls=%async_computation | async-start | bytes 1622016 | tf_op jit(solution)/shard_map/all_gather | solution.py:29
  8.6 1065.6 %all-reduce.2.cloned.1.call-start = ((), (), s32[]{:S(2)}) async-start(), calls=%async_computation.2 | async-start | bytes 3145728 | tf_op jit(solution)/shard_map/psum | solution.py:51
  748.6 147.2 %copy-start.2 = (f32[1024]{0:T(1024)}, f32[1024]{0:T(1024)S(1)}, u32[]{:S(2)}) copy-start(f32[1024]{0:T(1024)S(1)} %add_multiply_fusion) | copy-start | bytes 12292
  748.6 147.2 %copy-start = (f32[1024,384]{0,1:T(8,128)S(1)}, f32[1024,384]{0,1:T(8,128)}, u32[]{:S(2)}) copy-start(f32[1024,384]{0,1:T(8,128)} %all-gather.5.cloned.1.call-done) | copy-start | bytes 4718596
  895.8 178.4 %copy-start.1 = (f32[32,384]{1,0:T(8,128)S(1)}, f32[32,384]{1,0:T(8,128)}, u32[]{:S(2)}) copy-start(f32[32,384]{1,0:T(8,128)} %param.2) | copy-start | bytes 147460
Sparse Core Ops, SparseCore 0:
  10.1 45.5 all-gather.4
  58.9 82.5 all-gather.2
  912.5 161.7 all-reduce.1
where the time goes:
time: 1080 us
  blocking collectives  704 us (65%)
  waiting for transfers between devices  294 us (27%)
  other arithmetic  42.6 us (4%)
  matrix products  27 us (2%)
  between operations  13.9 us (1%)
    pmax x4, blocking collectives, row_merge(): top = lax.pmax(local_top, 'tgt')  287 us
    psum x4, blocking collectives, row_merge(): total = lax.psum(jnp.sum(jnp.exp(z_tile - top[:, None]), axis=1), 'tgt')  279 us
    psum x1, waiting for transfers between devices, per_device(): lax.psum(jnp.dot(weight, target_rows, precision=lax.Precision.HIGHEST, pr...  162 us
    all_gather x1, waiting for transfers between devices, per_device(): source_rows = lax.all_gather(noise, 'tgt', axis=0, tiled=True)  84.2 us
    psum x3, blocking collectives, col_merge(): total = lax.psum(jnp.sum(jnp.exp(z_tile - top[None, :]), axis=0), 'src')  70.7 us
    pmax x3, blocking collectives, col_merge(): top = lax.pmax(local_top, 'src')  67.7 us
    all_gather x1, waiting for transfers between devices, per_device(): target_rows = lax.all_gather(data, 'src', axis=1, tiled=True)  47 us
  transfers between devices with their start and end apart: 3, of which 3 were waited for; matrix products, arithmetic and copies ran while one was open for 0% of the time, Pallas kernels for 0%

commit v1 on v0

v1 whole, which is shorter than its diff:
```python
import math

import jax
import jax.numpy as jnp
from jax import lax
from jax.sharding import PartitionSpec as P

ITERS = 3


EPS = 0.05


def spread(value, axis):
    count = lax.axis_size(axis)
    return lax.all_to_all(jnp.broadcast_to(value[None], (count,) + value.shape), axis, 0, 0)


def total_over(local_sum, axis):
    tiles = local_sum.reshape(-1, 128)
    return jnp.sum(spread(tiles, axis), axis=0).reshape(local_sum.shape)


def lse_over(local_top, local_sum, axis):
    tiles = spread((local_top + jnp.log(local_sum)).reshape(-1, 128), axis)
    top = jnp.max(tiles, axis=0)
    merged = top + jnp.log(jnp.sum(jnp.exp(tiles - top[None]), axis=0))
    return merged.reshape(local_top.shape)


def per_device(noise, data):
    target_rows = lax.all_gather(data, "src", axis=1, tiled=True)
    own_rows, feat_width = noise.shape
    source_rows = spread(noise, "tgt").reshape(-1, feat_width)
    src_total = source_rows.shape[0] * lax.axis_size("src")
    tgt_total = target_rows.shape[0] * lax.axis_size("tgt")
    source_sq = jnp.sum(source_rows * source_rows, axis=1)
    target_sq = jnp.sum(target_rows * target_rows, axis=1)
    cross = jnp.dot(
        source_rows,
        target_rows.T,
        precision=lax.Precision.HIGHEST,
        preferred_element_type=jnp.float32,
    )
    gain = (2.0 * cross - source_sq[:, None] - target_sq[None, :]) / (feat_width * EPS)
    log_src, log_tgt = math.log(src_total), math.log(tgt_total)

    top = jnp.max(gain, axis=1)
    f_pot = -(log_src + lse_over(top, jnp.sum(jnp.exp(gain - top[:, None]), axis=1), "tgt"))
    z_tile = f_pot[:, None] + gain
    top = jnp.max(z_tile, axis=0)
    g_pot = -(log_tgt + lse_over(top, jnp.sum(jnp.exp(z_tile - top[None, :]), axis=0), "src"))
    for step_index in range(1, ITERS):
        mass = jnp.sum(jnp.exp((f_pot[:, None] + gain) + g_pot[None, :]), axis=1)
        f_pot = f_pot - (log_src + jnp.log(total_over(mass, "tgt")))
        mass = jnp.sum(jnp.exp((f_pot[:, None] + gain) + g_pot[None, :]), axis=0)
        g_pot = g_pot - (log_tgt + jnp.log(total_over(mass, "src")))
    plan = jnp.exp((f_pot[:, None] + gain) + g_pot[None, :])
    mass = jnp.sum(plan, axis=1)
    part = jnp.dot(
        plan, target_rows, precision=lax.Precision.HIGHEST, preferred_element_type=jnp.float32
    )
    count = lax.axis_size("tgt")
    part = lax.all_to_all(part.reshape(count, own_rows, feat_width), "tgt", 0, 0)
    mass = lax.all_to_all(mass.reshape(count, own_rows), "tgt", 0, 0)
    bary = jnp.sum(part, axis=0) / jnp.sum(mass, axis=0)[:, None]
    return (bary - noise, EPS * g_pot)


def solution(mesh):
    placed = (P(("src", "tgt"), None), P("tgt", "src"))
    return jax.shard_map(
        per_device,
        mesh=mesh,
        in_specs=placed,
        out_specs=(P(("src", "tgt"), None), P("tgt")),
        check_vma=False,
    )
```

time: 1080 us -> 253 us (0.23)
  blocking collectives: 704 us -> 79.1 us
  waiting for transfers between devices: 294 us -> 77.9 us
  starting transfers between devices: 0.11 us -> 27 us
  other arithmetic: 42.6 us -> 22.7 us
    pmax x7 -> x0, blocking collectives: 355 us -> none  [the longest x4 287 us: row_merge(): top = lax.pmax(local_top, 'tgt')]
    psum x7 -> x0, blocking collectives: 349 us -> none  [the longest x4 279 us: row_merge(): total = lax.psum(jnp.sum(jnp.exp(z_tile - top[:, None]), axis=1), 'tgt')]
    psum x1 -> x0, waiting for transfers between devices: 162 us -> none  [per_device(): lax.psum(jnp.dot(weight, target_rows, precision=lax.Precision.HIGHEST, pr...]
    all_gather x1 -> x0, waiting for transfers between devices: 84.2 us -> none  [per_device(): source_rows = lax.all_gather(noise, 'tgt', axis=0, tiled=True)]
    all_to_all x0 -> x6, blocking collectives: none -> 79.1 us  [spread(): lax.all_to_all(jnp.broadcast_to(value[None], (count,) + value.shape), axi...]
    all_to_all x0 -> x3, waiting for transfers between devices: none -> 44.8 us  [the longest x1 39.4 us: per_device(): lax.all_to_all(part.reshape(count, own_rows, feat_width), 'tgt', 0, 0)]
    all_to_all x0 -> x3, starting transfers between devices: none -> 26.9 us  [the longest x1 13.2 us: spread(): lax.all_to_all(jnp.broadcast_to(value[None], (count,) + value.shape), axi...]
    all_gather x1, waiting for transfers between devices: 47 us -> 32.4 us  [per_device(): target_rows = lax.all_gather(data, 'src', axis=1, tiled=True)]
  transfers between devices with their start and end apart: 3 -> 4, of which waited for: 3 -> 3; matrix products, arithmetic and copies ran while one was open for 0% -> 8% of each run, Pallas kernels for 0% -> 0%
where the time goes in v1:
time: 253 us; the launch traced here: 252 us
  blocking collectives  79.1 us (31%)
  waiting for transfers between devices  77.9 us (31%)
  starting transfers between devices  27 us (11%)
  matrix products  25.2 us (10%)
  other arithmetic  22.7 us (9%)
  between operations  14.2 us (6%)
  local copies, waits for them, and re-layouts  5.58 us (2%)
    all_to_all x6, blocking collectives, spread(): lax.all_to_all(jnp.broadcast_to(value[None], (count,) + value.shape), axi...  79.1 us
    all_to_all x1, waiting for transfers between devices, per_device(): lax.all_to_all(part.reshape(count, own_rows, feat_width), 'tgt', 0, 0)  39.4 us
    all_gather x1, waiting for transfers between devices, per_device(): target_rows = lax.all_gather(data, 'src', axis=1, tiled=True)  32.4 us
    dot_general x1, matrix products, per_device(): jnp.dot(plan, target_rows, precision=lax.Precision.HIGHEST, preferred_ele...  16.3 us
    all_to_all x1, starting transfers between devices, spread(): lax.all_to_all(jnp.broadcast_to(value[None], (count,) + value.shape), axi...  13.2 us
    all_to_all x1, starting transfers between devices, per_device(): lax.all_to_all(part.reshape(count, own_rows, feat_width), 'tgt', 0, 0)  9.7 us
    dot_general x1, matrix products, per_device(): jnp.dot(source_rows, target_rows.T, precision=lax.Precision.HIGHEST, pref...  8.88 us
    reduce_sum x2, other arithmetic, per_device(): mass = jnp.sum(jnp.exp(f_pot[:, None] + gain + g_pot[None, :]), axis=0)  6.26 us
  transfers between devices with their start and end apart: 4, of which 3 were waited for; matrix products, arithmetic and copies ran while one was open for 8% of the time, Pallas kernels for 0%

profile of v1, /device:TPU:8, one launch (start us, length us, event | category | flops | bytes accessed | tf_op | source)
XLA Modules:
  0.0 251.7 jit_solution(776631761340296787)
XLA Ops:
  7.2 0.0 all-gather.2.cloned.1.call-start
  7.2 0.7 all-gather.2.cloned.1.call-update
  7.9 2.1 broadcast_in_dim.22
  10.0 13.2 %all-to-all-start = ((f32[32,32,384]{2,1,0:T(8,128)}), f32[32,32,384]{2,1,0:T(8,128)S(1)}, u32[]{:S(2)}, u32[]{:S(2)}) async-start(f32[32,32,384]{2,1,0:T(8,128)} %broadcast_in_dim.22), calls=%async_computation | async-start | bytes 3145728 | tf_op jit(solution)/shard_map/all_to_all | solution.py:16
  23.2 32.4 %all-gather.2.cloned.1.call-done = f32[1024,384]{0,1:T(8,128)} async-done(((f32[1024,24]{0,1:T(8,128)}), f32[1024,384]{0,1:T(8,128)}) %all-gather.2.cloned.1.call-update) | async-done | bytes 1572880 | tf_op jit(solution)/shard_map/all_gather | solution.py:32
  55.6 1.5 multiply_reduce_fusion
  57.1 5.4 %all-to-all-done = f32[32,32,384]{2,1,0:T(8,128)S(1)} async-done(((f32[32,32,384]{2,1,0:T(8,128)}), f32[32,32,384]{2,1,0:T(8,128)S(1)}, u32[]{:S(2)}, u32[]{:S(2)}) %all-to-all-start) | async-done | bytes 1572896 | tf_op jit(solution)/shard_map/all_to_all | solution.py:16
  62.5 0.2 multiply_reduce_fusion.1
  62.8 0.1 sub.87
  62.8 8.9 %fusion.4 = (f32[1024]{0:T(1024)S(1)}, f32[1024,1024]{0,1:T(8,128)S(1)}) fusion(f32[1024]{0:T(1024)S(1)} %multiply_reduce_fusion, f32[1024]{0:T(1024)S(1)} %sub.87, f32[1024,384]{1,0:T(8,128)S(1)} %bitcast.27, f32[1024,384]{0,1:T(8,128)} %all-gather.2.cloned.1.call-done), kind=kOutput, calls=%fused_computation.27 | convolution fusion | flops 4837080064 | bytes 7352320 | tf_op jit(solution)/shard_map/dot_general | solution.py:39
  71.7 0.0 copy-start
  71.7 1.9 copy-done
  73.6 0.6 exponential_reduce_fusion.5
  74.3 15.8 %all_to_all.49 = f32[32,8,128]{2,1,0:T(8,128)S(1)} all-to-all(f32[32,8,128]{2,1,0:T(8,128)S(1)} %broadcast_in_dim.23), channel_id=1, replica_groups=mesh['src'=16,'tgt'=32] {'tgt'}, dimensions={0} | all-to-all | bytes 262144 | tf_op jit(solution)/shard_map/all_to_all | solution.py:16
  90.1 0.0 copy-start.1
  90.2 2.7 %add_reduce_fusion = f32[1024]{0:T(1024)S(1)} fusion(f32[1024,1024]{0,1:T(8,128)} %copy-done, f32[1024]{0:T(1024)S(1)} %negate_bitcast_fusion.1), kind=kLoop, calls=%fused_computation.8 | loop fusion | flops 2096128 | bytes 4202496 | tf_op jit(solution)/shard_map/reduce_max | solution.py:51
  92.8 0.7 copy-done.1
  93.5 0.9 exponential_reduce_fusion.4
  94.5 13.9 %all_to_all.50 = f32[16,8,128]{2,1,0:T(8,128)S(1)} all-to-all(f32[16,8,128]{2,1,0:T(8,128)S(1)} %broadcast_in_dim.24), channel_id=1, replica_groups=mesh['src'=16,'tgt'=32] {'src'}, dimensions={0} | all-to-all | bytes 131072 | tf_op jit(solution)/shard_map/all_to_all | solution.py:16
  108.5 2.9 %exponential_reduce_fusion.3 = f32[1024]{0:T(1024)S(1)} fusion(f32[1024,1024]{0,1:T(8,128)} %copy-done, f32[1024]{0:T(1024)S(1)} %negate_bitcast_fusion, f32[1024]{0:T(1024)S(1)} %negate_bitcast_fusion.1), kind=kLoop, calls=%fused_computation.4 | loop fusion | flops 3144704 | bytes 4206592 | tf_op jit(solution)/shard_map/reduce_sum | solution.py:54
  111.4 14.2 %all_to_all.51 = f32[32,8,128]{2,1,0:T(8,128)S(1)} all-to-all(f32[32,8,128]{2,1,0:T(8,128)S(1)} %broadcast_in_dim.26), channel_id=1, replica_groups=mesh['src'=16,'tgt'=32] {'tgt'}, dimensions={0} | all-to-all | bytes 262144 | tf_op jit(solution)/shard_map/all_to_all | solution.py:16
  125.6 3.1 %exponential_reduce_fusion.2 = f32[1024]{0:T(1024)S(1)} fusion(f32[1024,1024]{0,1:T(8,128)} %copy-done, f32[1024]{0:T(1024)S(1)} %bitcast_subtract_fusion.3, f32[1024]{0:T(1024)S(1)} %negate_bitcast_fusion), kind=kLoop, calls=%fused_computation.3 | loop fusion | flops 3144704 | bytes 4206592 | tf_op jit(solution)/shard_map/reduce_sum | solution.py:56
  128.7 10.5 %all_to_all.52 = f32[16,8,128]{2,1,0:T(8,128)S(1)} all-to-all(f32[16,8,128]{2,1,0:T(8,128)S(1)} %broadcast_in_dim.28), channel_id=1, replica_groups=mesh['src'=16,'tgt'=32] {'src'}, dimensions={0} | all-to-all | bytes 131072 | tf_op jit(solution)/shard_map/all_to_all | solution.py:16
  139.2 2.9 %exponential_reduce_fusion.1 = f32[1024]{0:T(1024)S(1)} fusion(f32[1024,1024]{0,1:T(8,128)} %copy-done, f32[1024]{0:T(1024)S(1)} %bitcast_subtract_fusion.2, f32[1024]{0:T(1024)S(1)} %bitcast_subtract_fusion.3), kind=kLoop, calls=%fused_computation.2 | loop fusion | flops 3144704 | bytes 4206592 | tf_op jit(solution)/shard_map/reduce_sum | solution.py:54
  142.2 14.2 %all_to_all.53 = f32[32,8,128]{2,1,0:T(8,128)S(1)} all-to-all(f32[32,8,128]{2,1,0:T(8,128)S(1)} %broadcast_in_dim.30), channel_id=1, replica_groups=mesh['src'=16,'tgt'=32] {'tgt'}, dimensions={0} | all-to-all | bytes 262144 | tf_op jit(solution)/shard_map/all_to_all | solution.py:16
  156.5 0.0 copy-start.2
  156.5 3.2 %exponential_reduce_fusion = f32[1024]{0:T(1024)S(1)} fusion(f32[1024,1024]{0,1:T(8,128)} %copy-done, f32[1024]{0:T(1024)S(1)} %bitcast_subtract_fusion.1, f32[1024]{0:T(1024)S(1)} %bitcast_subtract_fusion.2), kind=kLoop, calls=%fused_computation.1 | loop fusion | flops 3144704 | bytes 4206592 | tf_op jit(solution)/shard_map/reduce_sum | solution.py:56
  159.7 10.5 %all_to_all.54 = f32[16,8,128]{2,1,0:T(8,128)S(1)} all-to-all(f32[16,8,128]{2,1,0:T(8,128)S(1)} %broadcast_in_dim.32), channel_id=1, replica_groups=mesh['src'=16,'tgt'=32] {'src'}, dimensions={0} | all-to-all | bytes 131072 | tf_op jit(solution)/shard_map/all_to_all | solution.py:16
  170.2 0.6 broadcast_multiply_fusion
  170.8 2.9 %fusion = f32[1024]{0:T(1024)S(1)} fusion(f32[1024,1024]{0,1:T(8,128)} %copy-done, f32[1024]{0:T(1024)S(1)} %get-tuple-element.3, f32[1024]{0:T(1024)S(1)} %bitcast_subtract_fusion.1), kind=kLoop, calls=%fused_computation.9 | loop fusion | flops 3144704 | bytes 4206592 | tf_op jit(solution)/shard_map/reduce_sum | solution.py:59
  173.8 0.7 all_to_all.38
  174.5 4.0 %all-to-all-start.8 = ((f32[32,1,32]{2,1,0:T(1,128)}), f32[32,1,32]{2,1,0:T(1,128)S(1)}, u32[]{:S(2)}, u32[]{:S(2)}) async-start(f32[32,1,32]{2,1,0:T(1,128)} %all_to_all.38), calls=%async_computation.8 | async-start | bytes 32768 | tf_op jit(solution)/shard_map/all_to_all | solution.py:65
  178.5 0.0 copy-done.2
  178.5 16.3 %fusion.1 = f32[1024,384]{1,0:T(8,128)} fusion(f32[1024,384]{0,1:T(8,128)S(1)} %copy-done.2, f32[1024,1024]{0,1:T(8,128)} %copy-done, f32[1024]{0:T(1024)S(1)} %get-tuple-element.3, f32[1024]{0:T(1024)S(1)} %bitcast_subtract_fusion.1), kind=kOutput, calls=%fused_computation.10 | convolution fusion | flops 4833935360 | bytes 7348224 | tf_op jit(solution)/shard_map/dot_general | solution.py:60
  194.9 0.0 copy-start.3
  194.9 0.0 all-to-all-done.8
  194.9 9.7 %all-to-all-start.7 = ((f32[32,32,384]{2,1,0:T(8,128)}), f32[32,32,384]{2,1,0:T(8,128)S(1)}, u32[]{:S(2)}, u32[]{:S(2)}) async-start(f32[32,32,384]{2,1,0:T(8,128)} %bitcast.13), calls=%async_computation.7 | async-start | bytes 3145728 | tf_op jit(solution)/shard_map/all_to_all | solution.py:64
  204.6 39.4 %all-to-all-done.7 = f32[32,32,384]{2,1,0:T(8,128)S(1)} async-done(((f32[32,32,384]{2,1,0:T(8,128)}), f32[32,32,384]{2,1,0:T(8,128)S(1)}, u32[]{:S(2)}, u32[]{:S(2)}) %all-to-all-start.7) | async-done | bytes 1572896 | tf_op jit(solution)/shard_map/all_to_all | solution.py:64
  244.0 0.1 reduce_sum.167
  244.1 0.0 copy-done.3
  244.1 0.7 divide_subtract_fusion
  (22 shorter events, 0.4 us)
Async XLA Ops:
  7.2 48.4 %all-gather.2.cloned.1.call-start = ((), (), s32[]{:S(2)}) async-start(), calls=%async_computation.9 | async-start | bytes 1671168 | tf_op jit(solution)/shard_map/all_gather | solution.py:32
  10.0 52.5 %all-to-all-start = ((f32[32,32,384]{2,1,0:T(8,128)}), f32[32,32,384]{2,1,0:T(8,128)S(1)}, u32[]{:S(2)}, u32[]{:S(2)}) async-start(f32[32,32,384]{2,1,0:T(8,128)} %broadcast_in_dim.22), calls=%async_computation | async-start | bytes 3145728 | tf_op jit(solution)/shard_map/all_to_all | solution.py:16
  71.7 1.9 copy-start
  90.1 3.4 %copy-start.1 = (f32[1024,1024]{0,1:T(8,128)S(1)}, f32[1024,1024]{0,1:T(8,128)}, u32[]{:S(2)}) copy-start(f32[1024,1024]{0,1:T(8,128)} %copy-done) | copy-start | bytes 12582916
  156.5 22.0 %copy-start.2 = (f32[1024,384]{0,1:T(8,128)S(1)}, f32[1024,384]{0,1:T(8,128)}, u32[]{:S(2)}) copy-start(f32[1024,384]{0,1:T(8,128)} %all-gather.2.cloned.1.call-done) | copy-start | bytes 4718596
  174.5 20.4 %all-to-all-start.8 = ((f32[32,1,32]{2,1,0:T(1,128)}), f32[32,1,32]{2,1,0:T(1,128)S(1)}, u32[]{:S(2)}, u32[]{:S(2)}) async-start(f32[32,1,32]{2,1,0:T(1,128)} %all_to_all.38), calls=%async_computation.8 | async-start | bytes 32768 | tf_op jit(solution)/shard_map/all_to_all | solution.py:65
  194.9 49.3 %copy-start.3 = (f32[32,384]{1,0:T(8,128)S(1)}, f32[32,384]{1,0:T(8,128)}, u32[]{:S(2)}) copy-start(f32[32,384]{1,0:T(8,128)} %param.2) | copy-start | bytes 147460
  194.9 49.2 %all-to-all-start.7 = ((f32[32,32,384]{2,1,0:T(8,128)}), f32[32,32,384]{2,1,0:T(8,128)S(1)}, u32[]{:S(2)}, u32[]{:S(2)}) async-start(f32[32,32,384]{2,1,0:T(8,128)} %bitcast.13), calls=%async_computation.7 | async-start | bytes 3145728 | tf_op jit(solution)/shard_map/all_to_all | solution.py:64
Sparse Core Ops, SparseCore 0:
  10.1 45.4 all-gather.1

commit v2 on v1

--- a/solution.py
+++ b/solution.py
@@ -3,12 +3,13 @@
 import jax
 import jax.numpy as jnp
 from jax import lax
-from jax.sharding import PartitionSpec as P
+from jax.sharding import Mesh, PartitionSpec as P
 
 ITERS = 3
 
 
 EPS = 0.05
+SRC = ("y", "core")
 
 
 def spread(value, axis):
@@ -29,10 +30,21 @@
 
 
 def per_device(noise, data):
-    target_rows = lax.all_gather(data, "src", axis=1, tiled=True)
     own_rows, feat_width = noise.shape
+    count = lax.axis_size("y")
+    pair = lax.all_gather(data.T, "core").reshape(-1, data.shape[0])
     source_rows = spread(noise, "tgt").reshape(-1, feat_width)
-    src_total = source_rows.shape[0] * lax.axis_size("src")
+    slices = [pair] + [
+        lax.ppermute(pair, "y", [(i, (i + hop) % count) for i in range(count)])
+        for hop in range(1, count)
+    ]
+    at = lax.axis_index("y")
+    held = jnp.zeros((count * pair.shape[0], pair.shape[1]), jnp.float32)
+    for hop, piece in enumerate(slices):
+        start = (at + count - hop) % count * pair.shape[0]
+        held = lax.dynamic_update_slice_in_dim(held, piece, start, 0)
+    target_rows = held.T
+    src_total = source_rows.shape[0] * lax.axis_size(SRC)
     tgt_total = target_rows.shape[0] * lax.axis_size("tgt")
     source_sq = jnp.sum(source_rows * source_rows, axis=1)
     target_sq = jnp.sum(target_rows * target_rows, axis=1)
@@ -49,12 +61,12 @@
     f_pot = -(log_src + lse_over(top, jnp.sum(jnp.exp(gain - top[:, None]), axis=1), "tgt"))
     z_tile = f_pot[:, None] + gain
     top = jnp.max(z_tile, axis=0)
-    g_pot = -(log_tgt + lse_over(top, jnp.sum(jnp.exp(z_tile - top[None, :]), axis=0), "src"))
-    for step_index in range(1, ITERS):
+    g_pot = -(log_tgt + lse_over(top, jnp.sum(jnp.exp(z_tile - top[None, :]), axis=0), SRC))
+    for _ in range(1, ITERS):
         mass = jnp.sum(jnp.exp((f_pot[:, None] + gain) + g_pot[None, :]), axis=1)
         f_pot = f_pot - (log_src + jnp.log(total_over(mass, "tgt")))
         mass = jnp.sum(jnp.exp((f_pot[:, None] + gain) + g_pot[None, :]), axis=0)
-        g_pot = g_pot - (log_tgt + jnp.log(total_over(mass, "src")))
+        g_pot = g_pot - (log_tgt + jnp.log(total_over(mass, SRC)))
     plan = jnp.exp((f_pot[:, None] + gain) + g_pot[None, :])
     mass = jnp.sum(plan, axis=1)
     part = jnp.dot(
@@ -68,11 +80,12 @@
 
 
 def solution(mesh):
-    placed = (P(("src", "tgt"), None), P("tgt", "src"))
+    src, tgt = mesh.shape["src"], mesh.shape["tgt"]
+    split = Mesh(mesh.devices.reshape(src // 2, 2, tgt), ("y", "core", "tgt"))
     return jax.shard_map(
         per_device,
-        mesh=mesh,
-        in_specs=placed,
-        out_specs=(P(("src", "tgt"), None), P("tgt")),
+        mesh=split,
+        in_specs=(P((*SRC, "tgt"), None), P("tgt", SRC)),
+        out_specs=(P((*SRC, "tgt"), None), P("tgt")),
         check_vma=False,
     )

time: 253 us -> 259 us (1.024)
  starting transfers between devices: 27 us -> 54.3 us
  waiting for transfers between devices: 77.9 us -> 54.9 us
  between operations: 14.2 us -> 1.08 us
  blocking collectives: 79.1 us -> 86.8 us
  local copies, waits for them, and re-layouts: 5.58 us -> 9 us
    all_gather x1 -> x0, waiting for transfers between devices: 32.4 us -> none  [per_device(): target_rows = lax.all_gather(data, 'src', axis=1, tiled=True)]
    ppermute x0 -> x7, starting transfers between devices: none -> 27.3 us  [per_device(): lax.ppermute(pair, 'y', [(i, (i + hop) % count) for i in range(count)])]
    ppermute x0 -> x7, waiting for transfers between devices: none -> 15.5 us  [per_device(): lax.ppermute(pair, 'y', [(i, (i + hop) % count) for i in range(count)])]
    all_to_all x6, blocking collectives: 79.1 us -> 84.8 us  [spread(): lax.all_to_all(jnp.broadcast_to(value[None], (count,) + value.shape), axi...]
    all_to_all x1, waiting for transfers between devices: 5.41 us -> 0.01 us  [spread(): lax.all_to_all(jnp.broadcast_to(value[None], (count,) + value.shape), axi...]
    dynamic_update_slice x0 -> x8, local copies, waits for them, and re-layouts: none -> 3.86 us  [per_device(): held = lax.dynamic_update_slice_in_dim(held, piece, start, 0)]
  transfers between devices with their start and end apart: 4 -> 10, of which waited for: 3 -> 5; matrix products, arithmetic and copies ran while one was open for 8% -> 8% of each run, Pallas kernels for 0% -> 0%
where the time goes in v2:
time: 259 us; the launch traced here: 258 us
  blocking collectives  86.8 us (34%)
  waiting for transfers between devices  54.9 us (21%)
  starting transfers between devices  54.3 us (21%)
  matrix products  27.6 us (11%)
  other arithmetic  24.3 us (9%)
  local copies, waits for them, and re-layouts  9 us (3%)
    all_to_all x6, blocking collectives, spread(): lax.all_to_all(jnp.broadcast_to(value[None], (count,) + value.shape), axi...  84.8 us
    all_to_all x1, waiting for transfers between devices, per_device(): lax.all_to_all(part.reshape(count, own_rows, feat_width), 'tgt', 0, 0)  39.4 us
    ppermute x7, starting transfers between devices, per_device(): lax.ppermute(pair, 'y', [(i, (i + hop) % count) for i in range(count)])  27.3 us
    dot_general x1, matrix products, per_device(): jnp.dot(plan, target_rows, precision=lax.Precision.HIGHEST, preferred_ele...  16.8 us
    ppermute x7, waiting for transfers between devices, per_device(): lax.ppermute(pair, 'y', [(i, (i + hop) % count) for i in range(count)])  15.5 us
    all_to_all x1, starting transfers between devices, spread(): lax.all_to_all(jnp.broadcast_to(value[None], (count,) + value.shape), axi...  13.2 us
    dot_general x1, matrix products, per_device(): jnp.dot(source_rows, target_rows.T, precision=lax.Precision.HIGHEST, pref...  10.8 us
    all_to_all x1, starting transfers between devices, per_device(): lax.all_to_all(part.reshape(count, own_rows, feat_width), 'tgt', 0, 0)  9.7 us
  transfers between devices with their start and end apart: 10, of which 5 were waited for; matrix products, arithmetic and copies ran while one was open for 8% of the time, Pallas kernels for 0%

profile of v2, /device:TPU:8, one launch (start us, length us, event | category | flops | bytes accessed | tf_op | source)
XLA Modules:
  0.0 257.9 jit_solution(3329266819173216320)
XLA Ops:
  0.6 0.0 copy-start.3
  0.6 2.2 broadcast_in_dim.25
  2.8 13.2 %all-to-all-start = ((f32[32,32,384]{2,1,0:T(8,128)}), f32[32,32,384]{2,1,0:T(8,128)S(1)}, u32[]{:S(2)}, u32[]{:S(2)}) async-start(f32[32,32,384]{2,1,0:T(8,128)} %broadcast_in_dim.25), calls=%async_computation | async-start | bytes 3145728 | tf_op jit(solution)/shard_map/all_to_all | solution.py:17
  16.0 0.0 copy-done.3
  16.0 1.9 all-gather
  17.9 3.5 %collective-permute-start = (f32[48,1024]{1,0:T(8,128)S(1)}, f32[48,1024]{1,0:T(8,128)}, u32[]{:S(2)}, u32[]{:S(2)}) collective-permute-start(f32[48,1024]{1,0:T(8,128)S(1)} %all-gather), channel_id=1, source_target_pairs={{0,64},{64,128},{128,192},{192,256},{256,320},{320,384},{384,448},... | collective-permute-start | bytes 589832 | tf_op jit(solution)/shard_map/ppermute | solution.py:38
  21.4 3.7 %collective-permute-start.5 = (f32[48,1024]{1,0:T(8,128)S(1)}, f32[48,1024]{1,0:T(8,128)S(1)}, u32[]{:S(2)}, u32[]{:S(2)}) collective-permute-start(f32[48,1024]{1,0:T(8,128)S(1)} %all-gather), channel_id=1, source_target_pairs={{0,384},{64,448},{128,0},{192,64},{256,128},{320,192},{384,256},{4... | collective-permute-start | bytes 589832 | tf_op jit(solution)/shard_map/ppermute | solution.py:38
  25.1 5.5 %collective-permute-start.4 = (f32[48,1024]{1,0:T(8,128)S(1)}, f32[48,1024]{1,0:T(8,128)}, u32[]{:S(2)}, u32[]{:S(2)}) collective-permute-start(f32[48,1024]{1,0:T(8,128)S(1)} %all-gather), channel_id=1, source_target_pairs={{0,320},{64,384},{128,448},{192,0},{256,64},{320,128},{384,192},{4... | collective-permute-start | bytes 589832 | tf_op jit(solution)/shard_map/ppermute | solution.py:38
  30.6 3.9 %collective-permute-start.3 = (f32[48,1024]{1,0:T(8,128)S(1)}, f32[48,1024]{1,0:T(8,128)}, u32[]{:S(2)}, u32[]{:S(2)}) collective-permute-start(f32[48,1024]{1,0:T(8,128)S(1)} %all-gather), channel_id=1, source_target_pairs={{0,256},{64,320},{128,384},{192,448},{256,0},{320,64},{384,128},{4... | collective-permute-start | bytes 589832 | tf_op jit(solution)/shard_map/ppermute | solution.py:38
  34.6 3.5 %collective-permute-start.1 = (f32[48,1024]{1,0:T(8,128)S(1)}, f32[48,1024]{1,0:T(8,128)}, u32[]{:S(2)}, u32[]{:S(2)}) collective-permute-start(f32[48,1024]{1,0:T(8,128)S(1)} %all-gather), channel_id=1, source_target_pairs={{0,128},{64,192},{128,256},{192,320},{256,384},{320,448},{384,0},{... | collective-permute-start | bytes 589832 | tf_op jit(solution)/shard_map/ppermute | solution.py:38
  38.2 0.2 broadcast_in_dim.24
  38.4 0.0 collective-permute-done
  38.4 5.4 %collective-permute-start.2 = (f32[48,1024]{1,0:T(8,128)S(1)}, f32[48,1024]{1,0:T(8,128)S(1)}, u32[]{:S(2)}, u32[]{:S(2)}) collective-permute-start(f32[48,1024]{1,0:T(8,128)S(1)} %all-gather), channel_id=1, source_target_pairs={{0,192},{64,256},{128,320},{192,384},{256,448},{320,0},{384,64},{4... | collective-permute-start | bytes 589832 | tf_op jit(solution)/shard_map/ppermute | solution.py:38
  43.8 0.9 constant_dynamic-update-slice_fusion.6
  44.7 11.8 %collective-permute-done.1 = f32[48,1024]{1,0:T(8,128)} collective-permute-done((f32[48,1024]{1,0:T(8,128)S(1)}, f32[48,1024]{1,0:T(8,128)}, u32[]{:S(2)}, u32[]{:S(2)}) %collective-permute-start.1) | collective-permute-done | bytes 196640 | tf_op jit(solution)/shard_map/ppermute | solution.py:38
  56.5 1.9 collective-permute-start.6
  58.4 0.9 constant_dynamic-update-slice_fusion.5
  59.4 1.0 collective-permute-done.2
  60.4 0.2 collective-permute-done.3
  60.6 0.9 constant_dynamic-update-slice_fusion.3
  61.6 0.0 collective-permute-done.4
  61.6 0.9 constant_dynamic-update-slice_fusion.2
  62.5 0.0 collective-permute-done.5
  62.6 2.5 collective-permute-done.6
  65.1 0.1 multiply_reduce_fusion
  65.2 0.0 all-to-all-done
  65.2 0.2 multiply_reduce_fusion.1
  65.4 0.1 sub.117
  65.5 10.8 %fusion.4 = (f32[1024]{0:T(1024)S(1)}, f32[1024,1024]{1,0:T(8,128)S(1)}) fusion(f32[1024]{0:T(1024)S(1)} %multiply_reduce_fusion, f32[1024]{0:T(1024)S(1)} %sub.117, f32[384,1024]{1,0:T(8,128)S(1)} %constant_dynamic-update-slice_fusion, f32[1024,384]{1,0:T(8,128)S(1)} %bitcast.28), kind=kOutput, calls=%fused_computation.35 | convolution fusion | flops 4837080064 | bytes 7352320 | tf_op jit(solution)/shard_map/dot_general | solution.py:51
  76.3 0.0 copy-start
  76.3 1.9 copy-done
  78.2 1.3 exponential_reduce_fusion.5
  79.6 20.0 %all_to_all.49 = f32[32,8,128]{2,1,0:T(8,128)S(1)} all-to-all(f32[32,8,128]{2,1,0:T(8,128)S(1)} %broadcast_in_dim.26), channel_id=1, replica_groups=mesh['y'=8,'core'=2,'tgt'=32] {'tgt'}, dimensions={0} | all-to-all | bytes 262144 | tf_op jit(solution)/shard_map/all_to_all | solution.py:17
  99.6 0.0 copy-start.1
  99.7 3.3 %add_reduce_fusion = f32[1024]{0:T(1024)S(1)} fusion(f32[1024]{0:T(1024)S(1)} %negate_bitcast_fusion.1, f32[1024]{0:T(1024)S(1)} %multiply_reduce_fusion, f32[1024]{0:T(1024)S(1)} %sub.117, f32[1024,1024]{1,0:T(8,128)} %copy-done), kind=kLoop, calls=%fused_computation.8 | loop fusion | flops 6290432 | bytes 4210688 | tf_op jit(solution)/shard_map/reduce_max | solution.py:63
  103.0 0.1 copy-done.1
  103.0 1.9 exponential_reduce_fusion.4
  105.0 15.3 %all_to_all.50 = f32[16,8,128]{2,1,0:T(8,128)S(1)} all-to-all(f32[16,8,128]{2,1,0:T(8,128)S(1)} %broadcast_in_dim.27), channel_id=1, replica_groups=mesh['y'=8,'core'=2,'tgt'=32] {'y','core'}, dimensions={0} | all-to-all | bytes 131072 | tf_op jit(solution)/shard_map/all_to_all | solution.py:17
  120.3 3.0 %exponential_reduce_fusion.3 = f32[1024]{0:T(1024)S(1)} fusion(f32[1024]{0:T(1024)S(1)} %negate_bitcast_fusion, f32[1024]{0:T(1024)S(1)} %negate_bitcast_fusion.1, f32[1024]{0:T(1024)S(1)} %multiply_reduce_fusion, f32[1024]{0:T(1024)S(1)} %sub.117, f32[1024,1024]{1,0:T(8,128)} %copy-done), kind=kLoop, calls=%fused_computation.3 | loop fusion | flops 7339008 | bytes 4214784 | tf_op jit(solution)/shard_map/reduce_sum | solution.py:66
  123.3 14.3 %all_to_all.51 = f32[32,8,128]{2,1,0:T(8,128)S(1)} all-to-all(f32[32,8,128]{2,1,0:T(8,128)S(1)} %broadcast_in_dim.29), channel_id=1, replica_groups=mesh['y'=8,'core'=2,'tgt'=32] {'tgt'}, dimensions={0} | all-to-all | bytes 262144 | tf_op jit(solution)/shard_map/all_to_all | solution.py:17
  137.7 3.3 %exponential_reduce_fusion.2 = f32[1024]{0:T(1024)S(1)} fusion(f32[1024]{0:T(1024)S(1)} %negate_bitcast_fusion, f32[1024]{0:T(1024)S(1)} %bitcast_subtract_fusion.3, f32[1024]{0:T(1024)S(1)} %multiply_reduce_fusion, f32[1024]{0:T(1024)S(1)} %sub.117, f32[1024,1024]{1,0:T(8,128)} %copy-done), kind=kLoop, calls=%fused_computation.2 | loop fusion | flops 7339008 | bytes 4214784 | tf_op jit(solution)/shard_map/reduce_sum | solution.py:68
  141.1 10.5 %all_to_all.52 = f32[16,8,128]{2,1,0:T(8,128)S(1)} all-to-all(f32[16,8,128]{2,1,0:T(8,128)S(1)} %broadcast_in_dim.31), channel_id=1, replica_groups=mesh['y'=8,'core'=2,'tgt'=32] {'y','core'}, dimensions={0} | all-to-all | bytes 131072 | tf_op jit(solution)/shard_map/all_to_all | solution.py:17
  151.6 3.0 %exponential_reduce_fusion.1 = f32[1024]{0:T(1024)S(1)} fusion(f32[1024]{0:T(1024)S(1)} %bitcast_subtract_fusion.2, f32[1024]{0:T(1024)S(1)} %bitcast_subtract_fusion.3, f32[1024]{0:T(1024)S(1)} %multiply_reduce_fusion, f32[1024]{0:T(1024)S(1)} %sub.117, f32[1024,1024]{1,0:T(8,128)} %copy-done), kind=kLoop, calls=%fused_computation.1 | loop fusion | flops 7339008 | bytes 4214784 | tf_op jit(solution)/shard_map/reduce_sum | solution.py:66
  154.6 14.2 %all_to_all.53 = f32[32,8,128]{2,1,0:T(8,128)S(1)} all-to-all(f32[32,8,128]{2,1,0:T(8,128)S(1)} %broadcast_in_dim.33), channel_id=1, replica_groups=mesh['y'=8,'core'=2,'tgt'=32] {'tgt'}, dimensions={0} | all-to-all | bytes 262144 | tf_op jit(solution)/shard_map/all_to_all | solution.py:17
  168.9 3.3 %exponential_reduce_fusion = f32[1024]{0:T(1024)S(1)} fusion(f32[1024]{0:T(1024)S(1)} %bitcast_subtract_fusion.2, f32[1024]{0:T(1024)S(1)} %bitcast_subtract_fusion.1, f32[1024]{0:T(1024)S(1)} %multiply_reduce_fusion, f32[1024]{0:T(1024)S(1)} %sub.117, f32[1024,1024]{1,0:T(8,128)} %copy-done), kind=kLoop, calls=%fused_computation | loop fusion | flops 7339008 | bytes 4214784 | tf_op jit(solution)/shard_map/reduce_sum | solution.py:68
  172.3 10.5 %all_to_all.54 = f32[16,8,128]{2,1,0:T(8,128)S(1)} all-to-all(f32[16,8,128]{2,1,0:T(8,128)S(1)} %broadcast_in_dim.35), channel_id=1, replica_groups=mesh['y'=8,'core'=2,'tgt'=32] {'y','core'}, dimensions={0} | all-to-all | bytes 131072 | tf_op jit(solution)/shard_map/all_to_all | solution.py:17
  182.8 0.6 broadcast_multiply_fusion
  183.4 3.0 %fusion = f32[1024]{0:T(1024)S(1)} fusion(f32[1024]{0:T(1024)S(1)} %get-tuple-element.3, f32[1024]{0:T(1024)S(1)} %bitcast_subtract_fusion.1, f32[1024]{0:T(1024)S(1)} %multiply_reduce_fusion, f32[1024]{0:T(1024)S(1)} %sub.117, f32[1024,1024]{1,0:T(8,128)} %copy-done), kind=kLoop, calls=%fused_computation.9 | loop fusion | flops 7339008 | bytes 4214784 | tf_op jit(solution)/shard_map/reduce_sum | solution.py:71
  186.4 0.7 all_to_all.38
  187.1 4.0 %all-to-all-start.8 = ((f32[32,1,32]{2,1,0:T(1,128)}), f32[32,1,32]{2,1,0:T(1,128)S(1)}, u32[]{:S(2)}, u32[]{:S(2)}) async-start(f32[32,1,32]{2,1,0:T(1,128)} %all_to_all.38), calls=%async_computation.8 | async-start | bytes 32768 | tf_op jit(solution)/shard_map/all_to_all | solution.py:77
  191.1 16.8 %fusion.1 = f32[1024,384]{1,0:T(8,128)} fusion(f32[384,1024]{1,0:T(8,128)S(1)} %constant_dynamic-update-slice_fusion, f32[1024]{0:T(1024)S(1)} %get-tuple-element.3, f32[1024]{0:T(1024)S(1)} %bitcast_subtract_fusion.1, f32[1024,1024]{1,0:T(8,128)} %copy-done, f32[1024]{0:T(1024)S(1)} %multiply_reduce_fusion, f32[1024]{0:T(1024)S(1)} %sub.117), kind=kOutput, calls=%fused_computation.10 | convolution fusion | flops 4838129664 | bytes 7356416 | tf_op jit(solution)/shard_map/dot_general | solution.py:72
  207.9 0.0 copy-start.2
  207.9 0.0 all-to-all-done.8
  207.9 9.7 %all-to-all-start.7 = ((f32[32,32,384]{2,1,0:T(8,128)}), f32[32,32,384]{2,1,0:T(8,128)S(1)}, u32[]{:S(2)}, u32[]{:S(2)}) async-start(f32[32,32,384]{2,1,0:T(8,128)} %bitcast.29), calls=%async_computation.7 | async-start | bytes 3145728 | tf_op jit(solution)/shard_map/all_to_all | solution.py:76
  217.7 39.4 %all-to-all-done.7 = f32[32,32,384]{2,1,0:T(8,128)S(1)} async-done(((f32[32,32,384]{2,1,0:T(8,128)}), f32[32,32,384]{2,1,0:T(8,128)S(1)}, u32[]{:S(2)}, u32[]{:S(2)}) %all-to-all-start.7) | async-done | bytes 1572896 | tf_op jit(solution)/shard_map/all_to_all | solution.py:76
  257.1 0.1 reduce_sum.167
  257.2 0.0 copy-done.2
  257.2 0.7 divide_subtract_fusion
  (26 shorter events, 0.4 us)
Async XLA Ops:
  0.6 15.4 %copy-start.3 = (f32[1024,24]{0,1:T(8,128)S(1)}, f32[1024,24]{0,1:T(8,128)}, u32[]{:S(2)}) copy-start(f32[1024,24]{0,1:T(8,128)} %param.3) | copy-start | bytes 294916
  2.8 62.4 %all-to-all-start = ((f32[32,32,384]{2,1,0:T(8,128)}), f32[32,32,384]{2,1,0:T(8,128)S(1)}, u32[]{:S(2)}, u32[]{:S(2)}) async-start(f32[32,32,384]{2,1,0:T(8,128)} %broadcast_in_dim.25), calls=%async_computation | async-start | bytes 3145728 | tf_op jit(solution)/shard_map/all_to_all | solution.py:17
  17.9 20.5 %collective-permute-start = (f32[48,1024]{1,0:T(8,128)S(1)}, f32[48,1024]{1,0:T(8,128)}, u32[]{:S(2)}, u32[]{:S(2)}) collective-permute-start(f32[48,1024]{1,0:T(8,128)S(1)} %all-gather), channel_id=1, source_target_pairs={{0,64},{64,128},{128,192},{192,256},{256,320},{320,384},{384,448},... | collective-permute-start | bytes 589832 | tf_op jit(solution)/shard_map/ppermute | solution.py:38
  21.4 41.1 %collective-permute-start.5 = (f32[48,1024]{1,0:T(8,128)S(1)}, f32[48,1024]{1,0:T(8,128)S(1)}, u32[]{:S(2)}, u32[]{:S(2)}) collective-permute-start(f32[48,1024]{1,0:T(8,128)S(1)} %all-gather), channel_id=1, source_target_pairs={{0,384},{64,448},{128,0},{192,64},{256,128},{320,192},{384,256},{4... | collective-permute-start | bytes 589832 | tf_op jit(solution)/shard_map/ppermute | solution.py:38
  25.1 36.5 %collective-permute-start.4 = (f32[48,1024]{1,0:T(8,128)S(1)}, f32[48,1024]{1,0:T(8,128)}, u32[]{:S(2)}, u32[]{:S(2)}) collective-permute-start(f32[48,1024]{1,0:T(8,128)S(1)} %all-gather), channel_id=1, source_target_pairs={{0,320},{64,384},{128,448},{192,0},{256,64},{320,128},{384,192},{4... | collective-permute-start | bytes 589832 | tf_op jit(solution)/shard_map/ppermute | solution.py:38
  30.6 30.0 %collective-permute-start.3 = (f32[48,1024]{1,0:T(8,128)S(1)}, f32[48,1024]{1,0:T(8,128)}, u32[]{:S(2)}, u32[]{:S(2)}) collective-permute-start(f32[48,1024]{1,0:T(8,128)S(1)} %all-gather), channel_id=1, source_target_pairs={{0,256},{64,320},{128,384},{192,448},{256,0},{320,64},{384,128},{4... | collective-permute-start | bytes 589832 | tf_op jit(solution)/shard_map/ppermute | solution.py:38
  34.6 21.9 %collective-permute-start.1 = (f32[48,1024]{1,0:T(8,128)S(1)}, f32[48,1024]{1,0:T(8,128)}, u32[]{:S(2)}, u32[]{:S(2)}) collective-permute-start(f32[48,1024]{1,0:T(8,128)S(1)} %all-gather), channel_id=1, source_target_pairs={{0,128},{64,192},{128,256},{192,320},{256,384},{320,448},{384,0},{... | collective-permute-start | bytes 589832 | tf_op jit(solution)/shard_map/ppermute | solution.py:38
  38.4 22.0 %collective-permute-start.2 = (f32[48,1024]{1,0:T(8,128)S(1)}, f32[48,1024]{1,0:T(8,128)S(1)}, u32[]{:S(2)}, u32[]{:S(2)}) collective-permute-start(f32[48,1024]{1,0:T(8,128)S(1)} %all-gather), channel_id=1, source_target_pairs={{0,192},{64,256},{128,320},{192,384},{256,448},{320,0},{384,64},{4... | collective-permute-start | bytes 589832 | tf_op jit(solution)/shard_map/ppermute | solution.py:38
  56.5 8.6 %collective-permute-start.6 = (f32[48,1024]{1,0:T(8,128)S(1)}, f32[48,1024]{1,0:T(8,128)S(1)}, u32[]{:S(2)}, u32[]{:S(2)}) collective-permute-start(f32[48,1024]{1,0:T(8,128)S(1)} %all-gather), channel_id=1, source_target_pairs={{0,448},{64,0},{128,64},{192,128},{256,192},{320,256},{384,320},{4... | collective-permute-start | bytes 589832 | tf_op jit(solution)/shard_map/ppermute | solution.py:38
  76.3 1.9 copy-start
  99.6 3.4 %copy-start.1 = (f32[1024,1024]{1,0:T(8,128)S(1)}, f32[1024,1024]{1,0:T(8,128)}, u32[]{:S(2)}) copy-start(f32[1024,1024]{1,0:T(8,128)} %copy-done) | copy-start | bytes 12582916
  187.1 20.9 %all-to-all-start.8 = ((f32[32,1,32]{2,1,0:T(1,128)}), f32[32,1,32]{2,1,0:T(1,128)S(1)}, u32[]{:S(2)}, u32[]{:S(2)}) async-start(f32[32,1,32]{2,1,0:T(1,128)} %all_to_all.38), calls=%async_computation.8 | async-start | bytes 32768 | tf_op jit(solution)/shard_map/all_to_all | solution.py:77
  207.9 49.3 %copy-start.2 = (f32[32,384]{1,0:T(8,128)S(1)}, f32[32,384]{1,0:T(8,128)}, u32[]{:S(2)}) copy-start(f32[32,384]{1,0:T(8,128)} %param.2) | copy-start | bytes 147460
  207.9 49.2 %all-to-all-start.7 = ((f32[32,32,384]{2,1,0:T(8,128)}), f32[32,32,384]{2,1,0:T(8,128)S(1)}, u32[]{:S(2)}, u32[]{:S(2)}) async-start(f32[32,32,384]{2,1,0:T(8,128)} %bitcast.29), calls=%async_computation.7 | async-start | bytes 3145728 | tf_op jit(solution)/shard_map/all_to_all | solution.py:76

commit v3 on v1

v3 whole, which is shorter than its diff:
```python
import functools
import math

import jax
import jax.numpy as jnp
from jax import lax
from jax.experimental import pallas as pl
from jax.experimental.pallas import tpu as pltpu
from jax.sharding import Mesh, PartitionSpec as P

ITERS = 3


EPS = 0.05
LANES = 128
BLOCK = 256
X_CHIPS = 4
INTERPRET = False
SRC, TGT = ("y", "core"), ("x", "z")
F32 = jnp.float32


def spread(value, axis):
    count = lax.axis_size(axis)
    return lax.all_to_all(jnp.broadcast_to(value[None], (count,) + value.shape), axis, 0, 0)


def diagonal():
    shape = (LANES, LANES)
    return lax.broadcasted_iota(jnp.int32, shape, 0) == lax.broadcasted_iota(jnp.int32, shape, 1)


def down(row):
    return jnp.sum(jnp.where(diagonal(), row, 0.0), axis=1, keepdims=True)


def across(column):
    return jnp.sum(jnp.where(diagonal(), column, 0.0), axis=0, keepdims=True)


def flat(tiles):
    return jnp.concatenate([tiles[t : t + 1] for t in range(tiles.shape[0])], axis=1)


def merged(ref):
    parts = ref[...]
    top = jnp.max(parts, axis=0)
    return top + jnp.log(jnp.sum(jnp.exp(parts - top[None]), axis=0))


def send(out_ref, tiles):
    out_ref[...] = jnp.broadcast_to(tiles[None], out_ref.shape)


def cost_kernel(noise_ref, data_ref, gain_ref, out_ref, rows_ref):
    data = data_ref[...]
    scale = 1.0 / (data.shape[0] * EPS)
    data_sq = jnp.sum(data * data, axis=0, keepdims=True)

    def block(b, carry):
        at = pl.ds(pl.multiple_of(b * BLOCK, BLOCK), BLOCK)
        rows = noise_ref[at, :]
        cross = jnp.dot(rows, data_ref[...], precision=lax.Precision.HIGHEST,
                        preferred_element_type=F32)
        gain = (2.0 * cross - jnp.sum(rows * rows, axis=1, keepdims=True) - data_sq) * scale
        gain_ref[at, :] = gain
        top = jnp.max(gain, axis=1, keepdims=True)
        lse = top + jnp.log(jnp.sum(jnp.exp(gain - top), axis=1, keepdims=True))
        for t in range(BLOCK // LANES):
            rows_ref[pl.ds(b * (BLOCK // LANES) + t, 1), :] = across(
                lse[t * LANES : (t + 1) * LANES])
        return carry

    lax.fori_loop(0, noise_ref.shape[0] // BLOCK, block, 0)
    send(out_ref, rows_ref[...])


def first_column_kernel(log_src, in_ref, gain_ref, f_ref, out_ref):
    f_pot = -(log_src + merged(in_ref))
    f_ref[...] = f_pot
    top = total = None
    for b in range(f_pot.shape[0]):
        z = gain_ref[b * LANES : (b + 1) * LANES, :] + down(f_pot[b : b + 1])
        here = jnp.max(z, axis=0, keepdims=True)
        if b == 0:
            top, total = here, jnp.sum(jnp.exp(z - here), axis=0, keepdims=True)
        else:
            new = jnp.maximum(top, here)
            total = total * jnp.exp(top - new) + jnp.sum(jnp.exp(z - new), axis=0, keepdims=True)
            top = new
    lse = top + jnp.log(total)
    for t in range(out_ref.shape[1]):
        out_ref[:, t : t + 1, :] = jnp.broadcast_to(
            lse[None, :, t * LANES : (t + 1) * LANES], (out_ref.shape[0], 1, LANES))


def plan_kernel(in_ref, f_ref, gain_ref, lse_ref, plan_ref, out_ref, rows_ref):
    lse = merged(in_ref)
    lse_ref[...] = lse
    column = flat(lse)
    for b in range(rows_ref.shape[0]):
        at = slice(b * LANES, (b + 1) * LANES)
        plan = jnp.exp((gain_ref[at, :] + down(f_ref[b : b + 1, :])) - column)
        plan_ref[at, :] = plan
        rows_ref[b : b + 1, :] = across(jnp.sum(plan, axis=1, keepdims=True))
    send(out_ref, rows_ref[...])


def column_kernel(src_total, in_ref, plan_ref, out_ref):
    u = 1.0 / (src_total * jnp.sum(in_ref[...], axis=0))
    total = jnp.zeros((1, plan_ref.shape[1]), F32)
    for b in range(u.shape[0]):
        total += jnp.sum(plan_ref[b * LANES : (b + 1) * LANES, :] * down(u[b : b + 1]),
                         axis=0, keepdims=True)
    for t in range(out_ref.shape[1]):
        out_ref[:, t : t + 1, :] = jnp.broadcast_to(
            total[None, :, t * LANES : (t + 1) * LANES], (out_ref.shape[0], 1, LANES))


def row_kernel(tgt_total, in_ref, plan_ref, out_ref, rows_ref):
    v = flat(1.0 / (tgt_total * jnp.sum(in_ref[...], axis=0)))
    for b in range(rows_ref.shape[0]):
        rows_ref[b : b + 1, :] = across(
            jnp.sum(plan_ref[b * LANES : (b + 1) * LANES, :] * v, axis=1, keepdims=True))
    send(out_ref, rows_ref[...])


def halves(value):
    high = value.astype(jnp.bfloat16)
    return high, (value - high.astype(F32)).astype(jnp.bfloat16)


def final_kernel(tgt_total, own_rows, in_ref, lse_ref, plan_ref, data_ref, g_ref, part_ref,
                 high_ref, low_ref):
    v = 1.0 / (tgt_total * jnp.sum(in_ref[...], axis=0))
    g_ref[...] = EPS * (jnp.log(v) - (math.log(tgt_total) + lse_ref[...]))
    v = flat(v)
    feats = data_ref.shape[0]
    scaled = data_ref[...] * v
    high_ref[:feats, :], low_ref[:feats, :] = halves(scaled)
    high_ref[feats:, :], low_ref[feats:, :] = halves(jnp.broadcast_to(v, (LANES, v.shape[1])))
    lane = lax.broadcasted_iota(jnp.int32, (8, LANES), 1)
    tiles, wide = own_rows // 8, feats // LANES

    def block(b, carry):
        high, low = halves(plan_ref[pl.ds(pl.multiple_of(b * BLOCK, BLOCK), BLOCK), :])

        def times(a, w_ref):
            return lax.dot_general(a, w_ref[...], (((1,), (1,)), ((), ())),
                                   preferred_element_type=F32)

        got = times(high, low_ref) + times(low, high_ref) + times(high, high_ref)
        for p in range(BLOCK // own_rows):
            peer = b * (BLOCK // own_rows) + p
            mass = jnp.zeros((8, LANES), F32)
            for r in range(tiles):
                at = slice(p * own_rows + r * 8, p * own_rows + r * 8 + 8)
                for c in range(wide):
                    part_ref[peer, (r * wide + c) * 8 : (r * wide + c + 1) * 8, :] = got[
                        at, c * LANES : (c + 1) * LANES]
                mass = jnp.where(lane // (LANES // tiles) == r, got[at, feats:], mass)
            part_ref[peer, tiles * wide * 8 :, :] = mass
        return carry

    lax.fori_loop(0, plan_ref.shape[0] // BLOCK, block, 0)


def last_kernel(in_ref, noise_ref, out_ref):
    rows, feats = noise_ref.shape
    tiles, wide = rows // 8, feats // LANES
    parts = jnp.sum(in_ref[...], axis=0)
    mass = parts[tiles * wide * 8 :]
    for r in range(tiles):
        inverse = 1.0 / mass[:, r * (LANES // tiles) : r * (LANES // tiles) + 1]
        for c in range(wide):
            at = (r * wide + c) * 8
            spot = (slice(r * 8, r * 8 + 8), slice(c * LANES, (c + 1) * LANES))
            out_ref[spot] = parts[at : at + 8] * inverse - noise_ref[spot]


def call(kernel, outs, *args, scratch=(), limit=24 << 20):
    return pl.pallas_call(
        kernel,
        out_shape=[jax.ShapeDtypeStruct(shape, F32) for shape in outs],
        in_specs=[pl.BlockSpec(memory_space=pltpu.VMEM)] * len(args),
        out_specs=[pl.BlockSpec(memory_space=pltpu.VMEM)] * len(outs),
        scratch_shapes=list(scratch),
        compiler_params=pltpu.CompilerParams(vmem_limit_bytes=limit),
        interpret=INTERPRET,
    )(*args)


def gathered(noise, data):
    count = lax.axis_size("y")
    at, core = lax.axis_index("y"), lax.axis_index("core")
    rows = spread(noise, TGT).reshape(-1, noise.shape[1])

    def shifted(value, hop):
        return lax.ppermute(value, "y", [(i, (i + hop) % count) for i in range(count)])

    own = data.T
    far = shifted(own, count // 2)
    both = jnp.stack([own, far])
    hops = [0] + [h for k in range(1, count // 4 + 1) for h in (k, -k)][: count // 2 - 1]
    mine = jnp.stack([both] + [shifted(both, h) for h in hops[1:]])
    theirs = lax.ppermute(mine, "core", [(0, 1), (1, 0)])
    pair = jnp.where(core == 0, jnp.stack([mine, theirs]), jnp.stack([theirs, mine]))
    pair = jnp.moveaxis(pair, 0, 2)
    feats, width = own.shape
    held = jnp.zeros((count, 2 * feats, width), F32)
    for k, hop in enumerate(hops):
        for h in range(2):
            place = (at - hop - h * (count // 2) + 2 * count) % count
            held = lax.dynamic_update_slice_in_dim(
                held, pair[k, h].reshape(1, 2 * feats, width), place, 0)
    return rows, held.reshape(-1, width)


def per_device(noise, data):
    own_rows, feats = noise.shape
    rows, columns = gathered(noise, data)
    n_rows, n_cols = rows.shape[0], columns.shape[1]
    n_src, n_tgt, n_x, n_z = (lax.axis_size(a) for a in (SRC, TGT, "x", "z"))
    src_total, tgt_total = n_rows * n_src, n_cols * n_tgt
    r_tiles, c_tiles = (n_rows // LANES, LANES), (n_cols // LANES, LANES)
    to_tgt, to_src = (n_tgt, *r_tiles), (n_src, *c_tiles)
    row_scratch = [pltpu.VMEM(r_tiles, F32)]
    square = (n_rows, n_cols)

    def swap(value, axis):
        return lax.all_to_all(value, axis, 0, 0)

    gain, message = call(cost_kernel, [square, to_tgt], rows, columns, scratch=row_scratch)
    f_pot, message = call(functools.partial(first_column_kernel, math.log(src_total)),
                          [r_tiles, to_src], swap(message, TGT), gain)
    lse, plan, message = call(plan_kernel, [c_tiles, square, to_tgt], swap(message, SRC), f_pot,
                              gain, scratch=row_scratch)
    for step_index in range(1, ITERS):
        if step_index > 1:
            (message,) = call(functools.partial(row_kernel, float(tgt_total)), [to_tgt],
                              swap(message, SRC), plan, scratch=row_scratch)
        (message,) = call(functools.partial(column_kernel, float(src_total)), [to_src],
                          swap(message, TGT), plan)
    tall = own_rows // 8 * (feats // LANES) * 8 + 8
    g_pot, part = call(
        functools.partial(final_kernel, float(tgt_total), own_rows),
        [c_tiles, (n_tgt, tall, LANES)], swap(message, SRC), lse, plan, columns,
        scratch=[pltpu.VMEM((feats + LANES, n_cols), jnp.bfloat16)] * 2)
    part = jnp.sum(swap(part.reshape(n_x, n_z * tall, LANES), "x"), axis=0)
    part = swap(part.reshape(n_z, tall, LANES), "z")
    (velocity,) = call(last_kernel, [noise.shape], part, noise)
    return velocity, g_pot.reshape(-1)


def solution(mesh):
    src, tgt = mesh.shape["src"], mesh.shape["tgt"]
    split = Mesh(mesh.devices.reshape(src // 2, 2, X_CHIPS, tgt // X_CHIPS), SRC + TGT)
    return jax.shard_map(
        per_device,
        mesh=split,
        in_specs=(P((*SRC, *TGT), None), P(TGT, SRC)),
        out_specs=(P((*SRC, *TGT), None), P(TGT)),
        check_vma=False,
    )
```

time: 253 us -> 198 us (0.78)
  the two profiles are of different devices: /device:TPU:8 before, /device:TPU:1 now
where the time goes in v3:
time: 198 us; the launch traced here: 197 us
  blocking collectives  122 us (62%)
  starting transfers between devices  37.5 us (19%)
  Pallas kernels  17.6 us (9%)
  waiting for transfers between devices  15.2 us (8%)
  local copies, waits for them, and re-layouts  2.66 us (1%)
    all_to_all x8, blocking collectives, swap(): return lax.all_to_all(value, axis, 0, 0)  122 us
    ppermute x4, starting transfers between devices, shifted(): lax.ppermute(value, 'y', [(i, (i + hop) % count) for i in range(count)])  19.9 us
    pallas_call x8, Pallas kernels, call(): pl.pallas_call(kernel, out_shape=[jax.ShapeDtypeStruct(shape, F32) for sh...  17.6 us
    all_to_all x1, starting transfers between devices, spread(): lax.all_to_all(jnp.broadcast_to(value[None], (count,) + value.shape), axi...  13.8 us
    ppermute x4, waiting for transfers between devices, shifted(): lax.ppermute(value, 'y', [(i, (i + hop) % count) for i in range(count)])  13.2 us
  transfers between devices with their start and end apart: 6, of which 4 were waited for; matrix products, arithmetic and copies ran while one was open for 1% of the time, Pallas kernels for 0%

profile of v3, /device:TPU:1, one launch (start us, length us, event | category | flops | bytes accessed | tf_op | source)
XLA Modules:
  0.0 197.2 jit_solution(12587644137301298840)
XLA Ops:
  0.6 2.1 %broadcast_in_dim.4 = f32[32,32,384]{2,1,0:T(8,128)} broadcast(f32[32,384]{1,0:T(8,128)} %noise_ref.1), dimensions={1,2} | broadcast | bytes 1622016 | tf_op jit(solution)/shard_map/broadcast_in_dim | solution.py:25
  2.8 0.0 copy-start.1
  2.8 13.8 %all-to-all-start = ((f32[32,32,384]{2,1,0:T(8,128)}), f32[32,32,384]{2,1,0:T(8,128)S(1)}, u32[]{:S(2)}, u32[]{:S(2)}) async-start(f32[32,32,384]{2,1,0:T(8,128)} %broadcast_in_dim.4), calls=%async_computation | async-start | bytes 3145728 | tf_op jit(solution)/shard_map/all_to_all | solution.py:25
  16.6 0.0 copy-done.1
  16.6 7.5 %collective-permute-start = (f32[24,1024]{1,0:T(8,128)S(1)}, f32[24,1024]{1,0:T(8,128)S(1)}, u32[]{:S(2)}, u32[]{:S(2)}) collective-permute-start(f32[24,1024]{1,0:T(8,128)S(1)} %bitcast.44), channel_id=1, source_target_pairs={{0,256},{64,320},{128,384},{192,448},{256,0},{320,64},{384,128},{4... | collective-permute-start | bytes 294920 | tf_op jit(solution)/shard_map/ppermute | solution.py:199
  24.1 2.1 %collective-permute-done = f32[24,1024]{1,0:T(8,128)S(1)} collective-permute-done((f32[24,1024]{1,0:T(8,128)S(1)}, f32[24,1024]{1,0:T(8,128)S(1)}, u32[]{:S(2)}, u32[]{:S(2)}) %collective-permute-start) | collective-permute-done | bytes 98336 | tf_op jit(solution)/shard_map/ppermute | solution.py:199
  26.2 7.8 %collective-permute-start.2 = (f32[2,24,1024]{2,1,0:T(8,128)S(1)}, f32[2,24,1024]{2,1,0:T(8,128)S(1)}, u32[]{:S(2)}, u32[]{:S(2)}) collective-permute-start(f32[2,24,1024]{2,1,0:T(8,128)S(1)} %get-tuple-element.31), channel_id=1, source_target_pairs={{0,448},{64,0},{128,64},{192,128},{256,192},{320,256},{384,320},{4... | collective-permute-start | bytes 589832 | tf_op jit(solution)/shard_map/ppermute | solution.py:199
  34.0 1.9 collective-permute-start.1
  36.0 2.7 %collective-permute-start.3 = (f32[2,24,1024]{2,1,0:T(8,128)S(1)}, f32[2,24,1024]{2,1,0:T(8,128)S(1)}, u32[]{:S(2)}, u32[]{:S(2)}) collective-permute-start(f32[2,24,1024]{2,1,0:T(8,128)S(1)} %get-tuple-element.31), channel_id=1, source_target_pairs={{0,128},{64,192},{128,256},{192,320},{256,384},{320,448},{384,0},{... | collective-permute-start | bytes 589832 | tf_op jit(solution)/shard_map/ppermute | solution.py:199
  38.7 0.0 collective-permute-done.2
  38.7 3.9 %collective-permute-done.1 = f32[2,24,1024]{2,1,0:T(8,128)S(1)} collective-permute-done((f32[2,24,1024]{2,1,0:T(8,128)S(1)}, f32[2,24,1024]{2,1,0:T(8,128)S(1)}, u32[]{:S(2)}, u32[]{:S(2)}) %collective-permute-start.1) | collective-permute-done | bytes 196640 | tf_op jit(solution)/shard_map/ppermute | solution.py:199
  42.6 7.2 %collective-permute-done.3 = f32[2,24,1024]{2,1,0:T(8,128)S(1)} collective-permute-done((f32[2,24,1024]{2,1,0:T(8,128)S(1)}, f32[2,24,1024]{2,1,0:T(8,128)S(1)}, u32[]{:S(2)}, u32[]{:S(2)}) %collective-permute-start.3) | collective-permute-done | bytes 196640 | tf_op jit(solution)/shard_map/ppermute | solution.py:199
  49.8 1.1 fusion.2
  50.9 3.7 %collective-permute-start.4 = (f32[4,2,24,1024]{3,2,1,0:T(8,128)}, f32[4,2,24,1024]{3,2,1,0:T(8,128)S(1)}, u32[]{:S(2)}, u32[]{:S(2)}) collective-permute-start(f32[4,2,24,1024]{3,2,1,0:T(8,128)} %get-tuple-element.29), channel_id=1, source_target_pairs={{0,32},{32,0},{1,33},{33,1},{2,34},{34,2},{3,35},{35,3},{4,36},{36... | collective-permute-start | bytes 2359304 | tf_op jit(solution)/shard_map/ppermute | solution.py:206
  54.7 2.0 %collective-permute-done.4 = f32[4,2,24,1024]{3,2,1,0:T(8,128)S(1)} collective-permute-done((f32[4,2,24,1024]{3,2,1,0:T(8,128)}, f32[4,2,24,1024]{3,2,1,0:T(8,128)S(1)}, u32[]{:S(2)}, u32[]{:S(2)}) %collective-permute-start.4) | collective-permute-done | bytes 786464 | tf_op jit(solution)/shard_map/ppermute | solution.py:206
  56.7 0.2 fusion
  56.9 0.2 fusion.3
  57.0 0.2 broadcast_in_dim.10
  57.5 0.0 all-to-all-done
  57.5 8.7 %shard_map.41 = (f32[1024,1024]{1,0:T(8,128)S(1)}, f32[32,8,128]{2,1,0:T(8,128)S(1)}) custom-call(f32[1024,384]{1,0:T(8,128)S(1)} %bitcast.29, f32[384,1024]{1,0:T(8,128)S(1)} %bitcast.27), custom_call_target="tpu_custom_call" | custom-call | tf_op jit(solution)/shard_map/pallas_call | solution.py:182
  66.1 17.2 %all_to_all.45.in_ref = f32[32,8,128]{2,1,0:T(8,128)S(1)} all-to-all(f32[32,8,128]{2,1,0:T(8,128)S(1)} %get-tuple-element.11), channel_id=1, replica_groups=mesh['y'=8,'core'=2,'x'=4,'z'=8] {'x','z'}, dimensions={0} | all-to-all | bytes 262144 | tf_op jit(solution)/shard_map/all_to_all | solution.py:231
  83.3 1.3 shard_map.42
  84.7 14.6 %all_to_all.46.in_ref = f32[16,8,128]{2,1,0:T(8,128)S(1)} all-to-all(f32[16,8,128]{2,1,0:T(8,128)S(1)} %get-tuple-element.13), channel_id=1, replica_groups=mesh['y'=8,'core'=2,'x'=4,'z'=8] {'y','core'}, dimensions={0} | all-to-all | bytes 131072 | tf_op jit(solution)/shard_map/all_to_all | solution.py:231
  99.3 1.0 shard_map.43
  100.3 12.4 %all_to_all.47.in_ref = f32[32,8,128]{2,1,0:T(8,128)S(1)} all-to-all(f32[32,8,128]{2,1,0:T(8,128)S(1)} %get-tuple-element.15), channel_id=1, replica_groups=mesh['y'=8,'core'=2,'x'=4,'z'=8] {'x','z'}, dimensions={0} | all-to-all | bytes 262144 | tf_op jit(solution)/shard_map/all_to_all | solution.py:231
  112.7 0.5 shard_map.44
  113.2 12.3 %all_to_all.48.in_ref = f32[16,8,128]{2,1,0:T(8,128)S(1)} all-to-all(f32[16,8,128]{2,1,0:T(8,128)S(1)} %shard_map.44), channel_id=1, replica_groups=mesh['y'=8,'core'=2,'x'=4,'z'=8] {'y','core'}, dimensions={0} | all-to-all | bytes 131072 | tf_op jit(solution)/shard_map/all_to_all | solution.py:231
  125.5 0.4 shard_map.45
  125.9 12.4 %all_to_all.49.in_ref = f32[32,8,128]{2,1,0:T(8,128)S(1)} all-to-all(f32[32,8,128]{2,1,0:T(8,128)S(1)} %shard_map.45), channel_id=1, replica_groups=mesh['y'=8,'core'=2,'x'=4,'z'=8] {'x','z'}, dimensions={0} | all-to-all | bytes 262144 | tf_op jit(solution)/shard_map/all_to_all | solution.py:231
  138.3 0.5 shard_map.46
  138.8 12.3 %all_to_all.50.in_ref = f32[16,8,128]{2,1,0:T(8,128)S(1)} all-to-all(f32[16,8,128]{2,1,0:T(8,128)S(1)} %shard_map.46), channel_id=1, replica_groups=mesh['y'=8,'core'=2,'x'=4,'z'=8] {'y','core'}, dimensions={0} | all-to-all | bytes 131072 | tf_op jit(solution)/shard_map/all_to_all | solution.py:231
  151.1 4.5 %shard_map.47 = (f32[8,128]{1,0:T(8,128)}, f32[32,104,128]{2,1,0:T(8,128)S(1)}) custom-call(f32[16,8,128]{2,1,0:T(8,128)S(1)} %all_to_all.50.in_ref, f32[8,128]{1,0:T(8,128)S(1)} %get-tuple-element.17.lse_ref, f32[1024,1024]{1,0:T(8,128)S(1)} %get-tuple-element.16.plan_ref, f32[384,1024]{1,0:T(8,128)S(1)} %bitcast.28), custom_call_target="tpu_custom_call" | custom-call | tf_op jit(solution)/shard_map/pallas_call | solution.py:182
  155.6 24.4 %all_to_all.51 = f32[4,832,128]{2,1,0:T(8,128)S(1)} all-to-all(f32[4,832,128]{2,1,0:T(8,128)S(1)} %bitcast.30), channel_id=1, replica_groups=mesh['y'=8,'core'=2,'x'=4,'z'=8] {'x'}, dimensions={0} | all-to-all | bytes 3407872 | tf_op jit(solution)/shard_map/all_to_all | solution.py:231
  180.1 0.0 copy-start
  180.1 0.1 reduce_sum.9
  180.2 16.3 %all_to_all.52.in_ref = f32[8,104,128]{2,1,0:T(8,128)S(1)} all-to-all(f32[8,104,128]{2,1,0:T(8,128)S(1)} %bitcast.31), channel_id=1, replica_groups=mesh['y'=8,'core'=2,'x'=4,'z'=8] {'z'}, dimensions={0} | all-to-all | bytes 851968 | tf_op jit(solution)/shard_map/all_to_all | solution.py:231
  196.5 0.0 copy-done
  196.5 0.7 shard_map.48
  (9 shorter events, 0.2 us)
Async XLA Ops:
  2.8 13.8 %copy-start.1 = (f32[1024,24]{0,1:T(8,128)S(1)}, f32[1024,24]{0,1:T(8,128)}, u32[]{:S(2)}) copy-start(f32[1024,24]{0,1:T(8,128)} %param.3) | copy-start | bytes 294916
  2.8 54.7 %all-to-all-start = ((f32[32,32,384]{2,1,0:T(8,128)}), f32[32,32,384]{2,1,0:T(8,128)S(1)}, u32[]{:S(2)}, u32[]{:S(2)}) async-start(f32[32,32,384]{2,1,0:T(8,128)} %broadcast_in_dim.4), calls=%async_computation | async-start | bytes 3145728 | tf_op jit(solution)/shard_map/all_to_all | solution.py:25
  16.6 9.6 %collective-permute-start = (f32[24,1024]{1,0:T(8,128)S(1)}, f32[24,1024]{1,0:T(8,128)S(1)}, u32[]{:S(2)}, u32[]{:S(2)}) collective-permute-start(f32[24,1024]{1,0:T(8,128)S(1)} %bitcast.44), channel_id=1, source_target_pairs={{0,256},{64,320},{128,384},{192,448},{256,0},{320,64},{384,128},{4... | collective-permute-start | bytes 294920 | tf_op jit(solution)/shard_map/ppermute | solution.py:199
  26.2 12.5 %collective-permute-start.2 = (f32[2,24,1024]{2,1,0:T(8,128)S(1)}, f32[2,24,1024]{2,1,0:T(8,128)S(1)}, u32[]{:S(2)}, u32[]{:S(2)}) collective-permute-start(f32[2,24,1024]{2,1,0:T(8,128)S(1)} %get-tuple-element.31), channel_id=1, source_target_pairs={{0,448},{64,0},{128,64},{192,128},{256,192},{320,256},{384,320},{4... | collective-permute-start | bytes 589832 | tf_op jit(solution)/shard_map/ppermute | solution.py:199
  34.0 8.5 %collective-permute-start.1 = (f32[2,24,1024]{2,1,0:T(8,128)S(1)}, f32[2,24,1024]{2,1,0:T(8,128)S(1)}, u32[]{:S(2)}, u32[]{:S(2)}) collective-permute-start(f32[2,24,1024]{2,1,0:T(8,128)S(1)} %get-tuple-element.31), channel_id=1, source_target_pairs={{0,64},{64,128},{128,192},{192,256},{256,320},{320,384},{384,448},... | collective-permute-start | bytes 589832 | tf_op jit(solution)/shard_map/ppermute | solution.py:199
  36.0 13.8 %collective-permute-start.3 = (f32[2,24,1024]{2,1,0:T(8,128)S(1)}, f32[2,24,1024]{2,1,0:T(8,128)S(1)}, u32[]{:S(2)}, u32[]{:S(2)}) collective-permute-start(f32[2,24,1024]{2,1,0:T(8,128)S(1)} %get-tuple-element.31), channel_id=1, source_target_pairs={{0,128},{64,192},{128,256},{192,320},{256,384},{320,448},{384,0},{... | collective-permute-start | bytes 589832 | tf_op jit(solution)/shard_map/ppermute | solution.py:199
  50.9 5.8 %collective-permute-start.4 = (f32[4,2,24,1024]{3,2,1,0:T(8,128)}, f32[4,2,24,1024]{3,2,1,0:T(8,128)S(1)}, u32[]{:S(2)}, u32[]{:S(2)}) collective-permute-start(f32[4,2,24,1024]{3,2,1,0:T(8,128)} %get-tuple-element.29), channel_id=1, source_target_pairs={{0,32},{32,0},{1,33},{33,1},{2,34},{34,2},{3,35},{35,3},{4,36},{36... | collective-permute-start | bytes 2359304 | tf_op jit(solution)/shard_map/ppermute | solution.py:206
  180.1 16.4 %copy-start = (f32[32,384]{1,0:T(8,128)S(1)}, f32[32,384]{1,0:T(8,128)}, u32[]{:S(2)}) copy-start(f32[32,384]{1,0:T(8,128)} %noise_ref.1) | copy-start | bytes 147460

commit v4 on v3

--- a/solution.py
+++ b/solution.py
@@ -16,13 +16,9 @@
 BLOCK = 256
 X_CHIPS = 4
 INTERPRET = False
-SRC, TGT = ("y", "core"), ("x", "z")
+SRC, TGT = ("yh", "yb", "core"), ("x", "zh", "zb")
+ROW, COL = ("yb", "core", "x", "zb"), ("yh", "zh")
 F32 = jnp.float32
-
-
-def spread(value, axis):
-    count = lax.axis_size(axis)
-    return lax.all_to_all(jnp.broadcast_to(value[None], (count,) + value.shape), axis, 0, 0)
 
 
 def diagonal():
@@ -52,7 +48,12 @@
     out_ref[...] = jnp.broadcast_to(tiles[None], out_ref.shape)
 
 
-def cost_kernel(noise_ref, data_ref, gain_ref, out_ref, rows_ref):
+def cost_kernel(noise_ref, pieces_ref, gain_ref, data_ref, out_ref, rows_ref):
+    pieces, deep, wide = pieces_ref.shape
+    across_pieces = data_ref.shape[1] // wide
+    for p in range(pieces):
+        s, h = divmod(p, across_pieces)
+        data_ref[s * deep : (s + 1) * deep, h * wide : (h + 1) * wide] = pieces_ref[p]
     data = data_ref[...]
     scale = 1.0 / (data.shape[0] * EPS)
     data_sq = jnp.sum(data * data, axis=0, keepdims=True)
@@ -190,71 +191,74 @@
     )(*args)
 
 
+def swap(value, axis):
+    return lax.all_to_all(value, axis, 0, 0)
+
+
+def joined(value, axis, spot):
+    other = lax.ppermute(value, axis, [(0, 1), (1, 0)])
+    first = lax.axis_index(axis) == 0
+    return jnp.stack([jnp.where(first, value, other), jnp.where(first, other, value)], spot)
+
+
 def gathered(noise, data):
-    count = lax.axis_size("y")
-    at, core = lax.axis_index("y"), lax.axis_index("core")
-    rows = spread(noise, TGT).reshape(-1, noise.shape[1])
-
-    def shifted(value, hop):
-        return lax.ppermute(value, "y", [(i, (i + hop) % count) for i in range(count)])
-
-    own = data.T
-    far = shifted(own, count // 2)
-    both = jnp.stack([own, far])
-    hops = [0] + [h for k in range(1, count // 4 + 1) for h in (k, -k)][: count // 2 - 1]
-    mine = jnp.stack([both] + [shifted(both, h) for h in hops[1:]])
-    theirs = lax.ppermute(mine, "core", [(0, 1), (1, 0)])
-    pair = jnp.where(core == 0, jnp.stack([mine, theirs]), jnp.stack([theirs, mine]))
-    pair = jnp.moveaxis(pair, 0, 2)
-    feats, width = own.shape
-    held = jnp.zeros((count, 2 * feats, width), F32)
-    for k, hop in enumerate(hops):
-        for h in range(2):
-            place = (at - hop - h * (count // 2) + 2 * count) % count
-            held = lax.dynamic_update_slice_in_dim(
-                held, pair[k, h].reshape(1, 2 * feats, width), place, 0)
-    return rows, held.reshape(-1, width)
+    n_yh, n_zh, n_x = lax.axis_size("yh"), lax.axis_size("zh"), lax.axis_size("x")
+    at = lax.axis_index("x")
+    quarters = jnp.swapaxes(data.T.reshape(data.shape[1], 4, -1), 0, 1)
+    shape = (n_yh, 4, n_zh, *quarters.shape[1:])
+    pieces = jnp.broadcast_to(quarters[None, :, None], shape)
+    pieces = swap(pieces.reshape(-1, *shape[3:]), ("yh", "yb", "core", "zh"))
+    hops = [h for k in range(1, n_x // 2 + 1) for h in (k, -k)][: n_x - 1]
+    rows = jnp.zeros((n_x, *noise.shape), F32)
+    rows = lax.dynamic_update_slice_in_dim(rows, noise[None], at, 0)
+    for hop in hops:
+        piece = lax.ppermute(noise, "x", [(i, (i + hop) % n_x) for i in range(n_x)])
+        rows = lax.dynamic_update_slice_in_dim(
+            rows, piece[None], (at - hop + n_x) % n_x, 0)
+    rows = joined(joined(joined(rows, "yb", 0), "zb", 2), "core", 1)
+    return rows.reshape(-1, noise.shape[1]), pieces
 
 
 def per_device(noise, data):
     own_rows, feats = noise.shape
-    rows, columns = gathered(noise, data)
-    n_rows, n_cols = rows.shape[0], columns.shape[1]
-    n_src, n_tgt, n_x, n_z = (lax.axis_size(a) for a in (SRC, TGT, "x", "z"))
-    src_total, tgt_total = n_rows * n_src, n_cols * n_tgt
+    rows, pieces = gathered(noise, data)
+    n_row, n_col = lax.axis_size(ROW), lax.axis_size(COL)
+    n_rows, n_cols = rows.shape[0], pieces.shape[2] * lax.axis_size("zh")
+    src_total, tgt_total = n_rows * n_col, n_cols * n_row
     r_tiles, c_tiles = (n_rows // LANES, LANES), (n_cols // LANES, LANES)
-    to_tgt, to_src = (n_tgt, *r_tiles), (n_src, *c_tiles)
+    to_row, to_col = (n_row, *r_tiles), (n_col, *c_tiles)
     row_scratch = [pltpu.VMEM(r_tiles, F32)]
     square = (n_rows, n_cols)
 
-    def swap(value, axis):
-        return lax.all_to_all(value, axis, 0, 0)
-
-    gain, message = call(cost_kernel, [square, to_tgt], rows, columns, scratch=row_scratch)
+    gain, columns, message = call(cost_kernel, [square, (feats, n_cols), to_row], rows, pieces,
+                                  scratch=row_scratch)
     f_pot, message = call(functools.partial(first_column_kernel, math.log(src_total)),
-                          [r_tiles, to_src], swap(message, TGT), gain)
-    lse, plan, message = call(plan_kernel, [c_tiles, square, to_tgt], swap(message, SRC), f_pot,
+                          [r_tiles, to_col], swap(message, ROW), gain)
+    lse, plan, message = call(plan_kernel, [c_tiles, square, to_row], swap(message, COL), f_pot,
                               gain, scratch=row_scratch)
     for step_index in range(1, ITERS):
         if step_index > 1:
-            (message,) = call(functools.partial(row_kernel, float(tgt_total)), [to_tgt],
-                              swap(message, SRC), plan, scratch=row_scratch)
-        (message,) = call(functools.partial(column_kernel, float(src_total)), [to_src],
-                          swap(message, TGT), plan)
+            (message,) = call(functools.partial(row_kernel, float(tgt_total)), [to_row],
+                              swap(message, COL), plan, scratch=row_scratch)
+        (message,) = call(functools.partial(column_kernel, float(src_total)), [to_col],
+                          swap(message, ROW), plan)
     tall = own_rows // 8 * (feats // LANES) * 8 + 8
     g_pot, part = call(
         functools.partial(final_kernel, float(tgt_total), own_rows),
-        [c_tiles, (n_tgt, tall, LANES)], swap(message, SRC), lse, plan, columns,
+        [c_tiles, (n_row, tall, LANES)], swap(message, COL), lse, plan, columns,
         scratch=[pltpu.VMEM((feats + LANES, n_cols), jnp.bfloat16)] * 2)
-    part = jnp.sum(swap(part.reshape(n_x, n_z * tall, LANES), "x"), axis=0)
-    part = swap(part.reshape(n_z, tall, LANES), "z")
+    part = swap(part, ROW)
+    own = lax.dynamic_index_in_dim(
+        g_pot.reshape(lax.axis_size("zh"), -1), lax.axis_index("zh"), 0, False)
+    potential = joined(joined(own, "core", 0), "yb", 0).reshape(-1)
     (velocity,) = call(last_kernel, [noise.shape], part, noise)
-    return velocity, g_pot.reshape(-1)
+    return velocity, potential
 
 
 def solution(mesh):
     src, tgt = mesh.shape["src"], mesh.shape["tgt"]
-    split = Mesh(mesh.devices.reshape(src // 2, 2, X_CHIPS, tgt // X_CHIPS), SRC + TGT)
+    split = Mesh(
+        mesh.devices.reshape(src // 4, 2, 2, X_CHIPS, tgt // X_CHIPS // 2, 2), SRC + TGT)
     return jax.shard_map(
         per_device,
         mesh=split,

time: 198 us -> 225 us (1.14)
  waiting for transfers between devices: 15.2 us -> 64.6 us
  blocking collectives: 122 us -> 84.8 us
  starting transfers between devices: 37.5 us -> 49.4 us
    ppermute x5 -> x8, waiting for transfers between devices: 15.2 us -> 62.1 us  [the longest x5 62.1 us: joined(): other = lax.ppermute(value, axis, [(0, 1), (1, 0)])]
    all_to_all x8 -> x6, blocking collectives: 122 us -> 84.8 us  [swap(): return lax.all_to_all(value, axis, 0, 0)]
    all_to_all x1 -> x2, starting transfers between devices: 13.8 us -> 23 us  [swap(): return lax.all_to_all(value, axis, 0, 0)]
    ppermute x5 -> x8, starting transfers between devices: 23.6 us -> 26.4 us  [the longest x5 15.7 us: joined(): other = lax.ppermute(value, axis, [(0, 1), (1, 0)])]
    all_to_all x1 -> x2, waiting for transfers between devices: 0.01 us -> 2.5 us  [swap(): return lax.all_to_all(value, axis, 0, 0)]
  transfers between devices with their start and end apart: 6 -> 10, of which waited for: 4 -> 6; matrix products, arithmetic and copies ran while one was open for 1% -> 3% of each run, Pallas kernels for 0% -> 0%
where the time goes in v4:
time: 225 us; the launch traced here: 224 us
  blocking collectives  84.8 us (38%)
  waiting for transfers between devices  64.6 us (29%)
  starting transfers between devices  49.4 us (22%)
  Pallas kernels  18.9 us (8%)
  local copies, waits for them, and re-layouts  2.94 us (1%)
  other arithmetic  2.69 us (1%)
    all_to_all x6, blocking collectives, swap(): return lax.all_to_all(value, axis, 0, 0)  84.8 us
    ppermute x5, waiting for transfers between devices, joined(): other = lax.ppermute(value, axis, [(0, 1), (1, 0)])  62.1 us
    all_to_all x2, starting transfers between devices, swap(): return lax.all_to_all(value, axis, 0, 0)  23 us
    pallas_call x8, Pallas kernels, call(): pl.pallas_call(kernel, out_shape=[jax.ShapeDtypeStruct(shape, F32) for sh...  18.9 us
    ppermute x5, starting transfers between devices, joined(): other = lax.ppermute(value, axis, [(0, 1), (1, 0)])  15.7 us
    ppermute x3, starting transfers between devices, gathered(): piece = lax.ppermute(noise, 'x', [(i, (i + hop) % n_x) for i in range(n_x)])  10.8 us
  transfers between devices with their start and end apart: 10, of which 6 were waited for; matrix products, arithmetic and copies ran while one was open for 3% of the time, Pallas kernels for 0%

profile of v4, /device:TPU:1, one launch (start us, length us, event | category | flops | bytes accessed | tf_op | source)
XLA Modules:
  0.0 224.4 jit_solution(8396762549429140936)
XLA Ops:
  0.6 5.2 %collective-permute-start.1 = (f32[32,384]{1,0:T(8,128)}, f32[32,384]{1,0:T(8,128)S(1)}, u32[]{:S(2)}, u32[]{:S(2)}) collective-permute-start(f32[32,384]{1,0:T(8,128)} %noise_ref.1), channel_id=1, source_target_pairs={{0,24},{8,0},{16,8},{24,16},{1,25},{9,1},{17,9},{25,17},{2,26},{10... | collective-permute-start | bytes 147464 | tf_op jit(solution)/shard_map/ppermute | solution.py:215
  5.8 1.9 collective-permute-start
  7.8 3.6 %collective-permute-start.2 = (f32[32,384]{1,0:T(8,128)}, f32[32,384]{1,0:T(8,128)S(1)}, u32[]{:S(2)}, u32[]{:S(2)}) collective-permute-start(f32[32,384]{1,0:T(8,128)} %noise_ref.1), channel_id=1, source_target_pairs={{0,16},{8,24},{16,0},{24,8},{1,17},{9,25},{17,1},{25,9},{2,18},{10... | collective-permute-start | bytes 147464 | tf_op jit(solution)/shard_map/ppermute | solution.py:215
  11.4 0.9 reshape.21
  12.4 1.3 broadcast_in_dim.26
  13.7 0.0 copy-start
  13.7 17.8 %all-to-all-start = ((f32[64,24,256]{2,1,0:T(8,128)}), f32[64,24,256]{2,1,0:T(8,128)S(1)}, u32[]{:S(2)}, u32[]{:S(2)}) async-start(f32[64,24,256]{2,1,0:T(8,128)} %bitcast.15), calls=%async_computation | async-start | bytes 3145728 | tf_op jit(solution)/shard_map/all_to_all | solution.py:195
  31.5 0.0 copy-done
  31.6 0.0 collective-permute-done
  31.6 0.0 collective-permute-done.1
  31.6 0.0 collective-permute-done.2
  31.7 3.3 %collective-permute-start.3 = (f32[4,32,384]{2,1,0:T(8,128)S(1)}, f32[4,32,384]{2,1,0:T(8,128)S(1)}, u32[]{:S(2)}, u32[]{:S(2)}) collective-permute-start(f32[4,32,384]{2,1,0:T(8,128)S(1)} %bitcast_dynamic-update-slice_fusion), channel_id=1, source_target_pairs={{0,64},{64,0},{1,65},{65,1},{2,66},{66,2},{3,67},{67,3},{4,68},{68... | collective-permute-start | bytes 589832 | tf_op jit(solution)/shard_map/ppermute | solution.py:199
  34.9 36.3 %collective-permute-done.3 = f32[4,32,384]{2,1,0:T(8,128)S(1)} collective-permute-done((f32[4,32,384]{2,1,0:T(8,128)S(1)}, f32[4,32,384]{2,1,0:T(8,128)S(1)}, u32[]{:S(2)}, u32[]{:S(2)}) %collective-permute-start.3) | collective-permute-done | bytes 196640 | tf_op jit(solution)/shard_map/ppermute | solution.py:199
  71.3 3.1 %collective-permute-start.4 = (f32[2,4,32,384]{3,2,1,0:T(8,128)S(1)}, f32[2,4,32,384]{3,2,1,0:T(8,128)}, u32[]{:S(2)}, u32[]{:S(2)}) collective-permute-start(f32[2,4,32,384]{3,2,1,0:T(8,128)S(1)} %pad_maximum_fusion.2), channel_id=1, source_target_pairs={{0,1},{1,0},{2,3},{3,2},{4,5},{5,4},{6,7},{7,6},{8,9},{9,8},{10,11... | collective-permute-start | bytes 1179656 | tf_op jit(solution)/shard_map/ppermute | solution.py:199
  74.4 8.6 %collective-permute-done.4 = f32[2,4,32,384]{3,2,1,0:T(8,128)} collective-permute-done((f32[2,4,32,384]{3,2,1,0:T(8,128)S(1)}, f32[2,4,32,384]{3,2,1,0:T(8,128)}, u32[]{:S(2)}, u32[]{:S(2)}) %collective-permute-start.4) | collective-permute-done | bytes 393248 | tf_op jit(solution)/shard_map/ppermute | solution.py:199
  83.0 1.1 select_bitcast_fusion.3
  84.1 0.1 pad_maximum_fusion.1
  84.2 3.7 %collective-permute-start.5 = (f32[2,4,2,32,384]{4,3,2,1,0:T(8,128)S(1)}, f32[2,4,2,32,384]{4,3,2,1,0:T(8,128)}, u32[]{:S(2)}, u32[]{:S(2)}) collective-permute-start(f32[2,4,2,32,384]{4,3,2,1,0:T(8,128)S(1)} %pad_maximum_fusion.1), channel_id=1, source_target_pairs={{0,32},{32,0},{1,33},{33,1},{2,34},{34,2},{3,35},{35,3},{4,36},{36... | collective-permute-start | bytes 2359304 | tf_op jit(solution)/shard_map/ppermute | solution.py:199
  87.9 2.0 collective-permute-done.5
  89.9 1.3 select_bitcast_fusion.1
  91.3 0.1 pad_maximum_fusion
  91.4 0.0 all-to-all-done.pieces_ref
  91.4 8.8 %shard_map.41 = (f32[1024,1024]{1,0:T(8,128)S(1)}, f32[384,1024]{1,0:T(8,128)S(1)}, f32[32,8,128]{2,1,0:T(8,128)S(1)}) custom-call(f32[1024,384]{1,0:T(8,128)S(1)} %bitcast.38, f32[64,24,256]{2,1,0:T(8,128)S(1)} %all-to-all-done.pieces_ref), custom_call_target="tpu_custom_call" | custom-call | tf_op jit(solution)/shard_map/pallas_call | solution.py:183
  100.2 11.2 %all_to_all.40.in_ref = f32[32,8,128]{2,1,0:T(8,128)S(1)} all-to-all(f32[32,8,128]{2,1,0:T(8,128)S(1)} %get-tuple-element.12), channel_id=1, replica_groups=mesh['yh'=4,'yb'=2,'core'=2,'x'=4,'zh'=4,'zb'=2] {'yb','core','x','zb'}, dimensions={0} | all-to-all | bytes 262144 | tf_op jit(solution)/shard_map/all_to_all | solution.py:195
  111.4 1.3 shard_map.42
  112.7 22.8 %all_to_all.41.in_ref = f32[16,8,128]{2,1,0:T(8,128)S(1)} all-to-all(f32[16,8,128]{2,1,0:T(8,128)S(1)} %get-tuple-element.14), channel_id=1, replica_groups=mesh['yh'=4,'yb'=2,'core'=2,'x'=4,'zh'=4,'zb'=2] {'yh','zh'}, dimensions={0} | all-to-all | bytes 131072 | tf_op jit(solution)/shard_map/all_to_all | solution.py:195
  135.5 1.0 shard_map.43
  136.5 11.7 %all_to_all.42.in_ref = f32[32,8,128]{2,1,0:T(8,128)S(1)} all-to-all(f32[32,8,128]{2,1,0:T(8,128)S(1)} %get-tuple-element.16), channel_id=1, replica_groups=mesh['yh'=4,'yb'=2,'core'=2,'x'=4,'zh'=4,'zb'=2] {'yb','core','x','zb'}, dimensions={0} | all-to-all | bytes 262144 | tf_op jit(solution)/shard_map/all_to_all | solution.py:195
  148.2 0.5 shard_map.44
  148.7 13.9 %all_to_all.43.in_ref = f32[16,8,128]{2,1,0:T(8,128)S(1)} all-to-all(f32[16,8,128]{2,1,0:T(8,128)S(1)} %shard_map.44), channel_id=1, replica_groups=mesh['yh'=4,'yb'=2,'core'=2,'x'=4,'zh'=4,'zb'=2] {'yh','zh'}, dimensions={0} | all-to-all | bytes 131072 | tf_op jit(solution)/shard_map/all_to_all | solution.py:195
  162.6 0.4 shard_map.45
  163.0 11.4 %all_to_all.44.in_ref = f32[32,8,128]{2,1,0:T(8,128)S(1)} all-to-all(f32[32,8,128]{2,1,0:T(8,128)S(1)} %shard_map.45), channel_id=1, replica_groups=mesh['yh'=4,'yb'=2,'core'=2,'x'=4,'zh'=4,'zb'=2] {'yb','core','x','zb'}, dimensions={0} | all-to-all | bytes 262144 | tf_op jit(solution)/shard_map/all_to_all | solution.py:195
  174.4 0.5 shard_map.46
  174.8 13.9 %all_to_all.45.in_ref = f32[16,8,128]{2,1,0:T(8,128)S(1)} all-to-all(f32[16,8,128]{2,1,0:T(8,128)S(1)} %shard_map.46), channel_id=1, replica_groups=mesh['yh'=4,'yb'=2,'core'=2,'x'=4,'zh'=4,'zb'=2] {'yh','zh'}, dimensions={0} | all-to-all | bytes 131072 | tf_op jit(solution)/shard_map/all_to_all | solution.py:195
  188.8 5.7 %shard_map.47 = (f32[8,128]{1,0:T(8,128)S(1)}, f32[32,104,128]{2,1,0:T(8,128)}) custom-call(f32[16,8,128]{2,1,0:T(8,128)S(1)} %all_to_all.45.in_ref, f32[8,128]{1,0:T(8,128)S(1)} %get-tuple-element.18.lse_ref, f32[1024,1024]{1,0:T(8,128)S(1)} %get-tuple-element.17.plan_ref, f32[384,1024]{1,0:T(8,128)S(1)} %get-tuple-element.19.data_ref), custom_call_target="tpu_custom_call" | custom-call | tf_op jit(solution)/shard_map/pallas_call | solution.py:183
  194.5 5.2 %all-to-all-start.7 = ((f32[32,104,128]{2,1,0:T(8,128)}), f32[32,104,128]{2,1,0:T(8,128)S(1)}, u32[]{:S(2)}, u32[]{:S(2)}) async-start(f32[32,104,128]{2,1,0:T(8,128)} %get-tuple-element.20), calls=%async_computation.7 | async-start | bytes 3407872 | tf_op jit(solution)/shard_map/all_to_all | solution.py:195
  199.8 2.2 collective-permute-start.6
  202.0 0.8 collective-permute-done.6
  202.8 3.4 %collective-permute-start.7 = (f32[2,256]{1,0:T(2,128)S(1)}, f32[2,256]{1,0:T(2,128)S(1)}, u32[]{:S(2)}, u32[]{:S(2)}) collective-permute-start(f32[2,256]{1,0:T(2,128)S(1)} %pad_maximum_fusion.3), channel_id=1, source_target_pairs={{0,64},{64,0},{1,65},{65,1},{2,66},{66,2},{3,67},{67,3},{4,68},{68... | collective-permute-start | bytes 6152 | tf_op jit(solution)/shard_map/ppermute | solution.py:199
  206.2 14.4 %collective-permute-done.7 = f32[2,256]{1,0:T(2,128)S(1)} collective-permute-done((f32[2,256]{1,0:T(2,128)S(1)}, f32[2,256]{1,0:T(2,128)S(1)}, u32[]{:S(2)}, u32[]{:S(2)}) %collective-permute-start.7) | collective-permute-done | bytes 2080 | tf_op jit(solution)/shard_map/ppermute | solution.py:199
  220.6 0.6 copy.7
  221.2 2.5 %all-to-all-done.7.in_ref = f32[32,104,128]{2,1,0:T(8,128)S(1)} async-done(((f32[32,104,128]{2,1,0:T(8,128)}), f32[32,104,128]{2,1,0:T(8,128)S(1)}, u32[]{:S(2)}, u32[]{:S(2)}) %all-to-all-start.7) | async-done | bytes 1703968 | tf_op jit(solution)/shard_map/all_to_all | solution.py:195
  223.7 0.7 shard_map.48
  (14 shorter events, 0.2 us)
Async XLA Ops:
  0.6 31.0 %collective-permute-start.1 = (f32[32,384]{1,0:T(8,128)}, f32[32,384]{1,0:T(8,128)S(1)}, u32[]{:S(2)}, u32[]{:S(2)}) collective-permute-start(f32[32,384]{1,0:T(8,128)} %noise_ref.1), channel_id=1, source_target_pairs={{0,24},{8,0},{16,8},{24,16},{1,25},{9,1},{17,9},{25,17},{2,26},{10... | collective-permute-start | bytes 147464 | tf_op jit(solution)/shard_map/ppermute | solution.py:215
  5.8 25.7 %collective-permute-start = (f32[32,384]{1,0:T(8,128)}, f32[32,384]{1,0:T(8,128)S(1)}, u32[]{:S(2)}, u32[]{:S(2)}) collective-permute-start(f32[32,384]{1,0:T(8,128)} %noise_ref.1), channel_id=1, source_target_pairs={{0,8},{8,16},{16,24},{24,0},{1,9},{9,17},{17,25},{25,1},{2,10},{10... | collective-permute-start | bytes 147464 | tf_op jit(solution)/shard_map/ppermute | solution.py:215
  7.8 23.9 %collective-permute-start.2 = (f32[32,384]{1,0:T(8,128)}, f32[32,384]{1,0:T(8,128)S(1)}, u32[]{:S(2)}, u32[]{:S(2)}) collective-permute-start(f32[32,384]{1,0:T(8,128)} %noise_ref.1), channel_id=1, source_target_pairs={{0,16},{8,24},{16,0},{24,8},{1,17},{9,25},{17,1},{25,9},{2,18},{10... | collective-permute-start | bytes 147464 | tf_op jit(solution)/shard_map/ppermute | solution.py:215
  13.7 17.8 %copy-start = (f32[32,384]{1,0:T(8,128)S(1)}, f32[32,384]{1,0:T(8,128)}, u32[]{:S(2)}) copy-start(f32[32,384]{1,0:T(8,128)} %noise_ref.1) | copy-start | bytes 147460
  13.7 77.7 %all-to-all-start = ((f32[64,24,256]{2,1,0:T(8,128)}), f32[64,24,256]{2,1,0:T(8,128)S(1)}, u32[]{:S(2)}, u32[]{:S(2)}) async-start(f32[64,24,256]{2,1,0:T(8,128)} %bitcast.15), calls=%async_computation | async-start | bytes 3145728 | tf_op jit(solution)/shard_map/all_to_all | solution.py:195
  31.7 39.6 %collective-permute-start.3 = (f32[4,32,384]{2,1,0:T(8,128)S(1)}, f32[4,32,384]{2,1,0:T(8,128)S(1)}, u32[]{:S(2)}, u32[]{:S(2)}) collective-permute-start(f32[4,32,384]{2,1,0:T(8,128)S(1)} %bitcast_dynamic-update-slice_fusion), channel_id=1, source_target_pairs={{0,64},{64,0},{1,65},{65,1},{2,66},{66,2},{3,67},{67,3},{4,68},{68... | collective-permute-start | bytes 589832 | tf_op jit(solution)/shard_map/ppermute | solution.py:199
  71.3 11.7 %collective-permute-start.4 = (f32[2,4,32,384]{3,2,1,0:T(8,128)S(1)}, f32[2,4,32,384]{3,2,1,0:T(8,128)}, u32[]{:S(2)}, u32[]{:S(2)}) collective-permute-start(f32[2,4,32,384]{3,2,1,0:T(8,128)S(1)} %pad_maximum_fusion.2), channel_id=1, source_target_pairs={{0,1},{1,0},{2,3},{3,2},{4,5},{5,4},{6,7},{7,6},{8,9},{9,8},{10,11... | collective-permute-start | bytes 1179656 | tf_op jit(solution)/shard_map/ppermute | solution.py:199
  84.2 5.8 %collective-permute-start.5 = (f32[2,4,2,32,384]{4,3,2,1,0:T(8,128)S(1)}, f32[2,4,2,32,384]{4,3,2,1,0:T(8,128)}, u32[]{:S(2)}, u32[]{:S(2)}) collective-permute-start(f32[2,4,2,32,384]{4,3,2,1,0:T(8,128)S(1)} %pad_maximum_fusion.1), channel_id=1, source_target_pairs={{0,32},{32,0},{1,33},{33,1},{2,34},{34,2},{3,35},{35,3},{4,36},{36... | collective-permute-start | bytes 2359304 | tf_op jit(solution)/shard_map/ppermute | solution.py:199
  194.5 29.2 %all-to-all-start.7 = ((f32[32,104,128]{2,1,0:T(8,128)}), f32[32,104,128]{2,1,0:T(8,128)S(1)}, u32[]{:S(2)}, u32[]{:S(2)}) async-start(f32[32,104,128]{2,1,0:T(8,128)} %get-tuple-element.20), calls=%async_computation.7 | async-start | bytes 3407872 | tf_op jit(solution)/shard_map/all_to_all | solution.py:195
  199.8 3.1 %collective-permute-start.6 = (f32[256]{0:T(256)S(1)}, f32[256]{0:T(256)S(1)}, u32[]{:S(2)}, u32[]{:S(2)}) collective-permute-start(f32[256]{0:T(256)S(1)} %bitcast.46), channel_id=1, source_target_pairs={{0,32},{32,0},{1,33},{33,1},{2,34},{34,2},{3,35},{35,3},{4,36},{36... | collective-permute-start | bytes 3080 | tf_op jit(solution)/shard_map/ppermute | solution.py:199
  202.8 17.7 %collective-permute-start.7 = (f32[2,256]{1,0:T(2,128)S(1)}, f32[2,256]{1,0:T(2,128)S(1)}, u32[]{:S(2)}, u32[]{:S(2)}) collective-permute-start(f32[2,256]{1,0:T(2,128)S(1)} %pad_maximum_fusion.3), channel_id=1, source_target_pairs={{0,64},{64,0},{1,65},{65,1},{2,66},{66,2},{3,67},{67,3},{4,68},{68... | collective-permute-start | bytes 6152 | tf_op jit(solution)/shard_map/ppermute | solution.py:199

commit v5 on v3

--- a/solution.py
+++ b/solution.py
@@ -52,26 +52,49 @@
     out_ref[...] = jnp.broadcast_to(tiles[None], out_ref.shape)
 
 
-def cost_kernel(noise_ref, data_ref, gain_ref, out_ref, rows_ref):
+def thirds(value):
+    high = value.astype(jnp.bfloat16)
+    rest = value - high.astype(F32)
+    middle = rest.astype(jnp.bfloat16)
+    return high, middle, (rest - middle.astype(F32)).astype(jnp.bfloat16)
+
+
+LEFT, RIGHT = (2, 0, 1, 1, 0, 0), (0, 2, 1, 0, 1, 0)
+
+
+def pile_kernel(*refs):
+    for k, ref in enumerate(refs[:-1]):
+        refs[-1][k] = ref[...]
+
+
+def cost_kernel(spot_ref, mine_ref, theirs_ref, noise_ref, gain_ref, data_ref, out_ref,
+                rows_ref, terms_ref):
+    groups, halfs, deep, _ = mine_ref.shape
+    for c, ref in enumerate((mine_ref, theirs_ref)):
+        for k in range(groups):
+            for h in range(halfs):
+                spot = pl.multiple_of(spot_ref[(c * groups + k) * halfs + h], 8)
+                data_ref[pl.ds(spot, deep), :] = ref[k, h]
     data = data_ref[...]
-    scale = 1.0 / (data.shape[0] * EPS)
+    feats = data.shape[0]
+    scale = 1.0 / (feats * EPS)
     data_sq = jnp.sum(data * data, axis=0, keepdims=True)
-
-    def block(b, carry):
-        at = pl.ds(pl.multiple_of(b * BLOCK, BLOCK), BLOCK)
+    parts = thirds(data)
+    for k, which in enumerate(RIGHT):
+        terms_ref[k * feats : (k + 1) * feats, :] = parts[which]
+    for b in range(noise_ref.shape[0] // BLOCK):
+        at = slice(b * BLOCK, (b + 1) * BLOCK)
         rows = noise_ref[at, :]
-        cross = jnp.dot(rows, data_ref[...], precision=lax.Precision.HIGHEST,
-                        preferred_element_type=F32)
+        parts = thirds(rows)
+        cross = jnp.dot(jnp.concatenate([parts[which] for which in LEFT], axis=1),
+                        terms_ref[...], preferred_element_type=F32)
         gain = (2.0 * cross - jnp.sum(rows * rows, axis=1, keepdims=True) - data_sq) * scale
         gain_ref[at, :] = gain
         top = jnp.max(gain, axis=1, keepdims=True)
         lse = top + jnp.log(jnp.sum(jnp.exp(gain - top), axis=1, keepdims=True))
         for t in range(BLOCK // LANES):
-            rows_ref[pl.ds(b * (BLOCK // LANES) + t, 1), :] = across(
-                lse[t * LANES : (t + 1) * LANES])
-        return carry
-
-    lax.fori_loop(0, noise_ref.shape[0] // BLOCK, block, 0)
+            spot = b * (BLOCK // LANES) + t
+            rows_ref[spot : spot + 1, :] = across(lse[t * LANES : (t + 1) * LANES])
     send(out_ref, rows_ref[...])
 
 
@@ -182,7 +205,8 @@
     return pl.pallas_call(
         kernel,
         out_shape=[jax.ShapeDtypeStruct(shape, F32) for shape in outs],
-        in_specs=[pl.BlockSpec(memory_space=pltpu.VMEM)] * len(args),
+        in_specs=[pl.BlockSpec(memory_space=pltpu.VMEM if a.dtype == F32 else pltpu.SMEM)
+                  for a in args],
         out_specs=[pl.BlockSpec(memory_space=pltpu.VMEM)] * len(outs),
         scratch_shapes=list(scratch),
         compiler_params=pltpu.CompilerParams(vmem_limit_bytes=limit),
@@ -193,33 +217,29 @@
 def gathered(noise, data):
     count = lax.axis_size("y")
     at, core = lax.axis_index("y"), lax.axis_index("core")
-    rows = spread(noise, TGT).reshape(-1, noise.shape[1])
 
     def shifted(value, hop):
         return lax.ppermute(value, "y", [(i, (i + hop) % count) for i in range(count)])
 
+    hops = [0] + [h for k in range(1, count // 4 + 1) for h in (k, -k)][: count // 2 - 1]
     own = data.T
     far = shifted(own, count // 2)
+    rows = spread(noise, "z").reshape(-1, noise.shape[1])
     both = jnp.stack([own, far])
-    hops = [0] + [h for k in range(1, count // 4 + 1) for h in (k, -k)][: count // 2 - 1]
-    mine = jnp.stack([both] + [shifted(both, h) for h in hops[1:]])
+    near = [shifted(both, h) for h in hops[1:]]
+    rows = spread(rows, "x").reshape(-1, noise.shape[1])
+    (mine,) = call(pile_kernel, [(count // 2, *both.shape)], both, *near, limit=8 << 20)
     theirs = lax.ppermute(mine, "core", [(0, 1), (1, 0)])
-    pair = jnp.where(core == 0, jnp.stack([mine, theirs]), jnp.stack([theirs, mine]))
-    pair = jnp.moveaxis(pair, 0, 2)
-    feats, width = own.shape
-    held = jnp.zeros((count, 2 * feats, width), F32)
-    for k, hop in enumerate(hops):
-        for h in range(2):
-            place = (at - hop - h * (count // 2) + 2 * count) % count
-            held = lax.dynamic_update_slice_in_dim(
-                held, pair[k, h].reshape(1, 2 * feats, width), place, 0)
-    return rows, held.reshape(-1, width)
+    spots = [2 * ((at - hop - h * (count // 2) + 2 * count) % count) for hop in hops
+             for h in range(2)]
+    spots = jnp.stack([s + c for c in (core, 1 - core) for s in spots])
+    return rows, mine, theirs, (spots * own.shape[0]).astype(jnp.int32)
 
 
 def per_device(noise, data):
     own_rows, feats = noise.shape
-    rows, columns = gathered(noise, data)
-    n_rows, n_cols = rows.shape[0], columns.shape[1]
+    rows, mine, theirs, spots = gathered(noise, data)
+    n_rows, n_cols = rows.shape[0], mine.shape[-1]
     n_src, n_tgt, n_x, n_z = (lax.axis_size(a) for a in (SRC, TGT, "x", "z"))
     src_total, tgt_total = n_rows * n_src, n_cols * n_tgt
     r_tiles, c_tiles = (n_rows // LANES, LANES), (n_cols // LANES, LANES)
@@ -230,7 +250,9 @@
     def swap(value, axis):
         return lax.all_to_all(value, axis, 0, 0)
 
-    gain, message = call(cost_kernel, [square, to_tgt], rows, columns, scratch=row_scratch)
+    gain, columns, message = call(
+        cost_kernel, [square, (feats, n_cols), to_tgt], spots, mine, theirs, rows,
+        scratch=row_scratch + [pltpu.VMEM((len(LEFT) * feats, n_cols), jnp.bfloat16)])
     f_pot, message = call(functools.partial(first_column_kernel, math.log(src_total)),
                           [r_tiles, to_src], swap(message, TGT), gain)
     lse, plan, message = call(plan_kernel, [c_tiles, square, to_tgt], swap(message, SRC), f_pot,

time: 198 us -> 193 us (0.975)
  starting transfers between devices: 37.5 us -> 35 us
  waiting for transfers between devices: 15.2 us -> 17.7 us
  Pallas kernels: 17.6 us -> 15.4 us
  blocking collectives: 122 us -> 120 us
    all_to_all x1 -> x2, waiting for transfers between devices: 0.01 us -> 6.82 us  [spread(): lax.all_to_all(jnp.broadcast_to(value[None], (count,) + value.shape), axi...]
    ppermute x4, waiting for transfers between devices: 13.2 us -> 9.16 us  [shifted(): lax.ppermute(value, 'y', [(i, (i + hop) % count) for i in range(count)])]
    ppermute x4, starting transfers between devices: 19.9 us -> 16.9 us  [shifted(): lax.ppermute(value, 'y', [(i, (i + hop) % count) for i in range(count)])]
    pallas_call x8 -> x9, Pallas kernels: 17.6 us -> 15.4 us  [call(): pl.pallas_call(kernel, out_shape=[jax.ShapeDtypeStruct(shape, F32) for sh...]
    all_to_all x8, blocking collectives: 122 us -> 120 us  [swap(): return lax.all_to_all(value, axis, 0, 0)]
    all_to_all x1 -> x2, starting transfers between devices: 13.8 us -> 15 us  [spread(): lax.all_to_all(jnp.broadcast_to(value[None], (count,) + value.shape), axi...]
  transfers between devices with their start and end apart: 6 -> 7, of which waited for: 4 -> 4; matrix products, arithmetic and copies ran while one was open for 1% -> 1% of each run, Pallas kernels for 0% -> 0%
where the time goes in v5:
time: 193 us; the launch traced here: 192 us
  blocking collectives  120 us (62%)
  starting transfers between devices  35 us (18%)
  waiting for transfers between devices  17.7 us (9%)
  Pallas kernels  15.4 us (8%)
  local copies, waits for them, and re-layouts  2.94 us (2%)
    all_to_all x8, blocking collectives, swap(): return lax.all_to_all(value, axis, 0, 0)  120 us
    ppermute x4, starting transfers between devices, shifted(): lax.ppermute(value, 'y', [(i, (i + hop) % count) for i in range(count)])  16.9 us
    pallas_call x9, Pallas kernels, call(): pl.pallas_call(kernel, out_shape=[jax.ShapeDtypeStruct(shape, F32) for sh...  15.4 us
    all_to_all x2, starting transfers between devices, spread(): lax.all_to_all(jnp.broadcast_to(value[None], (count,) + value.shape), axi...  15 us
    ppermute x4, waiting for transfers between devices, shifted(): lax.ppermute(value, 'y', [(i, (i + hop) % count) for i in range(count)])  9.16 us
    all_to_all x2, waiting for transfers between devices, spread(): lax.all_to_all(jnp.broadcast_to(value[None], (count,) + value.shape), axi...  6.82 us
  transfers between devices with their start and end apart: 7, of which 4 were waited for; matrix products, arithmetic and copies ran while one was open for 1% of the time, Pallas kernels for 0%

profile of v5, /device:TPU:1, one launch (start us, length us, event | category | flops | bytes accessed | tf_op | source)
XLA Modules:
  0.0 191.8 jit_solution(12567594913698368987)
XLA Ops:
  0.6 1.6 broadcast_in_dim.6
  2.2 10.9 %all-to-all-start = ((f32[8,32,384]{2,1,0:T(8,128)}), f32[8,32,384]{2,1,0:T(8,128)S(1)}, u32[]{:S(2)}, u32[]{:S(2)}) async-start(f32[8,32,384]{2,1,0:T(8,128)} %broadcast_in_dim.6), calls=%async_computation | async-start | bytes 786432 | tf_op jit(solution)/shard_map/all_to_all | solution.py:25
  13.1 7.4 %collective-permute-start = (f32[24,1024]{1,0:T(8,128)}, f32[24,1024]{1,0:T(8,128)S(1)}, u32[]{:S(2)}, u32[]{:S(2)}) collective-permute-start(f32[24,1024]{1,0:T(8,128)} %bitcast.29), channel_id=1, source_target_pairs={{0,256},{64,320},{128,384},{192,448},{256,0},{320,64},{384,128},{4... | collective-permute-start | bytes 294920 | tf_op jit(solution)/shard_map/ppermute | solution.py:222
  20.5 6.8 %all-to-all-done = f32[8,32,384]{2,1,0:T(8,128)S(1)} async-done(((f32[8,32,384]{2,1,0:T(8,128)}), f32[8,32,384]{2,1,0:T(8,128)S(1)}, u32[]{:S(2)}, u32[]{:S(2)}) %all-to-all-start) | async-done | bytes 393248 | tf_op jit(solution)/shard_map/all_to_all | solution.py:25
  27.3 1.3 broadcast_in_dim.15
  28.6 0.0 copy-start.1
  28.6 4.1 %all-to-all-start.1 = ((f32[4,256,384]{2,1,0:T(8,128)}), f32[4,256,384]{2,1,0:T(8,128)S(1)}, u32[]{:S(2)}, u32[]{:S(2)}) async-start(f32[4,256,384]{2,1,0:T(8,128)} %broadcast_in_dim.15), calls=%async_computation.1 | async-start | bytes 3145728 | tf_op jit(solution)/shard_map/all_to_all | solution.py:25
  32.7 0.0 collective-permute-done
  32.7 0.0 copy-done.1
  32.8 4.2 %collective-permute-start.3 = (f32[2,24,1024]{2,1,0:T(8,128)S(1)}, f32[2,24,1024]{2,1,0:T(8,128)S(1)}, u32[]{:S(2)}, u32[]{:S(2)}) collective-permute-start(f32[2,24,1024]{2,1,0:T(8,128)S(1)} %pad_maximum_fusion.refs_0_), channel_id=1, source_target_pairs={{0,128},{64,192},{128,256},{192,320},{256,384},{320,448},{384,0},{... | collective-permute-start | bytes 589832 | tf_op jit(solution)/shard_map/ppermute | solution.py:222
  37.0 3.3 %collective-permute-start.2 = (f32[2,24,1024]{2,1,0:T(8,128)S(1)}, f32[2,24,1024]{2,1,0:T(8,128)S(1)}, u32[]{:S(2)}, u32[]{:S(2)}) collective-permute-start(f32[2,24,1024]{2,1,0:T(8,128)S(1)} %pad_maximum_fusion.refs_0_), channel_id=1, source_target_pairs={{0,448},{64,0},{128,64},{192,128},{256,192},{320,256},{384,320},{4... | collective-permute-start | bytes 589832 | tf_op jit(solution)/shard_map/ppermute | solution.py:222
  40.3 2.0 %collective-permute-start.1 = (f32[2,24,1024]{2,1,0:T(8,128)S(1)}, f32[2,24,1024]{2,1,0:T(8,128)S(1)}, u32[]{:S(2)}, u32[]{:S(2)}) collective-permute-start(f32[2,24,1024]{2,1,0:T(8,128)S(1)} %pad_maximum_fusion.refs_0_), channel_id=1, source_target_pairs={{0,64},{64,128},{128,192},{192,256},{256,320},{320,384},{384,448},... | collective-permute-start | bytes 589832 | tf_op jit(solution)/shard_map/ppermute | solution.py:222
  42.3 1.4 collective-permute-done.3.refs_3_
  43.7 0.0 collective-permute-done.2.refs_2_
  43.7 7.7 %collective-permute-done.1.refs_1_ = f32[2,24,1024]{2,1,0:T(8,128)S(1)} collective-permute-done((f32[2,24,1024]{2,1,0:T(8,128)S(1)}, f32[2,24,1024]{2,1,0:T(8,128)S(1)}, u32[]{:S(2)}, u32[]{:S(2)}) %collective-permute-start.1) | collective-permute-done | bytes 196640 | tf_op jit(solution)/shard_map/ppermute | solution.py:222
  51.5 0.1 shard_map.41.mine_ref
  51.5 3.1 %collective-permute-start.4 = (f32[4,2,24,1024]{3,2,1,0:T(8,128)S(1)}, f32[4,2,24,1024]{3,2,1,0:T(8,128)S(1)}, u32[]{:S(2)}, u32[]{:S(2)}) collective-permute-start(f32[4,2,24,1024]{3,2,1,0:T(8,128)S(1)} %shard_map.41.mine_ref), channel_id=1, source_target_pairs={{0,32},{32,0},{1,33},{33,1},{2,34},{34,2},{3,35},{35,3},{4,36},{36... | collective-permute-start | bytes 2359304 | tf_op jit(solution)/shard_map/ppermute | solution.py:232
  54.7 0.1 stack.76
  54.8 1.7 collective-permute-done.4.theirs_ref
  56.5 0.0 all-to-all-done.1
  56.5 6.4 %shard_map.42 = (f32[1024,1024]{1,0:T(8,128)S(1)}, f32[384,1024]{1,0:T(8,128)S(1)}, f32[32,8,128]{2,1,0:T(8,128)S(1)}) custom-call(s32[16]{0:T(128)S(1)} %broadcast_multiply_fusion.spot_ref, f32[4,2,24,1024]{3,2,1,0:T(8,128)S(1)} %shard_map.41.mine_ref, f32[4,2,24,1024]{3,2,1,0:T(8,128)S(1)} %collective-permute-done.4.theirs_ref, f32[1024,384]{1,0:T(8,128)S(1)} %bitcast.25), custom_call_target="tpu_custom_call" | custom-call | tf_op jit(solution)/shard_map/pallas_call | solution.py:205
  62.9 13.8 %all_to_all.50.in_ref = f32[32,8,128]{2,1,0:T(8,128)S(1)} all-to-all(f32[32,8,128]{2,1,0:T(8,128)S(1)} %get-tuple-element.12), channel_id=1, replica_groups=mesh['y'=8,'core'=2,'x'=4,'z'=8] {'x','z'}, dimensions={0} | all-to-all | bytes 262144 | tf_op jit(solution)/shard_map/all_to_all | solution.py:251
  76.7 1.3 shard_map.43
  78.0 15.9 %all_to_all.51.in_ref = f32[16,8,128]{2,1,0:T(8,128)S(1)} all-to-all(f32[16,8,128]{2,1,0:T(8,128)S(1)} %get-tuple-element.14), channel_id=1, replica_groups=mesh['y'=8,'core'=2,'x'=4,'z'=8] {'y','core'}, dimensions={0} | all-to-all | bytes 131072 | tf_op jit(solution)/shard_map/all_to_all | solution.py:251
  93.9 1.0 shard_map.44
  94.9 12.4 %all_to_all.52.in_ref = f32[32,8,128]{2,1,0:T(8,128)S(1)} all-to-all(f32[32,8,128]{2,1,0:T(8,128)S(1)} %get-tuple-element.16), channel_id=1, replica_groups=mesh['y'=8,'core'=2,'x'=4,'z'=8] {'x','z'}, dimensions={0} | all-to-all | bytes 262144 | tf_op jit(solution)/shard_map/all_to_all | solution.py:251
  107.3 0.5 shard_map.45
  107.8 12.3 %all_to_all.53.in_ref = f32[16,8,128]{2,1,0:T(8,128)S(1)} all-to-all(f32[16,8,128]{2,1,0:T(8,128)S(1)} %shard_map.45), channel_id=1, replica_groups=mesh['y'=8,'core'=2,'x'=4,'z'=8] {'y','core'}, dimensions={0} | all-to-all | bytes 131072 | tf_op jit(solution)/shard_map/all_to_all | solution.py:251
  120.1 0.4 shard_map.46
  120.5 12.4 %all_to_all.54.in_ref = f32[32,8,128]{2,1,0:T(8,128)S(1)} all-to-all(f32[32,8,128]{2,1,0:T(8,128)S(1)} %shard_map.46), channel_id=1, replica_groups=mesh['y'=8,'core'=2,'x'=4,'z'=8] {'x','z'}, dimensions={0} | all-to-all | bytes 262144 | tf_op jit(solution)/shard_map/all_to_all | solution.py:251
  132.9 0.5 shard_map.47
  133.4 12.3 %all_to_all.55.in_ref = f32[16,8,128]{2,1,0:T(8,128)S(1)} all-to-all(f32[16,8,128]{2,1,0:T(8,128)S(1)} %shard_map.47), channel_id=1, replica_groups=mesh['y'=8,'core'=2,'x'=4,'z'=8] {'y','core'}, dimensions={0} | all-to-all | bytes 131072 | tf_op jit(solution)/shard_map/all_to_all | solution.py:251
  145.8 4.5 %shard_map.48 = (f32[8,128]{1,0:T(8,128)}, f32[32,104,128]{2,1,0:T(8,128)S(1)}) custom-call(f32[16,8,128]{2,1,0:T(8,128)S(1)} %all_to_all.55.in_ref, f32[8,128]{1,0:T(8,128)S(1)} %get-tuple-element.18.lse_ref, f32[1024,1024]{1,0:T(8,128)S(1)} %get-tuple-element.17.plan_ref, f32[384,1024]{1,0:T(8,128)S(1)} %get-tuple-element.19.data_ref), custom_call_target="tpu_custom_call" | custom-call | tf_op jit(solution)/shard_map/pallas_call | solution.py:205
  150.3 24.4 %all_to_all.56 = f32[4,832,128]{2,1,0:T(8,128)S(1)} all-to-all(f32[4,832,128]{2,1,0:T(8,128)S(1)} %bitcast.26), channel_id=1, replica_groups=mesh['y'=8,'core'=2,'x'=4,'z'=8] {'x'}, dimensions={0} | all-to-all | bytes 3407872 | tf_op jit(solution)/shard_map/all_to_all | solution.py:251
  174.7 0.0 copy-start
  174.7 0.1 reduce_sum.9
  174.8 16.3 %all_to_all.57.in_ref = f32[8,104,128]{2,1,0:T(8,128)S(1)} all-to-all(f32[8,104,128]{2,1,0:T(8,128)S(1)} %bitcast.27), channel_id=1, replica_groups=mesh['y'=8,'core'=2,'x'=4,'z'=8] {'z'}, dimensions={0} | all-to-all | bytes 851968 | tf_op jit(solution)/shard_map/all_to_all | solution.py:251
  191.1 0.0 copy-done
  191.1 0.7 shard_map.49
  (2 shorter events, 0.0 us)
Async XLA Ops:
  2.2 25.1 %all-to-all-start = ((f32[8,32,384]{2,1,0:T(8,128)}), f32[8,32,384]{2,1,0:T(8,128)S(1)}, u32[]{:S(2)}, u32[]{:S(2)}) async-start(f32[8,32,384]{2,1,0:T(8,128)} %broadcast_in_dim.6), calls=%async_computation | async-start | bytes 786432 | tf_op jit(solution)/shard_map/all_to_all | solution.py:25
  13.1 19.7 %collective-permute-start = (f32[24,1024]{1,0:T(8,128)}, f32[24,1024]{1,0:T(8,128)S(1)}, u32[]{:S(2)}, u32[]{:S(2)}) collective-permute-start(f32[24,1024]{1,0:T(8,128)} %bitcast.29), channel_id=1, source_target_pairs={{0,256},{64,320},{128,384},{192,448},{256,0},{320,64},{384,128},{4... | collective-permute-start | bytes 294920 | tf_op jit(solution)/shard_map/ppermute | solution.py:222
  28.6 4.2 %copy-start.1 = (f32[1024,24]{0,1:T(8,128)S(1)}, f32[1024,24]{0,1:T(8,128)}, u32[]{:S(2)}) copy-start(f32[1024,24]{0,1:T(8,128)} %param.3) | copy-start | bytes 294916
  28.6 27.9 %all-to-all-start.1 = ((f32[4,256,384]{2,1,0:T(8,128)}), f32[4,256,384]{2,1,0:T(8,128)S(1)}, u32[]{:S(2)}, u32[]{:S(2)}) async-start(f32[4,256,384]{2,1,0:T(8,128)} %broadcast_in_dim.15), calls=%async_computation.1 | async-start | bytes 3145728 | tf_op jit(solution)/shard_map/all_to_all | solution.py:25
  32.8 10.9 %collective-permute-start.3 = (f32[2,24,1024]{2,1,0:T(8,128)S(1)}, f32[2,24,1024]{2,1,0:T(8,128)S(1)}, u32[]{:S(2)}, u32[]{:S(2)}) collective-permute-start(f32[2,24,1024]{2,1,0:T(8,128)S(1)} %pad_maximum_fusion.refs_0_), channel_id=1, source_target_pairs={{0,128},{64,192},{128,256},{192,320},{256,384},{320,448},{384,0},{... | collective-permute-start | bytes 589832 | tf_op jit(solution)/shard_map/ppermute | solution.py:222
  37.0 6.7 %collective-permute-start.2 = (f32[2,24,1024]{2,1,0:T(8,128)S(1)}, f32[2,24,1024]{2,1,0:T(8,128)S(1)}, u32[]{:S(2)}, u32[]{:S(2)}) collective-permute-start(f32[2,24,1024]{2,1,0:T(8,128)S(1)} %pad_maximum_fusion.refs_0_), channel_id=1, source_target_pairs={{0,448},{64,0},{128,64},{192,128},{256,192},{320,256},{384,320},{4... | collective-permute-start | bytes 589832 | tf_op jit(solution)/shard_map/ppermute | solution.py:222
  40.3 11.2 %collective-permute-start.1 = (f32[2,24,1024]{2,1,0:T(8,128)S(1)}, f32[2,24,1024]{2,1,0:T(8,128)S(1)}, u32[]{:S(2)}, u32[]{:S(2)}) collective-permute-start(f32[2,24,1024]{2,1,0:T(8,128)S(1)} %pad_maximum_fusion.refs_0_), channel_id=1, source_target_pairs={{0,64},{64,128},{128,192},{192,256},{256,320},{320,384},{384,448},... | collective-permute-start | bytes 589832 | tf_op jit(solution)/shard_map/ppermute | solution.py:222
  51.5 5.0 %collective-permute-start.4 = (f32[4,2,24,1024]{3,2,1,0:T(8,128)S(1)}, f32[4,2,24,1024]{3,2,1,0:T(8,128)S(1)}, u32[]{:S(2)}, u32[]{:S(2)}) collective-permute-start(f32[4,2,24,1024]{3,2,1,0:T(8,128)S(1)} %shard_map.41.mine_ref), channel_id=1, source_target_pairs={{0,32},{32,0},{1,33},{33,1},{2,34},{34,2},{3,35},{35,3},{4,36},{36... | collective-permute-start | bytes 2359304 | tf_op jit(solution)/shard_map/ppermute | solution.py:232
  174.7 16.4 %copy-start = (f32[32,384]{1,0:T(8,128)S(1)}, f32[32,384]{1,0:T(8,128)}, u32[]{:S(2)}) copy-start(f32[32,384]{1,0:T(8,128)} %noise_ref.1) | copy-start | bytes 147460

commit v6 on v5

--- a/solution.py
+++ b/solution.py
@@ -16,7 +16,8 @@
 BLOCK = 256
 X_CHIPS = 4
 INTERPRET = False
-SRC, TGT = ("y", "core"), ("x", "z")
+LIMIT = 24 << 20
+SRC, TGT, NEAR, FAR = ("y", "core"), ("x", "zh", "zb"), ("x", "zb"), "zh"
 F32 = jnp.float32
 
 
@@ -67,14 +68,18 @@
         refs[-1][k] = ref[...]
 
 
-def cost_kernel(spot_ref, mine_ref, theirs_ref, noise_ref, gain_ref, data_ref, out_ref,
-                rows_ref, terms_ref):
+def order_kernel(hops, count, mine_ref, theirs_ref, data_ref):
+    at, core = lax.axis_index("y"), lax.axis_index("core")
     groups, halfs, deep, _ = mine_ref.shape
     for c, ref in enumerate((mine_ref, theirs_ref)):
         for k in range(groups):
             for h in range(halfs):
-                spot = pl.multiple_of(spot_ref[(c * groups + k) * halfs + h], 8)
-                data_ref[pl.ds(spot, deep), :] = ref[k, h]
+                chip = lax.rem(at + (2 * count - hops[k] - h * (count // 2)), count)
+                spot = (2 * chip + (1 - core if c else core)) * deep
+                data_ref[pl.ds(pl.multiple_of(spot, 8), deep), :] = ref[k, h]
+
+
+def cost_kernel(data_ref, noise_ref, gain_ref, out_ref, rows_ref, terms_ref):
     data = data_ref[...]
     feats = data.shape[0]
     scale = 1.0 / (feats * EPS)
@@ -201,12 +206,11 @@
             out_ref[spot] = parts[at : at + 8] * inverse - noise_ref[spot]
 
 
-def call(kernel, outs, *args, scratch=(), limit=24 << 20):
+def call(kernel, outs, *args, scratch=(), limit=LIMIT):
     return pl.pallas_call(
         kernel,
-        out_shape=[jax.ShapeDtypeStruct(shape, F32) for shape in outs],
-        in_specs=[pl.BlockSpec(memory_space=pltpu.VMEM if a.dtype == F32 else pltpu.SMEM)
-                  for a in args],
+        out_shape=[jax.ShapeDtypeStruct(o, F32) if isinstance(o, tuple) else o for o in outs],
+        in_specs=[pl.BlockSpec(memory_space=pltpu.VMEM)] * len(args),
         out_specs=[pl.BlockSpec(memory_space=pltpu.VMEM)] * len(outs),
         scratch_shapes=list(scratch),
         compiler_params=pltpu.CompilerParams(vmem_limit_bytes=limit),
@@ -216,31 +220,30 @@
 
 def gathered(noise, data):
     count = lax.axis_size("y")
-    at, core = lax.axis_index("y"), lax.axis_index("core")
 
     def shifted(value, hop):
         return lax.ppermute(value, "y", [(i, (i + hop) % count) for i in range(count)])
 
     hops = [0] + [h for k in range(1, count // 4 + 1) for h in (k, -k)][: count // 2 - 1]
     own = data.T
+    rows = spread(noise, FAR).reshape(-1, noise.shape[1])
     far = shifted(own, count // 2)
-    rows = spread(noise, "z").reshape(-1, noise.shape[1])
     both = jnp.stack([own, far])
     near = [shifted(both, h) for h in hops[1:]]
-    rows = spread(rows, "x").reshape(-1, noise.shape[1])
+    rows = spread(rows, NEAR).reshape(-1, noise.shape[1])
     (mine,) = call(pile_kernel, [(count // 2, *both.shape)], both, *near, limit=8 << 20)
     theirs = lax.ppermute(mine, "core", [(0, 1), (1, 0)])
-    spots = [2 * ((at - hop - h * (count // 2) + 2 * count) % count) for hop in hops
-             for h in range(2)]
-    spots = jnp.stack([s + c for c in (core, 1 - core) for s in spots])
-    return rows, mine, theirs, (spots * own.shape[0]).astype(jnp.int32)
+    (columns,) = call(functools.partial(order_kernel, hops, count),
+                      [(2 * count * own.shape[0], own.shape[1])], mine, theirs,
+                      limit=8 << 20)
+    return rows, columns
 
 
 def per_device(noise, data):
     own_rows, feats = noise.shape
-    rows, mine, theirs, spots = gathered(noise, data)
-    n_rows, n_cols = rows.shape[0], mine.shape[-1]
-    n_src, n_tgt, n_x, n_z = (lax.axis_size(a) for a in (SRC, TGT, "x", "z"))
+    rows, columns = gathered(noise, data)
+    n_rows, n_cols = rows.shape[0], columns.shape[1]
+    n_src, n_tgt, n_near, n_far = (lax.axis_size(a) for a in (SRC, TGT, NEAR, FAR))
     src_total, tgt_total = n_rows * n_src, n_cols * n_tgt
     r_tiles, c_tiles = (n_rows // LANES, LANES), (n_cols // LANES, LANES)
     to_tgt, to_src = (n_tgt, *r_tiles), (n_src, *c_tiles)
@@ -250,8 +253,8 @@
     def swap(value, axis):
         return lax.all_to_all(value, axis, 0, 0)
 
-    gain, columns, message = call(
-        cost_kernel, [square, (feats, n_cols), to_tgt], spots, mine, theirs, rows,
+    gain, message = call(
+        cost_kernel, [square, to_tgt], columns, rows,
         scratch=row_scratch + [pltpu.VMEM((len(LEFT) * feats, n_cols), jnp.bfloat16)])
     f_pot, message = call(functools.partial(first_column_kernel, math.log(src_total)),
                           [r_tiles, to_src], swap(message, TGT), gain)
@@ -268,15 +271,15 @@
         functools.partial(final_kernel, float(tgt_total), own_rows),
         [c_tiles, (n_tgt, tall, LANES)], swap(message, SRC), lse, plan, columns,
         scratch=[pltpu.VMEM((feats + LANES, n_cols), jnp.bfloat16)] * 2)
-    part = jnp.sum(swap(part.reshape(n_x, n_z * tall, LANES), "x"), axis=0)
-    part = swap(part.reshape(n_z, tall, LANES), "z")
+    part = jnp.sum(swap(part.reshape(n_near, n_far * tall, LANES), NEAR), axis=0)
+    part = swap(part.reshape(n_far, tall, LANES), FAR)
     (velocity,) = call(last_kernel, [noise.shape], part, noise)
     return velocity, g_pot.reshape(-1)
 
 
 def solution(mesh):
     src, tgt = mesh.shape["src"], mesh.shape["tgt"]
-    split = Mesh(mesh.devices.reshape(src // 2, 2, X_CHIPS, tgt // X_CHIPS), SRC + TGT)
+    split = Mesh(mesh.devices.reshape(src // 2, 2, X_CHIPS, tgt // X_CHIPS // 2, 2), SRC + TGT)
     return jax.shard_map(
         per_device,
         mesh=split,

time: 193 us -> 194 us (level)
  the two profiles are of different devices: /device:TPU:1 before, /device:TPU:2 now
where the time goes in v6:
time: 194 us; the launch traced here: 193 us
  blocking collectives  138 us (71%)
  starting transfers between devices  24.6 us (13%)
  Pallas kernels  14.8 us (8%)
  waiting for transfers between devices  12.6 us (6%)
  local copies, waits for them, and re-layouts  2.08 us (1%)
    all_to_all x8, blocking collectives, swap(): return lax.all_to_all(value, axis, 0, 0)  118 us
    all_to_all x1, blocking collectives, spread(): lax.all_to_all(jnp.broadcast_to(value[None], (count,) + value.shape), axi...  20.4 us
    ppermute x4, starting transfers between devices, shifted(): lax.ppermute(value, 'y', [(i, (i + hop) % count) for i in range(count)])  17.3 us
    pallas_call x10, Pallas kernels, call(): pl.pallas_call(kernel, out_shape=[jax.ShapeDtypeStruct(o, F32) if isinsta...  14.8 us
    ppermute x4, waiting for transfers between devices, shifted(): lax.ppermute(value, 'y', [(i, (i + hop) % count) for i in range(count)])  10.3 us
    all_to_all x1, starting transfers between devices, spread(): lax.all_to_all(jnp.broadcast_to(value[None], (count,) + value.shape), axi...  5.3 us
  transfers between devices with their start and end apart: 6, of which 4 were waited for; matrix products, arithmetic and copies ran while one was open for 0% of the time, Pallas kernels for 0%

profile of v6, /device:TPU:2, one launch (start us, length us, event | category | flops | bytes accessed | tf_op | source)
XLA Modules:
  0.0 193.3 jit_solution(15318400563789376287)
XLA Ops:
  0.6 0.8 broadcast_in_dim.6
  1.4 20.4 %all_to_all.50 = f32[4,32,384]{2,1,0:T(8,128)S(1)} all-to-all(f32[4,32,384]{2,1,0:T(8,128)S(1)} %broadcast_in_dim.6), channel_id=1, replica_groups=mesh['y'=8,'core'=2,'x'=4,'zh'=4,'zb'=2] {'zh'}, dimensions={0} | all-to-all | bytes 393216 | tf_op jit(solution)/shard_map/all_to_all | solution.py:26
  21.8 1.3 broadcast_in_dim.15
  23.1 0.0 copy-start.1
  23.1 5.3 %all-to-all-start.1 = ((f32[8,128,384]{2,1,0:T(8,128)}), f32[8,128,384]{2,1,0:T(8,128)S(1)}, u32[]{:S(2)}, u32[]{:S(2)}) async-start(f32[8,128,384]{2,1,0:T(8,128)} %broadcast_in_dim.15), calls=%async_computation.1 | async-start | bytes 3145728 | tf_op jit(solution)/shard_map/all_to_all | solution.py:26
  28.4 0.0 copy-done.1
  28.4 7.7 %collective-permute-start = (f32[24,1024]{1,0:T(8,128)S(1)}, f32[24,1024]{1,0:T(8,128)S(1)}, u32[]{:S(2)}, u32[]{:S(2)}) collective-permute-start(f32[24,1024]{1,0:T(8,128)S(1)} %bitcast.13), channel_id=1, source_target_pairs={{0,256},{64,320},{128,384},{192,448},{256,0},{320,64},{384,128},{4... | collective-permute-start | bytes 294920 | tf_op jit(solution)/shard_map/ppermute | solution.py:225
  36.1 3.7 %collective-permute-done = f32[24,1024]{1,0:T(8,128)S(1)} collective-permute-done((f32[24,1024]{1,0:T(8,128)S(1)}, f32[24,1024]{1,0:T(8,128)S(1)}, u32[]{:S(2)}, u32[]{:S(2)}) %collective-permute-start) | collective-permute-done | bytes 98336 | tf_op jit(solution)/shard_map/ppermute | solution.py:225
  39.9 3.8 %collective-permute-start.3 = (f32[2,24,1024]{2,1,0:T(8,128)S(1)}, f32[2,24,1024]{2,1,0:T(8,128)S(1)}, u32[]{:S(2)}, u32[]{:S(2)}) collective-permute-start(f32[2,24,1024]{2,1,0:T(8,128)S(1)} %pad_maximum_fusion.refs_0_), channel_id=1, source_target_pairs={{0,128},{64,192},{128,256},{192,320},{256,384},{320,448},{384,0},{... | collective-permute-start | bytes 589832 | tf_op jit(solution)/shard_map/ppermute | solution.py:225
  43.7 3.5 %collective-permute-start.2 = (f32[2,24,1024]{2,1,0:T(8,128)S(1)}, f32[2,24,1024]{2,1,0:T(8,128)S(1)}, u32[]{:S(2)}, u32[]{:S(2)}) collective-permute-start(f32[2,24,1024]{2,1,0:T(8,128)S(1)} %pad_maximum_fusion.refs_0_), channel_id=1, source_target_pairs={{0,448},{64,0},{128,64},{192,128},{256,192},{320,256},{384,320},{4... | collective-permute-start | bytes 589832 | tf_op jit(solution)/shard_map/ppermute | solution.py:225
  47.2 2.3 %collective-permute-start.1 = (f32[2,24,1024]{2,1,0:T(8,128)S(1)}, f32[2,24,1024]{2,1,0:T(8,128)S(1)}, u32[]{:S(2)}, u32[]{:S(2)}) collective-permute-start(f32[2,24,1024]{2,1,0:T(8,128)S(1)} %pad_maximum_fusion.refs_0_), channel_id=1, source_target_pairs={{0,64},{64,128},{128,192},{192,256},{256,320},{320,384},{384,448},... | collective-permute-start | bytes 589832 | tf_op jit(solution)/shard_map/ppermute | solution.py:225
  49.5 4.7 %collective-permute-done.3.refs_3_ = f32[2,24,1024]{2,1,0:T(8,128)S(1)} collective-permute-done((f32[2,24,1024]{2,1,0:T(8,128)S(1)}, f32[2,24,1024]{2,1,0:T(8,128)S(1)}, u32[]{:S(2)}, u32[]{:S(2)}) %collective-permute-start.3) | collective-permute-done | bytes 196640 | tf_op jit(solution)/shard_map/ppermute | solution.py:225
  54.2 0.0 collective-permute-done.2.refs_2_
  54.2 1.9 collective-permute-done.1.refs_1_
  56.1 0.1 shard_map.41.mine_ref
  56.2 1.9 collective-permute-start.4
  58.1 2.3 %collective-permute-done.4.theirs_ref = f32[4,2,24,1024]{3,2,1,0:T(8,128)S(1)} collective-permute-done((f32[4,2,24,1024]{3,2,1,0:T(8,128)S(1)}, f32[4,2,24,1024]{3,2,1,0:T(8,128)S(1)}, u32[]{:S(2)}, u32[]{:S(2)}) %collective-permute-start.4) | collective-permute-done | bytes 786464 | tf_op jit(solution)/shard_map/ppermute | solution.py:235
  60.3 0.2 shard_map.42.data_ref
  60.5 0.0 all-to-all-done.1
  60.5 5.7 %shard_map.43 = (f32[1024,1024]{1,0:T(8,128)S(1)}, f32[32,8,128]{2,1,0:T(8,128)S(1)}) custom-call(f32[384,1024]{1,0:T(8,128)S(1)} %shard_map.42.data_ref, f32[1024,384]{1,0:T(8,128)S(1)} %bitcast.9), custom_call_target="tpu_custom_call" | custom-call | tf_op jit(solution)/shard_map/pallas_call | solution.py:210
  66.2 16.4 %all_to_all.51.in_ref = f32[32,8,128]{2,1,0:T(8,128)S(1)} all-to-all(f32[32,8,128]{2,1,0:T(8,128)S(1)} %get-tuple-element.11), channel_id=1, replica_groups=mesh['y'=8,'core'=2,'x'=4,'zh'=4,'zb'=2] {'x','zh','zb'}, dimensions={0} | all-to-all | bytes 262144 | tf_op jit(solution)/shard_map/all_to_all | solution.py:254
  82.6 1.3 shard_map.44
  84.0 13.9 %all_to_all.52.in_ref = f32[16,8,128]{2,1,0:T(8,128)S(1)} all-to-all(f32[16,8,128]{2,1,0:T(8,128)S(1)} %get-tuple-element.13), channel_id=1, replica_groups=mesh['y'=8,'core'=2,'x'=4,'zh'=4,'zb'=2] {'y','core'}, dimensions={0} | all-to-all | bytes 131072 | tf_op jit(solution)/shard_map/all_to_all | solution.py:254
  97.8 1.0 shard_map.45
  98.8 14.4 %all_to_all.53.in_ref = f32[32,8,128]{2,1,0:T(8,128)S(1)} all-to-all(f32[32,8,128]{2,1,0:T(8,128)S(1)} %get-tuple-element.15), channel_id=1, replica_groups=mesh['y'=8,'core'=2,'x'=4,'zh'=4,'zb'=2] {'x','zh','zb'}, dimensions={0} | all-to-all | bytes 262144 | tf_op jit(solution)/shard_map/all_to_all | solution.py:254
  113.2 0.5 shard_map.46
  113.7 10.4 %all_to_all.54.in_ref = f32[16,8,128]{2,1,0:T(8,128)S(1)} all-to-all(f32[16,8,128]{2,1,0:T(8,128)S(1)} %shard_map.46), channel_id=1, replica_groups=mesh['y'=8,'core'=2,'x'=4,'zh'=4,'zb'=2] {'y','core'}, dimensions={0} | all-to-all | bytes 131072 | tf_op jit(solution)/shard_map/all_to_all | solution.py:254
  124.1 0.4 shard_map.47
  124.5 14.4 %all_to_all.55.in_ref = f32[32,8,128]{2,1,0:T(8,128)S(1)} all-to-all(f32[32,8,128]{2,1,0:T(8,128)S(1)} %shard_map.47), channel_id=1, replica_groups=mesh['y'=8,'core'=2,'x'=4,'zh'=4,'zb'=2] {'x','zh','zb'}, dimensions={0} | all-to-all | bytes 262144 | tf_op jit(solution)/shard_map/all_to_all | solution.py:254
  138.9 0.5 shard_map.48
  139.4 10.4 %all_to_all.56.in_ref = f32[16,8,128]{2,1,0:T(8,128)S(1)} all-to-all(f32[16,8,128]{2,1,0:T(8,128)S(1)} %shard_map.48), channel_id=1, replica_groups=mesh['y'=8,'core'=2,'x'=4,'zh'=4,'zb'=2] {'y','core'}, dimensions={0} | all-to-all | bytes 131072 | tf_op jit(solution)/shard_map/all_to_all | solution.py:254
  149.7 4.5 %shard_map.49 = (f32[8,128]{1,0:T(8,128)}, f32[32,104,128]{2,1,0:T(8,128)S(1)}) custom-call(f32[16,8,128]{2,1,0:T(8,128)S(1)} %all_to_all.56.in_ref, f32[8,128]{1,0:T(8,128)S(1)} %get-tuple-element.17.lse_ref, f32[1024,1024]{1,0:T(8,128)S(1)} %get-tuple-element.16.plan_ref, f32[384,1024]{1,0:T(8,128)S(1)} %shard_map.42.data_ref), custom_call_target="tpu_custom_call" | custom-call | tf_op jit(solution)/shard_map/pallas_call | solution.py:210
  154.3 26.1 %all_to_all.57 = f32[8,416,128]{2,1,0:T(8,128)S(1)} all-to-all(f32[8,416,128]{2,1,0:T(8,128)S(1)} %bitcast.10), channel_id=1, replica_groups=mesh['y'=8,'core'=2,'x'=4,'zh'=4,'zb'=2] {'x','zb'}, dimensions={0} | all-to-all | bytes 3407872 | tf_op jit(solution)/shard_map/all_to_all | solution.py:254
  180.3 0.0 copy-start
  180.4 0.1 reduce_sum.9
  180.4 12.2 %all_to_all.58.in_ref = f32[4,104,128]{2,1,0:T(8,128)S(1)} all-to-all(f32[4,104,128]{2,1,0:T(8,128)S(1)} %bitcast.11), channel_id=1, replica_groups=mesh['y'=8,'core'=2,'x'=4,'zh'=4,'zb'=2] {'zh'}, dimensions={0} | all-to-all | bytes 425984 | tf_op jit(solution)/shard_map/all_to_all | solution.py:254
  192.6 0.0 copy-done
  192.6 0.7 shard_map.50
  (1 shorter events, 0.0 us)
Async XLA Ops:
  23.1 5.3 %copy-start.1 = (f32[1024,24]{0,1:T(8,128)S(1)}, f32[1024,24]{0,1:T(8,128)}, u32[]{:S(2)}) copy-start(f32[1024,24]{0,1:T(8,128)} %param.3) | copy-start | bytes 294916
  23.1 37.4 %all-to-all-start.1 = ((f32[8,128,384]{2,1,0:T(8,128)}), f32[8,128,384]{2,1,0:T(8,128)S(1)}, u32[]{:S(2)}, u32[]{:S(2)}) async-start(f32[8,128,384]{2,1,0:T(8,128)} %broadcast_in_dim.15), calls=%async_computation.1 | async-start | bytes 3145728 | tf_op jit(solution)/shard_map/all_to_all | solution.py:26
  28.4 11.5 %collective-permute-start = (f32[24,1024]{1,0:T(8,128)S(1)}, f32[24,1024]{1,0:T(8,128)S(1)}, u32[]{:S(2)}, u32[]{:S(2)}) collective-permute-start(f32[24,1024]{1,0:T(8,128)S(1)} %bitcast.13), channel_id=1, source_target_pairs={{0,256},{64,320},{128,384},{192,448},{256,0},{320,64},{384,128},{4... | collective-permute-start | bytes 294920 | tf_op jit(solution)/shard_map/ppermute | solution.py:225
  39.9 14.4 %collective-permute-start.3 = (f32[2,24,1024]{2,1,0:T(8,128)S(1)}, f32[2,24,1024]{2,1,0:T(8,128)S(1)}, u32[]{:S(2)}, u32[]{:S(2)}) collective-permute-start(f32[2,24,1024]{2,1,0:T(8,128)S(1)} %pad_maximum_fusion.refs_0_), channel_id=1, source_target_pairs={{0,128},{64,192},{128,256},{192,320},{256,384},{320,448},{384,0},{... | collective-permute-start | bytes 589832 | tf_op jit(solution)/shard_map/ppermute | solution.py:225
  43.7 10.6 %collective-permute-start.2 = (f32[2,24,1024]{2,1,0:T(8,128)S(1)}, f32[2,24,1024]{2,1,0:T(8,128)S(1)}, u32[]{:S(2)}, u32[]{:S(2)}) collective-permute-start(f32[2,24,1024]{2,1,0:T(8,128)S(1)} %pad_maximum_fusion.refs_0_), channel_id=1, source_target_pairs={{0,448},{64,0},{128,64},{192,128},{256,192},{320,256},{384,320},{4... | collective-permute-start | bytes 589832 | tf_op jit(solution)/shard_map/ppermute | solution.py:225
  47.2 8.9 %collective-permute-start.1 = (f32[2,24,1024]{2,1,0:T(8,128)S(1)}, f32[2,24,1024]{2,1,0:T(8,128)S(1)}, u32[]{:S(2)}, u32[]{:S(2)}) collective-permute-start(f32[2,24,1024]{2,1,0:T(8,128)S(1)} %pad_maximum_fusion.refs_0_), channel_id=1, source_target_pairs={{0,64},{64,128},{128,192},{192,256},{256,320},{320,384},{384,448},... | collective-permute-start | bytes 589832 | tf_op jit(solution)/shard_map/ppermute | solution.py:225
  56.2 4.2 %collective-permute-start.4 = (f32[4,2,24,1024]{3,2,1,0:T(8,128)S(1)}, f32[4,2,24,1024]{3,2,1,0:T(8,128)S(1)}, u32[]{:S(2)}, u32[]{:S(2)}) collective-permute-start(f32[4,2,24,1024]{3,2,1,0:T(8,128)S(1)} %shard_map.41.mine_ref), channel_id=1, source_target_pairs={{0,32},{32,0},{1,33},{33,1},{2,34},{34,2},{3,35},{35,3},{4,36},{36... | collective-permute-start | bytes 2359304 | tf_op jit(solution)/shard_map/ppermute | solution.py:235
  180.3 12.3 %copy-start = (f32[32,384]{1,0:T(8,128)S(1)}, f32[32,384]{1,0:T(8,128)}, u32[]{:S(2)}) copy-start(f32[32,384]{1,0:T(8,128)} %noise_ref.1) | copy-start | bytes 147460

commit v7 on v6

--- a/solution.py
+++ b/solution.py
@@ -68,14 +68,19 @@
         refs[-1][k] = ref[...]
 
 
+def turned(hop, core, count):
+    return hop * (1 - 2 * core) if abs(hop) < count // 2 else hop
+
+
 def order_kernel(hops, count, mine_ref, theirs_ref, data_ref):
     at, core = lax.axis_index("y"), lax.axis_index("core")
     groups, halfs, deep, _ = mine_ref.shape
     for c, ref in enumerate((mine_ref, theirs_ref)):
         for k in range(groups):
             for h in range(halfs):
-                chip = lax.rem(at + (2 * count - hops[k] - h * (count // 2)), count)
-                spot = (2 * chip + (1 - core if c else core)) * deep
+                owner = 1 - core if c else core
+                back = turned(hops[k], owner, count) + h * (count // 2)
+                spot = (2 * lax.rem(at + 2 * count - back, count) + owner) * deep
                 data_ref[pl.ds(pl.multiple_of(spot, 8), deep), :] = ref[k, h]
 
 
@@ -170,13 +175,12 @@
     lane = lax.broadcasted_iota(jnp.int32, (8, LANES), 1)
     tiles, wide = own_rows // 8, feats // LANES
 
-    def block(b, carry):
-        high, low = halves(plan_ref[pl.ds(pl.multiple_of(b * BLOCK, BLOCK), BLOCK), :])
-
-        def times(a, w_ref):
-            return lax.dot_general(a, w_ref[...], (((1,), (1,)), ((), ())),
-                                   preferred_element_type=F32)
-
+    def times(a, w_ref):
+        return lax.dot_general(a, w_ref[...], (((1,), (1,)), ((), ())),
+                               preferred_element_type=F32)
+
+    for b in range(plan_ref.shape[0] // BLOCK):
+        high, low = halves(plan_ref[b * BLOCK : (b + 1) * BLOCK, :])
         got = times(high, low_ref) + times(low, high_ref) + times(high, high_ref)
         for p in range(BLOCK // own_rows):
             peer = b * (BLOCK // own_rows) + p
@@ -188,9 +192,6 @@
                         at, c * LANES : (c + 1) * LANES]
                 mass = jnp.where(lane // (LANES // tiles) == r, got[at, feats:], mass)
             part_ref[peer, tiles * wide * 8 :, :] = mass
-        return carry
-
-    lax.fori_loop(0, plan_ref.shape[0] // BLOCK, block, 0)
 
 
 def last_kernel(in_ref, noise_ref, out_ref):
@@ -222,7 +223,9 @@
     count = lax.axis_size("y")
 
     def shifted(value, hop):
-        return lax.ppermute(value, "y", [(i, (i + hop) % count) for i in range(count)])
+        return lax.ppermute(value, SRC, [
+            (2 * i + c, 2 * ((i + turned(hop, c, count)) % count) + c)
+            for i in range(count) for c in range(2)])
 
     hops = [0] + [h for k in range(1, count // 4 + 1) for h in (k, -k)][: count // 2 - 1]
     own = data.T

time: 194 us -> 194 us (level)
  transfers between devices with their start and end apart: 6 -> 6, of which waited for: 4 -> 5; matrix products, arithmetic and copies ran while one was open for 0% -> 0% of each run, Pallas kernels for 0% -> 0%
where the time goes in v7:
time: 194 us; the launch traced here: 193 us
  blocking collectives  139 us (72%)
  starting transfers between devices  24.6 us (13%)
  Pallas kernels  14.3 us (7%)
  waiting for transfers between devices  12.4 us (6%)
  local copies, waits for them, and re-layouts  2.08 us (1%)
    all_to_all x8, blocking collectives, swap(): return lax.all_to_all(value, axis, 0, 0)  118 us
    all_to_all x1, blocking collectives, spread(): lax.all_to_all(jnp.broadcast_to(value[None], (count,) + value.shape), axi...  20.4 us
    ppermute x4, starting transfers between devices, shifted(): lax.ppermute(value, SRC, [(2 * i + c, 2 * ((i + turned(hop, c, count)) %...  17.3 us
    pallas_call x10, Pallas kernels, call(): pl.pallas_call(kernel, out_shape=[jax.ShapeDtypeStruct(o, F32) if isinsta...  14.3 us
    ppermute x4, waiting for transfers between devices, shifted(): lax.ppermute(value, SRC, [(2 * i + c, 2 * ((i + turned(hop, c, count)) %...  10.2 us
    all_to_all x1, starting transfers between devices, spread(): lax.all_to_all(jnp.broadcast_to(value[None], (count,) + value.shape), axi...  5.3 us
  transfers between devices with their start and end apart: 6, of which 5 were waited for; matrix products, arithmetic and copies ran while one was open for 0% of the time, Pallas kernels for 0%

profile of v7, /device:TPU:2, one launch (start us, length us, event | category | flops | bytes accessed | tf_op | source)
XLA Modules:
  0.0 192.8 jit_solution(15882431933325600249)
XLA Ops:
  0.6 0.8 broadcast_in_dim.6
  1.4 20.4 %all_to_all.50 = f32[4,32,384]{2,1,0:T(8,128)S(1)} all-to-all(f32[4,32,384]{2,1,0:T(8,128)S(1)} %broadcast_in_dim.6), channel_id=1, replica_groups=mesh['y'=8,'core'=2,'x'=4,'zh'=4,'zb'=2] {'zh'}, dimensions={0} | all-to-all | bytes 393216 | tf_op jit(solution)/shard_map/all_to_all | solution.py:26
  21.8 1.3 broadcast_in_dim.15
  23.1 0.0 copy-start.1
  23.1 5.3 %all-to-all-start.1 = ((f32[8,128,384]{2,1,0:T(8,128)}), f32[8,128,384]{2,1,0:T(8,128)S(1)}, u32[]{:S(2)}, u32[]{:S(2)}) async-start(f32[8,128,384]{2,1,0:T(8,128)} %broadcast_in_dim.15), calls=%async_computation.1 | async-start | bytes 3145728 | tf_op jit(solution)/shard_map/all_to_all | solution.py:26
  28.4 0.0 copy-done.1
  28.4 7.7 %collective-permute-start = (f32[24,1024]{1,0:T(8,128)S(1)}, f32[24,1024]{1,0:T(8,128)S(1)}, u32[]{:S(2)}, u32[]{:S(2)}) collective-permute-start(f32[24,1024]{1,0:T(8,128)S(1)} %bitcast.13), channel_id=1, source_target_pairs={{0,256},{32,288},{64,320},{96,352},{128,384},{160,416},{192,448},{... | collective-permute-start | bytes 294920 | tf_op jit(solution)/shard_map/ppermute | solution.py:226
  36.1 3.7 %collective-permute-done = f32[24,1024]{1,0:T(8,128)S(1)} collective-permute-done((f32[24,1024]{1,0:T(8,128)S(1)}, f32[24,1024]{1,0:T(8,128)S(1)}, u32[]{:S(2)}, u32[]{:S(2)}) %collective-permute-start) | collective-permute-done | bytes 98336 | tf_op jit(solution)/shard_map/ppermute | solution.py:226
  39.9 3.8 %collective-permute-start.3 = (f32[2,24,1024]{2,1,0:T(8,128)S(1)}, f32[2,24,1024]{2,1,0:T(8,128)S(1)}, u32[]{:S(2)}, u32[]{:S(2)}) collective-permute-start(f32[2,24,1024]{2,1,0:T(8,128)S(1)} %pad_maximum_fusion.refs_0_), channel_id=1, source_target_pairs={{0,128},{32,416},{64,192},{96,480},{128,256},{160,32},{192,320},{2... | collective-permute-start | bytes 589832 | tf_op jit(solution)/shard_map/ppermute | solution.py:226
  43.7 3.5 %collective-permute-start.2 = (f32[2,24,1024]{2,1,0:T(8,128)S(1)}, f32[2,24,1024]{2,1,0:T(8,128)S(1)}, u32[]{:S(2)}, u32[]{:S(2)}) collective-permute-start(f32[2,24,1024]{2,1,0:T(8,128)S(1)} %pad_maximum_fusion.refs_0_), channel_id=1, source_target_pairs={{0,448},{32,96},{64,0},{96,160},{128,64},{160,224},{192,128},{224,... | collective-permute-start | bytes 589832 | tf_op jit(solution)/shard_map/ppermute | solution.py:226
  47.2 2.3 %collective-permute-start.1 = (f32[2,24,1024]{2,1,0:T(8,128)S(1)}, f32[2,24,1024]{2,1,0:T(8,128)S(1)}, u32[]{:S(2)}, u32[]{:S(2)}) collective-permute-start(f32[2,24,1024]{2,1,0:T(8,128)S(1)} %pad_maximum_fusion.refs_0_), channel_id=1, source_target_pairs={{0,64},{32,480},{64,128},{96,32},{128,192},{160,96},{192,256},{224... | collective-permute-start | bytes 589832 | tf_op jit(solution)/shard_map/ppermute | solution.py:226
  49.5 2.1 %collective-permute-done.3.refs_3_ = f32[2,24,1024]{2,1,0:T(8,128)S(1)} collective-permute-done((f32[2,24,1024]{2,1,0:T(8,128)S(1)}, f32[2,24,1024]{2,1,0:T(8,128)S(1)}, u32[]{:S(2)}, u32[]{:S(2)}) %collective-permute-start.3) | collective-permute-done | bytes 196640 | tf_op jit(solution)/shard_map/ppermute | solution.py:226
  51.7 1.6 collective-permute-done.2.refs_2_
  53.3 2.7 %collective-permute-done.1.refs_1_ = f32[2,24,1024]{2,1,0:T(8,128)S(1)} collective-permute-done((f32[2,24,1024]{2,1,0:T(8,128)S(1)}, f32[2,24,1024]{2,1,0:T(8,128)S(1)}, u32[]{:S(2)}, u32[]{:S(2)}) %collective-permute-start.1) | collective-permute-done | bytes 196640 | tf_op jit(solution)/shard_map/ppermute | solution.py:226
  56.0 0.1 shard_map.41.mine_ref
  56.0 1.9 collective-permute-start.4
  58.0 2.3 %collective-permute-done.4.theirs_ref = f32[4,2,24,1024]{3,2,1,0:T(8,128)S(1)} collective-permute-done((f32[4,2,24,1024]{3,2,1,0:T(8,128)S(1)}, f32[4,2,24,1024]{3,2,1,0:T(8,128)S(1)}, u32[]{:S(2)}, u32[]{:S(2)}) %collective-permute-start.4) | collective-permute-done | bytes 786464 | tf_op jit(solution)/shard_map/ppermute | solution.py:238
  60.2 0.2 shard_map.42.data_ref
  60.4 0.0 all-to-all-done.1
  60.4 5.7 %shard_map.43 = (f32[1024,1024]{1,0:T(8,128)S(1)}, f32[32,8,128]{2,1,0:T(8,128)S(1)}) custom-call(f32[384,1024]{1,0:T(8,128)S(1)} %shard_map.42.data_ref, f32[1024,384]{1,0:T(8,128)S(1)} %bitcast.9), custom_call_target="tpu_custom_call" | custom-call | tf_op jit(solution)/shard_map/pallas_call | solution.py:211
  66.1 16.1 %all_to_all.51.in_ref = f32[32,8,128]{2,1,0:T(8,128)S(1)} all-to-all(f32[32,8,128]{2,1,0:T(8,128)S(1)} %get-tuple-element.11), channel_id=1, replica_groups=mesh['y'=8,'core'=2,'x'=4,'zh'=4,'zb'=2] {'x','zh','zb'}, dimensions={0} | all-to-all | bytes 262144 | tf_op jit(solution)/shard_map/all_to_all | solution.py:257
  82.2 1.3 shard_map.44
  83.6 14.3 %all_to_all.52.in_ref = f32[16,8,128]{2,1,0:T(8,128)S(1)} all-to-all(f32[16,8,128]{2,1,0:T(8,128)S(1)} %get-tuple-element.13), channel_id=1, replica_groups=mesh['y'=8,'core'=2,'x'=4,'zh'=4,'zb'=2] {'y','core'}, dimensions={0} | all-to-all | bytes 131072 | tf_op jit(solution)/shard_map/all_to_all | solution.py:257
  97.9 1.0 shard_map.45
  98.9 14.4 %all_to_all.53.in_ref = f32[32,8,128]{2,1,0:T(8,128)S(1)} all-to-all(f32[32,8,128]{2,1,0:T(8,128)S(1)} %get-tuple-element.15), channel_id=1, replica_groups=mesh['y'=8,'core'=2,'x'=4,'zh'=4,'zb'=2] {'x','zh','zb'}, dimensions={0} | all-to-all | bytes 262144 | tf_op jit(solution)/shard_map/all_to_all | solution.py:257
  113.3 0.5 shard_map.46
  113.8 10.4 %all_to_all.54.in_ref = f32[16,8,128]{2,1,0:T(8,128)S(1)} all-to-all(f32[16,8,128]{2,1,0:T(8,128)S(1)} %shard_map.46), channel_id=1, replica_groups=mesh['y'=8,'core'=2,'x'=4,'zh'=4,'zb'=2] {'y','core'}, dimensions={0} | all-to-all | bytes 131072 | tf_op jit(solution)/shard_map/all_to_all | solution.py:257
  124.1 0.4 shard_map.47
  124.5 14.4 %all_to_all.55.in_ref = f32[32,8,128]{2,1,0:T(8,128)S(1)} all-to-all(f32[32,8,128]{2,1,0:T(8,128)S(1)} %shard_map.47), channel_id=1, replica_groups=mesh['y'=8,'core'=2,'x'=4,'zh'=4,'zb'=2] {'x','zh','zb'}, dimensions={0} | all-to-all | bytes 262144 | tf_op jit(solution)/shard_map/all_to_all | solution.py:257
  138.9 0.5 shard_map.48
  139.4 10.4 %all_to_all.56.in_ref = f32[16,8,128]{2,1,0:T(8,128)S(1)} all-to-all(f32[16,8,128]{2,1,0:T(8,128)S(1)} %shard_map.48), channel_id=1, replica_groups=mesh['y'=8,'core'=2,'x'=4,'zh'=4,'zb'=2] {'y','core'}, dimensions={0} | all-to-all | bytes 131072 | tf_op jit(solution)/shard_map/all_to_all | solution.py:257
  149.8 4.0 %shard_map.49 = (f32[8,128]{1,0:T(8,128)}, f32[32,104,128]{2,1,0:T(8,128)S(1)}) custom-call(f32[16,8,128]{2,1,0:T(8,128)S(1)} %all_to_all.56.in_ref, f32[8,128]{1,0:T(8,128)S(1)} %get-tuple-element.17.lse_ref, f32[1024,1024]{1,0:T(8,128)S(1)} %get-tuple-element.16.plan_ref, f32[384,1024]{1,0:T(8,128)S(1)} %shard_map.42.data_ref), custom_call_target="tpu_custom_call" | custom-call | tf_op jit(solution)/shard_map/pallas_call | solution.py:211
  153.8 26.1 %all_to_all.57 = f32[8,416,128]{2,1,0:T(8,128)S(1)} all-to-all(f32[8,416,128]{2,1,0:T(8,128)S(1)} %bitcast.10), channel_id=1, replica_groups=mesh['y'=8,'core'=2,'x'=4,'zh'=4,'zb'=2] {'x','zb'}, dimensions={0} | all-to-all | bytes 3407872 | tf_op jit(solution)/shard_map/all_to_all | solution.py:257
  179.9 0.0 copy-start
  179.9 0.1 reduce_sum.9
  180.0 12.1 %all_to_all.58.in_ref = f32[4,104,128]{2,1,0:T(8,128)S(1)} all-to-all(f32[4,104,128]{2,1,0:T(8,128)S(1)} %bitcast.11), channel_id=1, replica_groups=mesh['y'=8,'core'=2,'x'=4,'zh'=4,'zb'=2] {'zh'}, dimensions={0} | all-to-all | bytes 425984 | tf_op jit(solution)/shard_map/all_to_all | solution.py:257
  192.1 0.0 copy-done
  192.1 0.7 shard_map.50
  (1 shorter events, 0.0 us)
Async XLA Ops:
  23.1 5.3 %copy-start.1 = (f32[1024,24]{0,1:T(8,128)S(1)}, f32[1024,24]{0,1:T(8,128)}, u32[]{:S(2)}) copy-start(f32[1024,24]{0,1:T(8,128)} %param.3) | copy-start | bytes 294916
  23.1 37.3 %all-to-all-start.1 = ((f32[8,128,384]{2,1,0:T(8,128)}), f32[8,128,384]{2,1,0:T(8,128)S(1)}, u32[]{:S(2)}, u32[]{:S(2)}) async-start(f32[8,128,384]{2,1,0:T(8,128)} %broadcast_in_dim.15), calls=%async_computation.1 | async-start | bytes 3145728 | tf_op jit(solution)/shard_map/all_to_all | solution.py:26
  28.4 11.5 %collective-permute-start = (f32[24,1024]{1,0:T(8,128)S(1)}, f32[24,1024]{1,0:T(8,128)S(1)}, u32[]{:S(2)}, u32[]{:S(2)}) collective-permute-start(f32[24,1024]{1,0:T(8,128)S(1)} %bitcast.13), channel_id=1, source_target_pairs={{0,256},{32,288},{64,320},{96,352},{128,384},{160,416},{192,448},{... | collective-permute-start | bytes 294920 | tf_op jit(solution)/shard_map/ppermute | solution.py:226
  39.9 11.8 %collective-permute-start.3 = (f32[2,24,1024]{2,1,0:T(8,128)S(1)}, f32[2,24,1024]{2,1,0:T(8,128)S(1)}, u32[]{:S(2)}, u32[]{:S(2)}) collective-permute-start(f32[2,24,1024]{2,1,0:T(8,128)S(1)} %pad_maximum_fusion.refs_0_), channel_id=1, source_target_pairs={{0,128},{32,416},{64,192},{96,480},{128,256},{160,32},{192,320},{2... | collective-permute-start | bytes 589832 | tf_op jit(solution)/shard_map/ppermute | solution.py:226
  43.7 9.6 %collective-permute-start.2 = (f32[2,24,1024]{2,1,0:T(8,128)S(1)}, f32[2,24,1024]{2,1,0:T(8,128)S(1)}, u32[]{:S(2)}, u32[]{:S(2)}) collective-permute-start(f32[2,24,1024]{2,1,0:T(8,128)S(1)} %pad_maximum_fusion.refs_0_), channel_id=1, source_target_pairs={{0,448},{32,96},{64,0},{96,160},{128,64},{160,224},{192,128},{224,... | collective-permute-start | bytes 589832 | tf_op jit(solution)/shard_map/ppermute | solution.py:226
  47.2 8.8 %collective-permute-start.1 = (f32[2,24,1024]{2,1,0:T(8,128)S(1)}, f32[2,24,1024]{2,1,0:T(8,128)S(1)}, u32[]{:S(2)}, u32[]{:S(2)}) collective-permute-start(f32[2,24,1024]{2,1,0:T(8,128)S(1)} %pad_maximum_fusion.refs_0_), channel_id=1, source_target_pairs={{0,64},{32,480},{64,128},{96,32},{128,192},{160,96},{192,256},{224... | collective-permute-start | bytes 589832 | tf_op jit(solution)/shard_map/ppermute | solution.py:226
  56.0 4.2 %collective-permute-start.4 = (f32[4,2,24,1024]{3,2,1,0:T(8,128)S(1)}, f32[4,2,24,1024]{3,2,1,0:T(8,128)S(1)}, u32[]{:S(2)}, u32[]{:S(2)}) collective-permute-start(f32[4,2,24,1024]{3,2,1,0:T(8,128)S(1)} %shard_map.41.mine_ref), channel_id=1, source_target_pairs={{0,32},{32,0},{1,33},{33,1},{2,34},{34,2},{3,35},{35,3},{4,36},{36... | collective-permute-start | bytes 2359304 | tf_op jit(solution)/shard_map/ppermute | solution.py:238
  179.9 12.2 %copy-start = (f32[32,384]{1,0:T(8,128)S(1)}, f32[32,384]{1,0:T(8,128)}, u32[]{:S(2)}) copy-start(f32[32,384]{1,0:T(8,128)} %noise_ref.1) | copy-start | bytes 147460

commit v8 on v7

--- a/solution.py
+++ b/solution.py
@@ -163,7 +163,7 @@
     return high, (value - high.astype(F32)).astype(jnp.bfloat16)
 
 
-def final_kernel(tgt_total, own_rows, in_ref, lse_ref, plan_ref, data_ref, g_ref, part_ref,
+def final_kernel(tgt_total, own_rows, n_far, in_ref, lse_ref, plan_ref, data_ref, g_ref, part_ref,
                  high_ref, low_ref):
     v = 1.0 / (tgt_total * jnp.sum(in_ref[...], axis=0))
     g_ref[...] = EPS * (jnp.log(v) - (math.log(tgt_total) + lse_ref[...]))
@@ -172,39 +172,42 @@
     scaled = data_ref[...] * v
     high_ref[:feats, :], low_ref[:feats, :] = halves(scaled)
     high_ref[feats:, :], low_ref[feats:, :] = halves(jnp.broadcast_to(v, (LANES, v.shape[1])))
-    lane = lax.broadcasted_iota(jnp.int32, (8, LANES), 1)
     tiles, wide = own_rows // 8, feats // LANES
+    tall = tiles * wide * 8
+    own = [lax.broadcasted_iota(jnp.int32, (own_rows, LANES), d) for d in range(2)]
 
     def times(a, w_ref):
         return lax.dot_general(a, w_ref[...], (((1,), (1,)), ((), ())),
                                preferred_element_type=F32)
 
+    part_ref[:, n_far * tall :, :] = jnp.zeros((part_ref.shape[0], 8, LANES), F32)
     for b in range(plan_ref.shape[0] // BLOCK):
         high, low = halves(plan_ref[b * BLOCK : (b + 1) * BLOCK, :])
         got = times(high, low_ref) + times(low, high_ref) + times(high, high_ref)
         for p in range(BLOCK // own_rows):
-            peer = b * (BLOCK // own_rows) + p
-            mass = jnp.zeros((8, LANES), F32)
+            near, far = divmod(b * (BLOCK // own_rows) + p, n_far)
             for r in range(tiles):
                 at = slice(p * own_rows + r * 8, p * own_rows + r * 8 + 8)
                 for c in range(wide):
-                    part_ref[peer, (r * wide + c) * 8 : (r * wide + c + 1) * 8, :] = got[
-                        at, c * LANES : (c + 1) * LANES]
-                mass = jnp.where(lane // (LANES // tiles) == r, got[at, feats:], mass)
-            part_ref[peer, tiles * wide * 8 :, :] = mass
+                    spot = far * tall + (r * wide + c) * 8
+                    part_ref[near, spot : spot + 8, :] = got[at, c * LANES : (c + 1) * LANES]
+            mass = got[p * own_rows : (p + 1) * own_rows, feats:]
+            part_ref[near, n_far * tall + far : n_far * tall + far + 1, :] = jnp.sum(
+                jnp.where(own[0] == own[1], mass, 0.0), axis=0, keepdims=True)
 
 
 def last_kernel(in_ref, noise_ref, out_ref):
     rows, feats = noise_ref.shape
     tiles, wide = rows // 8, feats // LANES
     parts = jnp.sum(in_ref[...], axis=0)
-    mass = parts[tiles * wide * 8 :]
+    masses = parts[tiles * wide * 8 :]
+    mine = lax.broadcasted_iota(jnp.int32, masses.shape, 0) == lax.axis_index(FAR)
+    inverse = 1.0 / down(jnp.sum(jnp.where(mine, masses, 0.0), axis=0, keepdims=True))[:rows]
     for r in range(tiles):
-        inverse = 1.0 / mass[:, r * (LANES // tiles) : r * (LANES // tiles) + 1]
         for c in range(wide):
             at = (r * wide + c) * 8
             spot = (slice(r * 8, r * 8 + 8), slice(c * LANES, (c + 1) * LANES))
-            out_ref[spot] = parts[at : at + 8] * inverse - noise_ref[spot]
+            out_ref[spot] = parts[at : at + 8] * inverse[spot[0]] - noise_ref[spot]
 
 
 def call(kernel, outs, *args, scratch=(), limit=LIMIT):
@@ -269,13 +272,15 @@
                               swap(message, SRC), plan, scratch=row_scratch)
         (message,) = call(functools.partial(column_kernel, float(src_total)), [to_src],
                           swap(message, TGT), plan)
-    tall = own_rows // 8 * (feats // LANES) * 8 + 8
+    tall = own_rows // 8 * (feats // LANES) * 8
     g_pot, part = call(
-        functools.partial(final_kernel, float(tgt_total), own_rows),
-        [c_tiles, (n_tgt, tall, LANES)], swap(message, SRC), lse, plan, columns,
+        functools.partial(final_kernel, float(tgt_total), own_rows, n_far),
+        [c_tiles, (n_near, n_far * tall + 8, LANES)], swap(message, SRC), lse, plan, columns,
         scratch=[pltpu.VMEM((feats + LANES, n_cols), jnp.bfloat16)] * 2)
-    part = jnp.sum(swap(part.reshape(n_near, n_far * tall, LANES), NEAR), axis=0)
-    part = swap(part.reshape(n_far, tall, LANES), FAR)
+    part = jnp.sum(swap(part, NEAR), axis=0)
+    masses = jnp.broadcast_to(part[None, n_far * tall :], (n_far, 8, LANES))
+    part = jnp.concatenate([part[: n_far * tall].reshape(n_far, tall, LANES), masses], axis=1)
+    part = swap(part, FAR)
     (velocity,) = call(last_kernel, [noise.shape], part, noise)
     return velocity, g_pot.reshape(-1)
 

time: 194 us -> 193 us (level)
  no operation moved by 1% of the time
where the time goes in v8:
time: 193 us; the launch traced here: 192 us
  blocking collectives  138 us (72%)
  starting transfers between devices  24.6 us (13%)
  Pallas kernels  14.4 us (7%)
  waiting for transfers between devices  12.4 us (6%)
  local copies, waits for them, and re-layouts  2.1 us (1%)
    all_to_all x8, blocking collectives, swap(): return lax.all_to_all(value, axis, 0, 0)  118 us
    all_to_all x1, blocking collectives, spread(): lax.all_to_all(jnp.broadcast_to(value[None], (count,) + value.shape), axi...  20.4 us
    ppermute x4, starting transfers between devices, shifted(): lax.ppermute(value, SRC, [(2 * i + c, 2 * ((i + turned(hop, c, count)) %...  17.3 us
    pallas_call x10, Pallas kernels, call(): pl.pallas_call(kernel, out_shape=[jax.ShapeDtypeStruct(o, F32) if isinsta...  14.4 us
    ppermute x4, waiting for transfers between devices, shifted(): lax.ppermute(value, SRC, [(2 * i + c, 2 * ((i + turned(hop, c, count)) %...  10.2 us
    all_to_all x1, starting transfers between devices, spread(): lax.all_to_all(jnp.broadcast_to(value[None], (count,) + value.shape), axi...  5.3 us
  transfers between devices with their start and end apart: 6, of which 5 were waited for; matrix products, arithmetic and copies ran while one was open for 0% of the time, Pallas kernels for 0%

profile of v8, /device:TPU:2, one launch (start us, length us, event | category | flops | bytes accessed | tf_op | source)
XLA Modules:
  0.0 192.3 jit_solution(1847860497618084958)
XLA Ops:
  0.6 0.8 broadcast_in_dim.8
  1.4 20.4 %all_to_all.50 = f32[4,32,384]{2,1,0:T(8,128)S(1)} all-to-all(f32[4,32,384]{2,1,0:T(8,128)S(1)} %broadcast_in_dim.8), channel_id=1, replica_groups=mesh['y'=8,'core'=2,'x'=4,'zh'=4,'zb'=2] {'zh'}, dimensions={0} | all-to-all | bytes 393216 | tf_op jit(solution)/shard_map/all_to_all | solution.py:26
  21.8 1.3 broadcast_in_dim.10
  23.1 0.0 copy-start.1
  23.1 5.3 %all-to-all-start.1 = ((f32[8,128,384]{2,1,0:T(8,128)}), f32[8,128,384]{2,1,0:T(8,128)S(1)}, u32[]{:S(2)}, u32[]{:S(2)}) async-start(f32[8,128,384]{2,1,0:T(8,128)} %broadcast_in_dim.10), calls=%async_computation.1 | async-start | bytes 3145728 | tf_op jit(solution)/shard_map/all_to_all | solution.py:26
  28.4 0.0 copy-done.1
  28.4 7.7 %collective-permute-start = (f32[24,1024]{1,0:T(8,128)S(1)}, f32[24,1024]{1,0:T(8,128)S(1)}, u32[]{:S(2)}, u32[]{:S(2)}) collective-permute-start(f32[24,1024]{1,0:T(8,128)S(1)} %bitcast.11), channel_id=1, source_target_pairs={{0,256},{32,288},{64,320},{96,352},{128,384},{160,416},{192,448},{... | collective-permute-start | bytes 294920 | tf_op jit(solution)/shard_map/ppermute | solution.py:229
  36.1 3.7 %collective-permute-done = f32[24,1024]{1,0:T(8,128)S(1)} collective-permute-done((f32[24,1024]{1,0:T(8,128)S(1)}, f32[24,1024]{1,0:T(8,128)S(1)}, u32[]{:S(2)}, u32[]{:S(2)}) %collective-permute-start) | collective-permute-done | bytes 98336 | tf_op jit(solution)/shard_map/ppermute | solution.py:229
  39.9 3.8 %collective-permute-start.3 = (f32[2,24,1024]{2,1,0:T(8,128)S(1)}, f32[2,24,1024]{2,1,0:T(8,128)S(1)}, u32[]{:S(2)}, u32[]{:S(2)}) collective-permute-start(f32[2,24,1024]{2,1,0:T(8,128)S(1)} %pad_maximum_fusion.1.refs_0_), channel_id=1, source_target_pairs={{0,128},{32,416},{64,192},{96,480},{128,256},{160,32},{192,320},{2... | collective-permute-start | bytes 589832 | tf_op jit(solution)/shard_map/ppermute | solution.py:229
  43.7 3.5 %collective-permute-start.2 = (f32[2,24,1024]{2,1,0:T(8,128)S(1)}, f32[2,24,1024]{2,1,0:T(8,128)S(1)}, u32[]{:S(2)}, u32[]{:S(2)}) collective-permute-start(f32[2,24,1024]{2,1,0:T(8,128)S(1)} %pad_maximum_fusion.1.refs_0_), channel_id=1, source_target_pairs={{0,448},{32,96},{64,0},{96,160},{128,64},{160,224},{192,128},{224,... | collective-permute-start | bytes 589832 | tf_op jit(solution)/shard_map/ppermute | solution.py:229
  47.2 2.3 %collective-permute-start.1 = (f32[2,24,1024]{2,1,0:T(8,128)S(1)}, f32[2,24,1024]{2,1,0:T(8,128)S(1)}, u32[]{:S(2)}, u32[]{:S(2)}) collective-permute-start(f32[2,24,1024]{2,1,0:T(8,128)S(1)} %pad_maximum_fusion.1.refs_0_), channel_id=1, source_target_pairs={{0,64},{32,480},{64,128},{96,32},{128,192},{160,96},{192,256},{224... | collective-permute-start | bytes 589832 | tf_op jit(solution)/shard_map/ppermute | solution.py:229
  49.5 2.1 %collective-permute-done.3.refs_3_ = f32[2,24,1024]{2,1,0:T(8,128)S(1)} collective-permute-done((f32[2,24,1024]{2,1,0:T(8,128)S(1)}, f32[2,24,1024]{2,1,0:T(8,128)S(1)}, u32[]{:S(2)}, u32[]{:S(2)}) %collective-permute-start.3) | collective-permute-done | bytes 196640 | tf_op jit(solution)/shard_map/ppermute | solution.py:229
  51.7 1.6 collective-permute-done.2.refs_2_
  53.3 2.7 %collective-permute-done.1.refs_1_ = f32[2,24,1024]{2,1,0:T(8,128)S(1)} collective-permute-done((f32[2,24,1024]{2,1,0:T(8,128)S(1)}, f32[2,24,1024]{2,1,0:T(8,128)S(1)}, u32[]{:S(2)}, u32[]{:S(2)}) %collective-permute-start.1) | collective-permute-done | bytes 196640 | tf_op jit(solution)/shard_map/ppermute | solution.py:229
  56.0 0.1 shard_map.41.mine_ref
  56.0 1.9 collective-permute-start.4
  58.0 2.3 %collective-permute-done.4.theirs_ref = f32[4,2,24,1024]{3,2,1,0:T(8,128)S(1)} collective-permute-done((f32[4,2,24,1024]{3,2,1,0:T(8,128)S(1)}, f32[4,2,24,1024]{3,2,1,0:T(8,128)S(1)}, u32[]{:S(2)}, u32[]{:S(2)}) %collective-permute-start.4) | collective-permute-done | bytes 786464 | tf_op jit(solution)/shard_map/ppermute | solution.py:241
  60.2 0.2 shard_map.42.data_ref
  60.4 0.0 all-to-all-done.1
  60.4 5.7 %shard_map.43 = (f32[1024,1024]{1,0:T(8,128)S(1)}, f32[32,8,128]{2,1,0:T(8,128)S(1)}) custom-call(f32[384,1024]{1,0:T(8,128)S(1)} %shard_map.42.data_ref, f32[1024,384]{1,0:T(8,128)S(1)} %bitcast.8), custom_call_target="tpu_custom_call" | custom-call | tf_op jit(solution)/shard_map/pallas_call | solution.py:214
  66.1 16.1 %all_to_all.51.in_ref = f32[32,8,128]{2,1,0:T(8,128)S(1)} all-to-all(f32[32,8,128]{2,1,0:T(8,128)S(1)} %get-tuple-element.11), channel_id=1, replica_groups=mesh['y'=8,'core'=2,'x'=4,'zh'=4,'zb'=2] {'x','zh','zb'}, dimensions={0} | all-to-all | bytes 262144 | tf_op jit(solution)/shard_map/all_to_all | solution.py:260
  82.2 1.3 shard_map.44
  83.6 14.3 %all_to_all.52.in_ref = f32[16,8,128]{2,1,0:T(8,128)S(1)} all-to-all(f32[16,8,128]{2,1,0:T(8,128)S(1)} %get-tuple-element.13), channel_id=1, replica_groups=mesh['y'=8,'core'=2,'x'=4,'zh'=4,'zb'=2] {'y','core'}, dimensions={0} | all-to-all | bytes 131072 | tf_op jit(solution)/shard_map/all_to_all | solution.py:260
  97.9 1.0 shard_map.45
  98.9 14.4 %all_to_all.53.in_ref = f32[32,8,128]{2,1,0:T(8,128)S(1)} all-to-all(f32[32,8,128]{2,1,0:T(8,128)S(1)} %get-tuple-element.15), channel_id=1, replica_groups=mesh['y'=8,'core'=2,'x'=4,'zh'=4,'zb'=2] {'x','zh','zb'}, dimensions={0} | all-to-all | bytes 262144 | tf_op jit(solution)/shard_map/all_to_all | solution.py:260
  113.3 0.5 shard_map.46
  113.8 10.4 %all_to_all.54.in_ref = f32[16,8,128]{2,1,0:T(8,128)S(1)} all-to-all(f32[16,8,128]{2,1,0:T(8,128)S(1)} %shard_map.46), channel_id=1, replica_groups=mesh['y'=8,'core'=2,'x'=4,'zh'=4,'zb'=2] {'y','core'}, dimensions={0} | all-to-all | bytes 131072 | tf_op jit(solution)/shard_map/all_to_all | solution.py:260
  124.1 0.4 shard_map.47
  124.5 14.4 %all_to_all.55.in_ref = f32[32,8,128]{2,1,0:T(8,128)S(1)} all-to-all(f32[32,8,128]{2,1,0:T(8,128)S(1)} %shard_map.47), channel_id=1, replica_groups=mesh['y'=8,'core'=2,'x'=4,'zh'=4,'zb'=2] {'x','zh','zb'}, dimensions={0} | all-to-all | bytes 262144 | tf_op jit(solution)/shard_map/all_to_all | solution.py:260
  138.9 0.5 shard_map.48
  139.4 10.4 %all_to_all.56.in_ref = f32[16,8,128]{2,1,0:T(8,128)S(1)} all-to-all(f32[16,8,128]{2,1,0:T(8,128)S(1)} %shard_map.48), channel_id=1, replica_groups=mesh['y'=8,'core'=2,'x'=4,'zh'=4,'zb'=2] {'y','core'}, dimensions={0} | all-to-all | bytes 131072 | tf_op jit(solution)/shard_map/all_to_all | solution.py:260
  149.8 4.0 %shard_map.49 = (f32[8,128]{1,0:T(8,128)}, f32[8,392,128]{2,1,0:T(8,128)S(1)}) custom-call(f32[16,8,128]{2,1,0:T(8,128)S(1)} %all_to_all.56.in_ref, f32[8,128]{1,0:T(8,128)S(1)} %get-tuple-element.17.lse_ref, f32[1024,1024]{1,0:T(8,128)S(1)} %get-tuple-element.16.plan_ref, f32[384,1024]{1,0:T(8,128)S(1)} %shard_map.42.data_ref), custom_call_target="tpu_custom_call" | custom-call | tf_op jit(solution)/shard_map/pallas_call | solution.py:214
  153.8 25.3 %all_to_all.57 = f32[8,392,128]{2,1,0:T(8,128)S(1)} all-to-all(f32[8,392,128]{2,1,0:T(8,128)S(1)} %get-tuple-element.18), channel_id=1, replica_groups=mesh['y'=8,'core'=2,'x'=4,'zh'=4,'zb'=2] {'x','zb'}, dimensions={0} | all-to-all | bytes 3211264 | tf_op jit(solution)/shard_map/all_to_all | solution.py:260
  179.1 0.0 copy-start
  179.1 0.1 reduce_sum.9
  179.3 12.3 %all_to_all.58.in_ref = f32[4,104,128]{2,1,0:T(8,128)S(1)} all-to-all(f32[4,104,128]{2,1,0:T(8,128)S(1)} %pad_maximum_fusion), channel_id=1, replica_groups=mesh['y'=8,'core'=2,'x'=4,'zh'=4,'zb'=2] {'zh'}, dimensions={0} | all-to-all | bytes 425984 | tf_op jit(solution)/shard_map/all_to_all | solution.py:260
  191.6 0.0 copy-done
  191.6 0.7 shard_map.50
  (5 shorter events, 0.1 us)
Async XLA Ops:
  23.1 5.3 %copy-start.1 = (f32[1024,24]{0,1:T(8,128)S(1)}, f32[1024,24]{0,1:T(8,128)}, u32[]{:S(2)}) copy-start(f32[1024,24]{0,1:T(8,128)} %param.3) | copy-start | bytes 294916
  23.1 37.3 %all-to-all-start.1 = ((f32[8,128,384]{2,1,0:T(8,128)}), f32[8,128,384]{2,1,0:T(8,128)S(1)}, u32[]{:S(2)}, u32[]{:S(2)}) async-start(f32[8,128,384]{2,1,0:T(8,128)} %broadcast_in_dim.10), calls=%async_computation.1 | async-start | bytes 3145728 | tf_op jit(solution)/shard_map/all_to_all | solution.py:26
  28.4 11.5 %collective-permute-start = (f32[24,1024]{1,0:T(8,128)S(1)}, f32[24,1024]{1,0:T(8,128)S(1)}, u32[]{:S(2)}, u32[]{:S(2)}) collective-permute-start(f32[24,1024]{1,0:T(8,128)S(1)} %bitcast.11), channel_id=1, source_target_pairs={{0,256},{32,288},{64,320},{96,352},{128,384},{160,416},{192,448},{... | collective-permute-start | bytes 294920 | tf_op jit(solution)/shard_map/ppermute | solution.py:229
  39.9 11.8 %collective-permute-start.3 = (f32[2,24,1024]{2,1,0:T(8,128)S(1)}, f32[2,24,1024]{2,1,0:T(8,128)S(1)}, u32[]{:S(2)}, u32[]{:S(2)}) collective-permute-start(f32[2,24,1024]{2,1,0:T(8,128)S(1)} %pad_maximum_fusion.1.refs_0_), channel_id=1, source_target_pairs={{0,128},{32,416},{64,192},{96,480},{128,256},{160,32},{192,320},{2... | collective-permute-start | bytes 589832 | tf_op jit(solution)/shard_map/ppermute | solution.py:229
  43.7 9.6 %collective-permute-start.2 = (f32[2,24,1024]{2,1,0:T(8,128)S(1)}, f32[2,24,1024]{2,1,0:T(8,128)S(1)}, u32[]{:S(2)}, u32[]{:S(2)}) collective-permute-start(f32[2,24,1024]{2,1,0:T(8,128)S(1)} %pad_maximum_fusion.1.refs_0_), channel_id=1, source_target_pairs={{0,448},{32,96},{64,0},{96,160},{128,64},{160,224},{192,128},{224,... | collective-permute-start | bytes 589832 | tf_op jit(solution)/shard_map/ppermute | solution.py:229
  47.2 8.8 %collective-permute-start.1 = (f32[2,24,1024]{2,1,0:T(8,128)S(1)}, f32[2,24,1024]{2,1,0:T(8,128)S(1)}, u32[]{:S(2)}, u32[]{:S(2)}) collective-permute-start(f32[2,24,1024]{2,1,0:T(8,128)S(1)} %pad_maximum_fusion.1.refs_0_), channel_id=1, source_target_pairs={{0,64},{32,480},{64,128},{96,32},{128,192},{160,96},{192,256},{224... | collective-permute-start | bytes 589832 | tf_op jit(solution)/shard_map/ppermute | solution.py:229
  56.0 4.2 %collective-permute-start.4 = (f32[4,2,24,1024]{3,2,1,0:T(8,128)S(1)}, f32[4,2,24,1024]{3,2,1,0:T(8,128)S(1)}, u32[]{:S(2)}, u32[]{:S(2)}) collective-permute-start(f32[4,2,24,1024]{3,2,1,0:T(8,128)S(1)} %shard_map.41.mine_ref), channel_id=1, source_target_pairs={{0,32},{32,0},{1,33},{33,1},{2,34},{34,2},{3,35},{35,3},{4,36},{36... | collective-permute-start | bytes 2359304 | tf_op jit(solution)/shard_map/ppermute | solution.py:241
  179.1 12.5 %copy-start = (f32[32,384]{1,0:T(8,128)S(1)}, f32[32,384]{1,0:T(8,128)}, u32[]{:S(2)}) copy-start(f32[32,384]{1,0:T(8,128)} %noise_ref.1) | copy-start | bytes 147460

commit v9 on v8

--- a/solution.py
+++ b/solution.py
@@ -17,7 +17,7 @@
 X_CHIPS = 4
 INTERPRET = False
 LIMIT = 24 << 20
-SRC, TGT, NEAR, FAR = ("y", "core"), ("x", "zh", "zb"), ("x", "zb"), "zh"
+SRC, TGT, NEAR, FAR = ("y", "core"), ("x", "zh", "zb"), ("zb", "x"), "zh"
 F32 = jnp.float32
 
 
@@ -111,16 +111,17 @@
 def first_column_kernel(log_src, in_ref, gain_ref, f_ref, out_ref):
     f_pot = -(log_src + merged(in_ref))
     f_ref[...] = f_pot
-    top = total = None
-    for b in range(f_pot.shape[0]):
-        z = gain_ref[b * LANES : (b + 1) * LANES, :] + down(f_pot[b : b + 1])
-        here = jnp.max(z, axis=0, keepdims=True)
-        if b == 0:
-            top, total = here, jnp.sum(jnp.exp(z - here), axis=0, keepdims=True)
-        else:
-            new = jnp.maximum(top, here)
-            total = total * jnp.exp(top - new) + jnp.sum(jnp.exp(z - new), axis=0, keepdims=True)
-            top = new
+    blocks, wide = range(f_pot.shape[0]), gain_ref.shape[1]
+    columns = [down(f_pot[b : b + 1]) for b in blocks]
+
+    def tiles(b):
+        z = gain_ref[b * LANES : (b + 1) * LANES, :] + columns[b]
+        return z.reshape(LANES // 8, 8, wide)
+
+    top = functools.reduce(jnp.maximum, [jnp.max(tiles(b), axis=0) for b in blocks])
+    top = jnp.max(top, axis=0, keepdims=True)
+    total = sum(jnp.sum(jnp.exp(tiles(b) - top[None]), axis=0) for b in blocks)
+    total = jnp.sum(total, axis=0, keepdims=True)
     lse = top + jnp.log(total)
     for t in range(out_ref.shape[1]):
         out_ref[:, t : t + 1, :] = jnp.broadcast_to(

time: 193 us -> 193 us (level)
  no operation moved by 1% of the time
where the time goes in v9:
time: 193 us; the launch traced here: 192 us
  blocking collectives  138 us (72%)
  starting transfers between devices  24.6 us (13%)
  Pallas kernels  14.2 us (7%)
  waiting for transfers between devices  12.4 us (6%)
  local copies, waits for them, and re-layouts  2.1 us (1%)
    all_to_all x8, blocking collectives, swap(): return lax.all_to_all(value, axis, 0, 0)  118 us
    all_to_all x1, blocking collectives, spread(): lax.all_to_all(jnp.broadcast_to(value[None], (count,) + value.shape), axi...  20.4 us
    ppermute x4, starting transfers between devices, shifted(): lax.ppermute(value, SRC, [(2 * i + c, 2 * ((i + turned(hop, c, count)) %...  17.3 us
    pallas_call x10, Pallas kernels, call(): pl.pallas_call(kernel, out_shape=[jax.ShapeDtypeStruct(o, F32) if isinsta...  14.2 us
    ppermute x4, waiting for transfers between devices, shifted(): lax.ppermute(value, SRC, [(2 * i + c, 2 * ((i + turned(hop, c, count)) %...  10.2 us
    all_to_all x1, starting transfers between devices, spread(): lax.all_to_all(jnp.broadcast_to(value[None], (count,) + value.shape), axi...  5.3 us
  transfers between devices with their start and end apart: 6, of which 5 were waited for; matrix products, arithmetic and copies ran while one was open for 0% of the time, Pallas kernels for 0%

profile of v9, /device:TPU:2, one launch (start us, length us, event | category | flops | bytes accessed | tf_op | source)
XLA Modules:
  0.0 192.3 jit_solution(18181134694724509729)
XLA Ops:
  0.6 0.8 broadcast_in_dim.8
  1.4 20.4 %all_to_all.50 = f32[4,32,384]{2,1,0:T(8,128)S(1)} all-to-all(f32[4,32,384]{2,1,0:T(8,128)S(1)} %broadcast_in_dim.8), channel_id=1, replica_groups=mesh['y'=8,'core'=2,'x'=4,'zh'=4,'zb'=2] {'zh'}, dimensions={0} | all-to-all | bytes 393216 | tf_op jit(solution)/shard_map/all_to_all | solution.py:26
  21.8 1.3 broadcast_in_dim.10
  23.1 0.0 copy-start.1
  23.1 5.3 %all-to-all-start.1 = ((f32[8,128,384]{2,1,0:T(8,128)}), f32[8,128,384]{2,1,0:T(8,128)S(1)}, u32[]{:S(2)}, u32[]{:S(2)}) async-start(f32[8,128,384]{2,1,0:T(8,128)} %broadcast_in_dim.10), calls=%async_computation.1 | async-start | bytes 3145728 | tf_op jit(solution)/shard_map/all_to_all | solution.py:26
  28.4 0.0 copy-done.1
  28.4 7.7 %collective-permute-start = (f32[24,1024]{1,0:T(8,128)S(1)}, f32[24,1024]{1,0:T(8,128)S(1)}, u32[]{:S(2)}, u32[]{:S(2)}) collective-permute-start(f32[24,1024]{1,0:T(8,128)S(1)} %bitcast.11), channel_id=1, source_target_pairs={{0,256},{32,288},{64,320},{96,352},{128,384},{160,416},{192,448},{... | collective-permute-start | bytes 294920 | tf_op jit(solution)/shard_map/ppermute | solution.py:230
  36.1 3.7 %collective-permute-done = f32[24,1024]{1,0:T(8,128)S(1)} collective-permute-done((f32[24,1024]{1,0:T(8,128)S(1)}, f32[24,1024]{1,0:T(8,128)S(1)}, u32[]{:S(2)}, u32[]{:S(2)}) %collective-permute-start) | collective-permute-done | bytes 98336 | tf_op jit(solution)/shard_map/ppermute | solution.py:230
  39.9 3.8 %collective-permute-start.3 = (f32[2,24,1024]{2,1,0:T(8,128)S(1)}, f32[2,24,1024]{2,1,0:T(8,128)S(1)}, u32[]{:S(2)}, u32[]{:S(2)}) collective-permute-start(f32[2,24,1024]{2,1,0:T(8,128)S(1)} %pad_maximum_fusion.1.refs_0_), channel_id=1, source_target_pairs={{0,128},{32,416},{64,192},{96,480},{128,256},{160,32},{192,320},{2... | collective-permute-start | bytes 589832 | tf_op jit(solution)/shard_map/ppermute | solution.py:230
  43.7 3.5 %collective-permute-start.2 = (f32[2,24,1024]{2,1,0:T(8,128)S(1)}, f32[2,24,1024]{2,1,0:T(8,128)S(1)}, u32[]{:S(2)}, u32[]{:S(2)}) collective-permute-start(f32[2,24,1024]{2,1,0:T(8,128)S(1)} %pad_maximum_fusion.1.refs_0_), channel_id=1, source_target_pairs={{0,448},{32,96},{64,0},{96,160},{128,64},{160,224},{192,128},{224,... | collective-permute-start | bytes 589832 | tf_op jit(solution)/shard_map/ppermute | solution.py:230
  47.2 2.3 %collective-permute-start.1 = (f32[2,24,1024]{2,1,0:T(8,128)S(1)}, f32[2,24,1024]{2,1,0:T(8,128)S(1)}, u32[]{:S(2)}, u32[]{:S(2)}) collective-permute-start(f32[2,24,1024]{2,1,0:T(8,128)S(1)} %pad_maximum_fusion.1.refs_0_), channel_id=1, source_target_pairs={{0,64},{32,480},{64,128},{96,32},{128,192},{160,96},{192,256},{224... | collective-permute-start | bytes 589832 | tf_op jit(solution)/shard_map/ppermute | solution.py:230
  49.5 2.1 %collective-permute-done.3.refs_3_ = f32[2,24,1024]{2,1,0:T(8,128)S(1)} collective-permute-done((f32[2,24,1024]{2,1,0:T(8,128)S(1)}, f32[2,24,1024]{2,1,0:T(8,128)S(1)}, u32[]{:S(2)}, u32[]{:S(2)}) %collective-permute-start.3) | collective-permute-done | bytes 196640 | tf_op jit(solution)/shard_map/ppermute | solution.py:230
  51.7 1.6 collective-permute-done.2.refs_2_
  53.3 2.7 %collective-permute-done.1.refs_1_ = f32[2,24,1024]{2,1,0:T(8,128)S(1)} collective-permute-done((f32[2,24,1024]{2,1,0:T(8,128)S(1)}, f32[2,24,1024]{2,1,0:T(8,128)S(1)}, u32[]{:S(2)}, u32[]{:S(2)}) %collective-permute-start.1) | collective-permute-done | bytes 196640 | tf_op jit(solution)/shard_map/ppermute | solution.py:230
  56.0 0.1 shard_map.41.mine_ref
  56.0 1.9 collective-permute-start.4
  58.0 2.3 %collective-permute-done.4.theirs_ref = f32[4,2,24,1024]{3,2,1,0:T(8,128)S(1)} collective-permute-done((f32[4,2,24,1024]{3,2,1,0:T(8,128)S(1)}, f32[4,2,24,1024]{3,2,1,0:T(8,128)S(1)}, u32[]{:S(2)}, u32[]{:S(2)}) %collective-permute-start.4) | collective-permute-done | bytes 786464 | tf_op jit(solution)/shard_map/ppermute | solution.py:242
  60.2 0.2 shard_map.42.data_ref
  60.4 0.0 all-to-all-done.1
  60.4 5.7 %shard_map.43 = (f32[1024,1024]{1,0:T(8,128)S(1)}, f32[32,8,128]{2,1,0:T(8,128)S(1)}) custom-call(f32[384,1024]{1,0:T(8,128)S(1)} %shard_map.42.data_ref, f32[1024,384]{1,0:T(8,128)S(1)} %bitcast.8), custom_call_target="tpu_custom_call" | custom-call | tf_op jit(solution)/shard_map/pallas_call | solution.py:215
  66.1 16.1 %all_to_all.51.in_ref = f32[32,8,128]{2,1,0:T(8,128)S(1)} all-to-all(f32[32,8,128]{2,1,0:T(8,128)S(1)} %get-tuple-element.11), channel_id=1, replica_groups=mesh['y'=8,'core'=2,'x'=4,'zh'=4,'zb'=2] {'x','zh','zb'}, dimensions={0} | all-to-all | bytes 262144 | tf_op jit(solution)/shard_map/all_to_all | solution.py:261
  82.2 1.1 shard_map.44
  83.3 14.3 %all_to_all.52.in_ref = f32[16,8,128]{2,1,0:T(8,128)S(1)} all-to-all(f32[16,8,128]{2,1,0:T(8,128)S(1)} %get-tuple-element.13), channel_id=1, replica_groups=mesh['y'=8,'core'=2,'x'=4,'zh'=4,'zb'=2] {'y','core'}, dimensions={0} | all-to-all | bytes 131072 | tf_op jit(solution)/shard_map/all_to_all | solution.py:261
  97.7 1.0 shard_map.45
  98.7 14.4 %all_to_all.53.in_ref = f32[32,8,128]{2,1,0:T(8,128)S(1)} all-to-all(f32[32,8,128]{2,1,0:T(8,128)S(1)} %get-tuple-element.15), channel_id=1, replica_groups=mesh['y'=8,'core'=2,'x'=4,'zh'=4,'zb'=2] {'x','zh','zb'}, dimensions={0} | all-to-all | bytes 262144 | tf_op jit(solution)/shard_map/all_to_all | solution.py:261
  113.1 0.5 shard_map.46
  113.6 10.4 %all_to_all.54.in_ref = f32[16,8,128]{2,1,0:T(8,128)S(1)} all-to-all(f32[16,8,128]{2,1,0:T(8,128)S(1)} %shard_map.46), channel_id=1, replica_groups=mesh['y'=8,'core'=2,'x'=4,'zh'=4,'zb'=2] {'y','core'}, dimensions={0} | all-to-all | bytes 131072 | tf_op jit(solution)/shard_map/all_to_all | solution.py:261
  123.9 0.4 shard_map.47
  124.3 14.4 %all_to_all.55.in_ref = f32[32,8,128]{2,1,0:T(8,128)S(1)} all-to-all(f32[32,8,128]{2,1,0:T(8,128)S(1)} %shard_map.47), channel_id=1, replica_groups=mesh['y'=8,'core'=2,'x'=4,'zh'=4,'zb'=2] {'x','zh','zb'}, dimensions={0} | all-to-all | bytes 262144 | tf_op jit(solution)/shard_map/all_to_all | solution.py:261
  138.7 0.5 shard_map.48
  139.2 10.4 %all_to_all.56.in_ref = f32[16,8,128]{2,1,0:T(8,128)S(1)} all-to-all(f32[16,8,128]{2,1,0:T(8,128)S(1)} %shard_map.48), channel_id=1, replica_groups=mesh['y'=8,'core'=2,'x'=4,'zh'=4,'zb'=2] {'y','core'}, dimensions={0} | all-to-all | bytes 131072 | tf_op jit(solution)/shard_map/all_to_all | solution.py:261
  149.6 4.0 %shard_map.49 = (f32[8,128]{1,0:T(8,128)}, f32[8,392,128]{2,1,0:T(8,128)S(1)}) custom-call(f32[16,8,128]{2,1,0:T(8,128)S(1)} %all_to_all.56.in_ref, f32[8,128]{1,0:T(8,128)S(1)} %get-tuple-element.17.lse_ref, f32[1024,1024]{1,0:T(8,128)S(1)} %get-tuple-element.16.plan_ref, f32[384,1024]{1,0:T(8,128)S(1)} %shard_map.42.data_ref), custom_call_target="tpu_custom_call" | custom-call | tf_op jit(solution)/shard_map/pallas_call | solution.py:215
  153.6 25.3 %all_to_all.57 = f32[8,392,128]{2,1,0:T(8,128)S(1)} all-to-all(f32[8,392,128]{2,1,0:T(8,128)S(1)} %get-tuple-element.18), channel_id=1, replica_groups=mesh['y'=8,'core'=2,'x'=4,'zh'=4,'zb'=2] {'zb','x'}, dimensions={0} | all-to-all | bytes 3211264 | tf_op jit(solution)/shard_map/all_to_all | solution.py:261
  178.9 0.0 copy-start
  178.9 0.1 reduce_sum.9
  179.1 12.5 %all_to_all.58.in_ref = f32[4,104,128]{2,1,0:T(8,128)S(1)} all-to-all(f32[4,104,128]{2,1,0:T(8,128)S(1)} %pad_maximum_fusion), channel_id=1, replica_groups=mesh['y'=8,'core'=2,'x'=4,'zh'=4,'zb'=2] {'zh'}, dimensions={0} | all-to-all | bytes 425984 | tf_op jit(solution)/shard_map/all_to_all | solution.py:261
  191.5 0.0 copy-done
  191.5 0.7 shard_map.50
  (5 shorter events, 0.1 us)
Async XLA Ops:
  23.1 5.3 %copy-start.1 = (f32[1024,24]{0,1:T(8,128)S(1)}, f32[1024,24]{0,1:T(8,128)}, u32[]{:S(2)}) copy-start(f32[1024,24]{0,1:T(8,128)} %param.3) | copy-start | bytes 294916
  23.1 37.3 %all-to-all-start.1 = ((f32[8,128,384]{2,1,0:T(8,128)}), f32[8,128,384]{2,1,0:T(8,128)S(1)}, u32[]{:S(2)}, u32[]{:S(2)}) async-start(f32[8,128,384]{2,1,0:T(8,128)} %broadcast_in_dim.10), calls=%async_computation.1 | async-start | bytes 3145728 | tf_op jit(solution)/shard_map/all_to_all | solution.py:26
  28.4 11.5 %collective-permute-start = (f32[24,1024]{1,0:T(8,128)S(1)}, f32[24,1024]{1,0:T(8,128)S(1)}, u32[]{:S(2)}, u32[]{:S(2)}) collective-permute-start(f32[24,1024]{1,0:T(8,128)S(1)} %bitcast.11), channel_id=1, source_target_pairs={{0,256},{32,288},{64,320},{96,352},{128,384},{160,416},{192,448},{... | collective-permute-start | bytes 294920 | tf_op jit(solution)/shard_map/ppermute | solution.py:230
  39.9 11.8 %collective-permute-start.3 = (f32[2,24,1024]{2,1,0:T(8,128)S(1)}, f32[2,24,1024]{2,1,0:T(8,128)S(1)}, u32[]{:S(2)}, u32[]{:S(2)}) collective-permute-start(f32[2,24,1024]{2,1,0:T(8,128)S(1)} %pad_maximum_fusion.1.refs_0_), channel_id=1, source_target_pairs={{0,128},{32,416},{64,192},{96,480},{128,256},{160,32},{192,320},{2... | collective-permute-start | bytes 589832 | tf_op jit(solution)/shard_map/ppermute | solution.py:230
  43.7 9.6 %collective-permute-start.2 = (f32[2,24,1024]{2,1,0:T(8,128)S(1)}, f32[2,24,1024]{2,1,0:T(8,128)S(1)}, u32[]{:S(2)}, u32[]{:S(2)}) collective-permute-start(f32[2,24,1024]{2,1,0:T(8,128)S(1)} %pad_maximum_fusion.1.refs_0_), channel_id=1, source_target_pairs={{0,448},{32,96},{64,0},{96,160},{128,64},{160,224},{192,128},{224,... | collective-permute-start | bytes 589832 | tf_op jit(solution)/shard_map/ppermute | solution.py:230
  47.2 8.8 %collective-permute-start.1 = (f32[2,24,1024]{2,1,0:T(8,128)S(1)}, f32[2,24,1024]{2,1,0:T(8,128)S(1)}, u32[]{:S(2)}, u32[]{:S(2)}) collective-permute-start(f32[2,24,1024]{2,1,0:T(8,128)S(1)} %pad_maximum_fusion.1.refs_0_), channel_id=1, source_target_pairs={{0,64},{32,480},{64,128},{96,32},{128,192},{160,96},{192,256},{224... | collective-permute-start | bytes 589832 | tf_op jit(solution)/shard_map/ppermute | solution.py:230
  56.0 4.2 %collective-permute-start.4 = (f32[4,2,24,1024]{3,2,1,0:T(8,128)S(1)}, f32[4,2,24,1024]{3,2,1,0:T(8,128)S(1)}, u32[]{:S(2)}, u32[]{:S(2)}) collective-permute-start(f32[4,2,24,1024]{3,2,1,0:T(8,128)S(1)} %shard_map.41.mine_ref), channel_id=1, source_target_pairs={{0,32},{32,0},{1,33},{33,1},{2,34},{34,2},{3,35},{35,3},{4,36},{36... | collective-permute-start | bytes 2359304 | tf_op jit(solution)/shard_map/ppermute | solution.py:242
  178.9 12.6 %copy-start = (f32[32,384]{1,0:T(8,128)S(1)}, f32[32,384]{1,0:T(8,128)}, u32[]{:S(2)}) copy-start(f32[32,384]{1,0:T(8,128)} %noise_ref.1) | copy-start | bytes 147460
